TPU v7x, 256 devices: a whole 4x4x8 slice. The times are simulated.
256 devices in a mesh: ctx: 32 (over z, x), head: 8 (over y, core).
Axes of the slice: x: 4, y: 4, z: 8, core: 2. Of those that a mesh axis runs over, the one named last changes fastest.
Arguments:
- queries: bfloat16 [256, 4096], P(None, 'head'), may hold values from -40 to 40
- keys: bfloat16 [64, 2048, 2048], P('ctx', None, 'head'), may hold values from -6 to 6
- values: bfloat16 [64, 2048, 2048], P('ctx', None, 'head'), may hold values from -6 to 6
- page_map: int32 [64], replicated, may hold values from 0 to 63, each once
- selected: int32 [2, 8], replicated, may hold values from 0 to 63, as said below
- residual_in: bfloat16 [256, 5376], P('head', 'ctx'), may hold values from -7 to 7
- out_weight: bfloat16 [4096, 5376], P('head', 'ctx'), may hold values from -0.09375 to 0.09375
- norm_gain: float32 [5376], P('ctx'), may hold values from 0.5 to 1.5
- gate_weight: bfloat16 [5376, 21504], P('head', 'ctx'), may hold values from -0.078125 to 0.078125
- up_weight: bfloat16 [5376, 21504], P('head', 'ctx'), may hold values from -0.078125 to 0.078125
- down_weight: bfloat16 [21504, 5376], P('ctx', 'head'), may hold values from -0.0390625 to 0.0390625
Outputs:
- layer_out: bfloat16 [256, 5376], P('ctx', 'head')
Inputs may be any that keep to these rules, and one draw needn't show every extreme that they name: `selected`: each row names 8 different logical pages, among them 64 - 1, the page that holds the block's own positions.
All inputs are finite; a program needn't handle non-finite values.
Results may differ from a plain program's by a relative error of at most 0.02.
Values may be sent and summed in bfloat16 or wider, within the bound.
No kernel may reach another device: no remote copies, remote signals or barrier semaphores. Data moves between devices by JAX's collectives and lax.ppermute only.
A program may use at most 128 MiB of HBM per device.

v0:
```python
import jax
import jax.numpy as jnp
from jax import lax
from jax.sharding import PartitionSpec as P

D = 5376
HEAD_SIZE = 128


score_scale = 168.0 ** (-0.5)
masked_score = -1e30
norm_epsilon = 1e-06


def sent_to_all(array, axis):
    copies = jnp.broadcast_to(array, (lax.axis_size(axis), *array.shape))
    return lax.all_to_all(copies, axis, split_axis=0, concat_axis=0, tiled=True)


def of_everyone(array, axis):
    return sent_to_all(array, axis).max(axis=0)


def cut_along(array, dim, count):
    shape = array.shape
    parts = array.reshape(*shape[:dim], count, shape[dim] // count, *shape[dim + 1 :])
    return jnp.moveaxis(parts, dim, 0)


def sent_and_summed(array, axis, dim):
    parts = cut_along(array, dim, lax.axis_size(axis))
    arrived = lax.all_to_all(parts, axis, split_axis=0, concat_axis=0, tiled=True)
    return arrived.astype(jnp.float32).sum(axis=0)


def in_one_piece(arrays, axis, dim, along):
    ends, at = ([], 0)
    for a in arrays[:-1]:
        at += a.shape[along]
        ends.append(at)
    both = jnp.concatenate(arrays, axis=along)
    return tuple(jnp.split(sent_and_summed(both, axis, dim), ends, axis=along))


def laid_out(parts, dim):
    shape = list(parts.shape[1:])
    shape[dim] *= parts.shape[0]
    return jnp.moveaxis(parts, 0, dim).reshape(shape)


def gathered_copies(array, axis, dim):
    return laid_out(sent_to_all(array, axis), dim)


def taken_together(array, axis):
    return sent_to_all(array, axis).sum(axis=0)


def turned_gather(arrays, axis, dims):
    turned = [jnp.moveaxis(a, dim, 0) for a, dim in zip(arrays, dims)]
    widths = [t[0].size for t in turned]
    both = jnp.concatenate([t.reshape(-1, w) for t, w in zip(turned, widths)], axis=1)
    filled = lax.all_gather(both, axis, axis=0, tiled=True)
    parts = jnp.split(filled, [sum(widths[:k]) for k in range(1, len(widths))], axis=1)
    return tuple(
        (
            jnp.moveaxis(b.reshape(-1, *t.shape[1:]), 0, dim)
            for b, t, dim in zip(parts, turned, dims)
        )
    )


def block_scores(grouped_queries, block_keys, block_values, visible):
    scores = (
        jnp.einsum(
            "rkgd,jkd->kgrj", grouped_queries, block_keys, preferred_element_type=jnp.float32
        )
        * score_scale
    )
    scores = jnp.where(visible[None, None], scores, masked_score)
    row_max = jnp.max(scores, axis=-1)
    weights = jnp.where(visible[None, None], jnp.exp(scores - row_max[..., None]), 0.0)
    row_total = jnp.sum(weights, axis=-1)
    mixture = jnp.einsum(
        "kgrj,jkd->rkgd",
        weights.astype(jnp.bfloat16),
        block_values,
        preferred_element_type=jnp.float32,
    )
    row_count = grouped_queries.shape[0]
    row_max = jnp.transpose(row_max, (2, 0, 1)).reshape(row_count, -1)
    row_total = jnp.transpose(row_total, (2, 0, 1)).reshape(row_count, -1)
    return (row_max, row_total, mixture.reshape(row_count, -1))


def merge_parts(earlier, later):
    new_max = jnp.maximum(earlier[0], later[0])
    earlier_scale = jnp.exp(earlier[0] - new_max)
    later_scale = jnp.exp(later[0] - new_max)
    row_total = earlier[1] * earlier_scale + later[1] * later_scale
    row_count, head_count = new_max.shape
    mixture = earlier[2].reshape(row_count, head_count, -1) * earlier_scale[..., None]
    mixture = mixture + later[2].reshape(row_count, head_count, -1) * later_scale[..., None]
    return (new_max, row_total, mixture.reshape(row_count, -1))


def owner_pass(queries, keys, values, page_map, selected, ctx_index, ctx_count):
    pages_local, page_len, kv_width = keys.shape
    row_count, query_width = queries.shape
    kv_local = kv_width // HEAD_SIZE
    query_group_size = query_width // kv_width
    heads_local = kv_local * query_group_size
    tile_count = selected.shape[0]
    tile_rows = row_count // tile_count
    page_total = pages_local * ctx_count
    offset = page_len - row_count
    slot_ids = ctx_index * pages_local + jnp.arange(pages_local, dtype=jnp.int32)
    all_pages = jnp.arange(page_total, dtype=jnp.int32)
    logical = jnp.sum(
        jnp.where(page_map[None, :] == slot_ids[:, None], all_pages[None, :], 0), axis=1
    )
    chosen = jnp.any(selected[:, None, :] == logical[None, :, None], axis=2)
    is_causal = logical == page_total - 1
    key_position = jnp.arange(page_len, dtype=jnp.int32)
    grouped_tiles = queries.reshape(tile_count, tile_rows, kv_local, query_group_size, HEAD_SIZE)
    page_keys = keys.reshape(pages_local, page_len, kv_local, HEAD_SIZE)
    page_values = values.reshape(pages_local, page_len, kv_local, HEAD_SIZE)

    def one_tile(inputs):
        grouped_queries, tile_index, tile_chosen = inputs
        query_position = offset + tile_index * tile_rows + jnp.arange(tile_rows, dtype=jnp.int32)
        result = (
            jnp.full((tile_rows, heads_local), masked_score, jnp.float32),
            jnp.zeros((tile_rows, heads_local), jnp.float32),
            jnp.zeros((tile_rows, heads_local * HEAD_SIZE), jnp.float32),
        )
        for page_index in range(pages_local):
            visible = jnp.logical_or(
                jnp.logical_not(is_causal[page_index]),
                key_position[None, :] <= query_position[:, None],
            )

            def compute(carry, page_index=page_index, visible=visible):
                return merge_parts(
                    carry,
                    block_scores(
                        grouped_queries, page_keys[page_index], page_values[page_index], visible
                    ),
                )

            def keep(carry):
                return carry

            result = lax.cond(tile_chosen[page_index], compute, keep, result)
        return result

    tiles_out = lax.map(one_tile, (grouped_tiles, jnp.arange(tile_count, dtype=jnp.int32), chosen))
    return tuple((stacked.reshape(row_count, -1) for stacked in tiles_out))


def shards(
    queries,
    keys,
    values,
    page_map,
    selected,
    residual_in,
    out_weight,
    norm_gain,
    gate_weight,
    up_weight,
    down_weight,
):
    ctx_index = lax.axis_index("ctx")
    ctx_count = lax.axis_size("ctx")
    row_count = queries.shape[0]
    row_max, row_total, mixture = owner_pass(
        queries, keys, values, page_map, selected, ctx_index, ctx_count
    )
    heads_local = row_max.shape[1]
    global_max = of_everyone(row_max, "ctx")
    factor = jnp.exp(row_max - global_max)
    scaled = (mixture.reshape(row_count, heads_local, -1) * factor[..., None]).reshape(
        row_count, -1
    )
    summed, weight_sums = in_one_piece(
        (scaled.astype(jnp.bfloat16), (row_total * factor).astype(jnp.bfloat16)), "ctx", 0, 1
    )
    share_rows = summed.shape[0]
    shared = (summed.reshape(share_rows, heads_local, -1) / weight_sums[..., None]).reshape(
        share_rows, -1
    )
    attention = gathered_copies(shared.astype(jnp.bfloat16), "ctx", 0)
    projected = sent_and_summed(
        jnp.dot(attention, out_weight, preferred_element_type=jnp.float32).astype(jnp.bfloat16),
        "head",
        0,
    )
    stream = (residual_in.astype(jnp.float32) + projected).astype(jnp.bfloat16)
    stream_float = stream.astype(jnp.float32)
    square_sums = taken_together(jnp.sum(stream_float * stream_float, axis=1), "ctx")
    normed = (
        stream_float * lax.rsqrt(square_sums / D + norm_epsilon)[:, None] * norm_gain[None, :]
    ).astype(jnp.bfloat16)
    normed_wide, stream_wide = turned_gather((normed, stream), "ctx", (1, 1))
    normed_block, stream_block = (
        lax.all_to_all(normed_wide, "head", split_axis=1, concat_axis=0, tiled=True),
        lax.all_to_all(stream_wide, "head", split_axis=1, concat_axis=0, tiled=True),
    )
    hidden_width = gate_weight.shape[1]
    gate_part = jnp.dot(normed_block, gate_weight, preferred_element_type=jnp.float32)
    up_part = jnp.dot(normed_block, up_weight, preferred_element_type=jnp.float32)
    both_sums = sent_and_summed(
        jnp.concatenate([gate_part, up_part], axis=1).astype(jnp.bfloat16), "head", 0
    )
    hidden_share = (
        jax.nn.gelu(both_sums[:, :hidden_width], approximate=True) * both_sums[:, hidden_width:]
    ).astype(jnp.bfloat16)
    hidden = gathered_copies(hidden_share, "head", 0)
    own_rows = row_count // ctx_count
    mlp_out = sent_and_summed(
        jnp.dot(hidden, down_weight, preferred_element_type=jnp.float32).astype(jnp.bfloat16),
        "ctx",
        0,
    )
    own_stream = lax.dynamic_slice_in_dim(stream_block, ctx_index * own_rows, own_rows, 0)
    return (own_stream.astype(jnp.float32) + mlp_out).astype(jnp.bfloat16)


def solution(mesh):
    in_specs = (
        P(None, "head"),
        P("ctx", None, "head"),
        P("ctx", None, "head"),
        P(),
        P(),
        P("head", "ctx"),
        P("head", "ctx"),
        P("ctx"),
        P("head", "ctx"),
        P("head", "ctx"),
        P("ctx", "head"),
    )
    out_specs = P("ctx", "head")
    return jax.shard_map(shards, mesh=mesh, in_specs=in_specs, out_specs=out_specs, check_vma=False)
```

profile of v0, /device:TPU:32, one launch (start us, length us, event | category | flops | bytes accessed | tf_op | source)
XLA Modules:
  0.0 249.4 jit_solution(12064902824977745670)
XLA Ops:
  0.0 0.9 fusion.51
  1.0 0.9 compare_reduce_fusion
  1.8 0.6 fusion.53
  3.7 1.0 reshape.151
  4.7 2.9 %copy.135 = bf16[2,2048,256]{1,2,0:T(8,128)(2,1)S(1)} copy(bf16[2,2048,256]{2,1,0:T(8,128)(2,1)} %param.18) | data formatting | bytes 4194304 | tf_op args[1]
  7.7 2.5 %copy.138 = bf16[2,2048,2,128]{3,1,2,0:T(8,128)(2,1)} copy(bf16[2,2048,2,128]{1,3,2,0:T(8,128)(2,1)S(1)} %bitcast.163) | data formatting | bytes 4194304
  10.2 4.1 %copy.136 = bf16[2,2048,256]{1,2,0:T(8,128)(2,1)} copy(bf16[2,2048,256]{2,1,0:T(8,128)(2,1)} %param.19) | data formatting | bytes 4194304 | tf_op args[2]
  14.3 21.6 %while.17 = (s32[]{:T(128)}, f32[2,128,4]{1,2,0:T(4,128)S(1)}, f32[2,128,4]{1,0,2:T(2,128)S(1)}, f32[2,128,512]{2,1,0:T(8,128)S(1)}, pred[2,2]{1,0:T(4,128)(4,1)...) while((s32[]{:T(128)}, f32[2,128,4]{1,2,0:T(4,128)S(1)}, ...), condition=%wide.region_11.12_spmd.clone, body=%wide.region_2.11_spmd.clone.sunk | while | flops 1102124160 | bytes 52495788 | solution.py:157
  15.5 0.6 fusion.60
  17.8 0.6 conditional.6
  18.5 5.7 %conditional.7 = (f32[1,128,4]{1,2,0:T(4,128)}, f32[1,128,4]{1,2,0:T(4,128)S(1)}, f32[1,128,512]{1,2,0:T(8,128)S(1)}) conditional(s32[]{:T(128)} %bitcast.156, (f32[128,4]{0,1:T(4,128)}, f32[128,4]{0,1:T(4,128)S(1)}, f32[128,512]{0,1:T(8,128)S(1)}) %conditional.6, (pred[]{:T(512)}, pred[128,2048]{0,1:T(8,128)(4,1)S(1)}, ...), branch_computations={%region_7.7_spmd, %region_8.10_spmd} | conditional | flops 550963200 | bytes 25587764 | solution.py:154
  18.6 2.1 fusion.17
  20.7 1.0 fusion.20
  21.8 1.0 fusion.19
  22.8 1.3 add_bitcast_fusion
  24.2 0.7 constant_dynamic-update-slice_fusion.4
  25.1 0.6 dynamic_slice.33
  26.4 0.6 fusion.60
  28.6 0.6 conditional.6
  29.3 5.7 %conditional.7 = (f32[1,128,4]{1,2,0:T(4,128)}, f32[1,128,4]{1,2,0:T(4,128)S(1)}, f32[1,128,512]{1,2,0:T(8,128)S(1)}) conditional(s32[]{:T(128)} %bitcast.156, (f32[128,4]{0,1:T(4,128)}, f32[128,4]{0,1:T(4,128)S(1)}, f32[128,512]{0,1:T(8,128)S(1)}) %conditional.6, (pred[]{:T(512)}, pred[128,2048]{0,1:T(8,128)(4,1)S(1)}, ...), branch_computations={%region_7.7_spmd, %region_8.10_spmd} | conditional | flops 550963200 | bytes 25587764 | solution.py:154
  29.4 2.1 fusion.17
  31.5 1.0 fusion.20
  32.6 1.0 fusion.19
  33.6 1.3 add_bitcast_fusion
  35.0 0.7 constant_dynamic-update-slice_fusion.4
  35.9 0.7 broadcast_in_dim.130
  36.6 19.4 %all-to-all-start = ((f32[32,256,4]{1,2,0:T(4,128)}), f32[32,256,4]{1,2,0:T(4,128)S(1)}, u32[]{:S(2)}, u32[]{:S(2)}) async-start(f32[32,256,4]{1,2,0:T(4,128)} %broadcast_in_dim.130), calls=%async_computation | async-start | bytes 262144 | tf_op jit(solution)/shard_map/all_to_all | solution.py:17
  56.4 9.3 %all-to-all-done = f32[32,256,4]{1,2,0:T(4,128)S(1)} async-done(((f32[32,256,4]{1,2,0:T(4,128)}), f32[32,256,4]{1,2,0:T(4,128)S(1)}, u32[]{:S(2)}, u32[]{:S(2)}) %all-to-all-start) | async-done | bytes 131104 | tf_op jit(solution)/shard_map/all_to_all | solution.py:17
  66.9 16.4 %all_to_all.76 = bf16[32,8,516]{2,1,0:T(8,128)(2,1)S(1)} all-to-all(bf16[32,8,516]{2,1,0:T(8,128)(2,1)S(1)} %pad_maximum_fusion.1), channel_id=1, replica_groups=mesh['ctx'=32,'head'=8] {'ctx'}, dimensions={0} | all-to-all | bytes 528384 | tf_op jit(solution)/shard_map/all_to_all | solution.py:32
  83.6 15.3 %all_to_all.77 = bf16[32,8,512]{2,1,0:T(8,128)(2,1)S(1)} all-to-all(bf16[32,8,512]{2,1,0:T(8,128)(2,1)S(1)} %broadcast_in_dim.131), channel_id=1, replica_groups=mesh['ctx'=32,'head'=8] {'ctx'}, dimensions={0} | all-to-all | bytes 524288 | tf_op jit(solution)/shard_map/all_to_all | solution.py:17
  99.2 10.4 %all_to_all.78 = bf16[8,32,168]{2,1,0:T(8,128)(2,1)S(1)} all-to-all(bf16[8,32,168]{2,1,0:T(8,128)(2,1)S(1)} %bitcast.169), channel_id=1, replica_groups=mesh['ctx'=32,'head'=8] {'head'}, dimensions={0} | all-to-all | bytes 172032 | tf_op jit(solution)/shard_map/all_to_all | solution.py:32
  109.8 13.0 %all_to_all.79 = f32[32,1,32]{2,1,0:T(1,128)S(1)} all-to-all(f32[32,1,32]{2,1,0:T(1,128)S(1)} %broadcast_in_dim.132), channel_id=1, replica_groups=mesh['ctx'=32,'head'=8] {'ctx'}, dimensions={0} | all-to-all | bytes 8192 | tf_op jit(solution)/shard_map/all_to_all | solution.py:17
  123.0 48.3 %all-gather = bf16[32,168,64]{1,2,0:T(8,128)(2,1)S(1)} all-gather(bf16[1,168,64]{1,2,0:T(8,128)(2,1)S(1)} %maximum_bitcast_fusion.1), channel_id=1, replica_groups=mesh['ctx'=32,'head'=8] {'ctx'}, dimensions={0}, use_global_device_ids=true | all-gather | bytes 709632 | tf_op jit(solution)/shard_map/all_gather | solution.py:63
  171.3 0.6 copy.150
  171.9 1.7 reshape.164
  173.7 0.7 all_to_all.60
  174.4 11.3 %all_to_all.80 = bf16[32,8,672]{2,0,1:T(8,128)(2,1)S(1)} all-to-all(bf16[32,8,672]{2,0,1:T(8,128)(2,1)S(1)} %copy.152), channel_id=1, replica_groups=mesh['ctx'=32,'head'=8] {'head'}, dimensions={1} | all-to-all | bytes 688128 | tf_op jit(solution)/shard_map/all_to_all | solution.py:207
  186.2 1.7 convolution_convert_fusion.1
  188.2 14.9 %all_to_all.81 = bf16[8,32,1344]{2,1,0:T(8,128)(2,1)S(1)} all-to-all(bf16[8,32,1344]{2,1,0:T(8,128)(2,1)S(1)} %pad_maximum_fusion), channel_id=1, replica_groups=mesh['ctx'=32,'head'=8] {'head'}, dimensions={0} | all-to-all | bytes 1376256 | tf_op jit(solution)/shard_map/all_to_all | solution.py:32
  203.3 11.3 %all_to_all.82 = bf16[8,32,672]{2,1,0:T(8,128)(2,1)S(1)} all-to-all(bf16[8,32,672]{2,1,0:T(8,128)(2,1)S(1)} %broadcast_in_dim.133), channel_id=1, replica_groups=mesh['ctx'=32,'head'=8] {'head'}, dimensions={0} | all-to-all | bytes 688128 | tf_op jit(solution)/shard_map/all_to_all | solution.py:17
  215.2 0.9 copy.153
  216.1 5.7 %all-to-all-start.9 = ((bf16[32,8,672]{2,1,0:T(8,128)(2,1)}), bf16[32,8,672]{2,1,0:T(8,128)(2,1)S(1)}, u32[]{:S(2)}, u32[]{:S(2)}) async-start(bf16[32,8,672]{2,1,0:T(8,128)(2,1)} %bitcast.59), calls=%async_computation.9 | async-start | bytes 786432 | tf_op jit(solution)/shard_map/all_to_all | solution.py:32
  221.9 0.7 all_to_all.56
  222.6 0.8 copy.151
  223.4 13.0 %all-to-all-done.9 = bf16[32,8,672]{2,1,0:T(8,128)(2,1)S(1)} async-done(((bf16[32,8,672]{2,1,0:T(8,128)(2,1)}), bf16[32,8,672]{2,1,0:T(8,128)(2,1)S(1)}, u32[]{:S(2)}, u32[]{:S(2)}) %all-to-all-start.9) | async-done | bytes 344096 | tf_op jit(solution)/shard_map/all_to_all | solution.py:32
  236.4 3.5 %all-to-all-start.5 = ((bf16[32,8,672]{2,0,1:T(8,128)(2,1)}), bf16[32,8,672]{2,0,1:T(8,128)(2,1)S(1)}, u32[]{:S(2)}, u32[]{:S(2)}) async-start(bf16[32,8,672]{2,0,1:T(8,128)(2,1)} %copy.151), calls=%async_computation.5 | async-start | bytes 786432 | tf_op jit(solution)/shard_map/all_to_all | solution.py:208
  240.0 8.8 %all-to-all-done.5 = bf16[32,8,672]{2,0,1:T(8,128)(2,1)S(1)} async-done(((bf16[32,8,672]{2,0,1:T(8,128)(2,1)}), bf16[32,8,672]{2,0,1:T(8,128)(2,1)S(1)}, u32[]{:S(2)}, u32[]{:S(2)}) %all-to-all-start.5) | async-done | bytes 344096 | tf_op jit(solution)/shard_map/all_to_all | solution.py:208
  248.7 0.6 add_convert_fusion.1
  (88 shorter events, 7.6 us)
Async XLA Ops:
  0.0 185.7 %copy-start = (bf16[672,672]{1,0:T(8,128)(2,1)S(1)}, bf16[672,672]{1,0:T(8,128)(2,1)}, u32[]{:S(2)}) copy-start(bf16[672,672]{1,0:T(8,128)(2,1)} %param.26) | copy-start | bytes 2709508
  10.2 4.1 %copy-start.4 = (f32[2,128,512]{2,1,0:T(8,128)S(1)}, f32[2,128,512]{2,1,0:T(8,128)}, u32[]{:S(2)}) copy-start(f32[2,128,512]{2,1,0:T(8,128)} %custom-call.2) | copy-start | bytes 1572868
  18.5 2.2 copy-start.2
  29.3 2.2 copy-start.2
  35.9 63.0 %copy-start.5 = (bf16[512,168]{0,1:T(8,128)(2,1)S(1)}, bf16[512,168]{0,1:T(8,128)(2,1)}, u32[]{:S(2)}) copy-start(bf16[512,168]{0,1:T(8,128)(2,1)} %param.23) | copy-start | bytes 516100
  35.9 73.8 %copy-start.6 = (bf16[32,168]{1,0:T(8,128)(2,1)S(1)}, bf16[32,168]{1,0:T(8,128)(2,1)}, u32[]{:S(2)}) copy-start(bf16[32,168]{1,0:T(8,128)(2,1)} %param.22) | copy-start | bytes 32260
  35.9 87.0 %copy-start.7 = (f32[168]{0:T(256)S(1)}, f32[168]{0:T(256)}, u32[]{:S(2)}) copy-start(f32[168]{0:T(256)} %param.24) | copy-start | bytes 2020
  36.6 29.1 %all-to-all-start = ((f32[32,256,4]{1,2,0:T(4,128)}), f32[32,256,4]{1,2,0:T(4,128)S(1)}, u32[]{:S(2)}, u32[]{:S(2)}) async-start(f32[32,256,4]{1,2,0:T(4,128)} %broadcast_in_dim.130), calls=%async_computation | async-start | bytes 262144 | tf_op jit(solution)/shard_map/all_to_all | solution.py:17
  185.7 28.9 %copy-start.3 = (bf16[672,672]{1,0:T(8,128)(2,1)S(1)}, bf16[672,672]{1,0:T(8,128)(2,1)}, u32[]{:S(2)}) copy-start(bf16[672,672]{1,0:T(8,128)(2,1)} %param.27) | copy-start | bytes 2709508
  216.1 20.3 %all-to-all-start.9 = ((bf16[32,8,672]{2,1,0:T(8,128)(2,1)}), bf16[32,8,672]{2,1,0:T(8,128)(2,1)S(1)}, u32[]{:S(2)}, u32[]{:S(2)}) async-start(bf16[32,8,672]{2,1,0:T(8,128)(2,1)} %bitcast.59), calls=%async_computation.9 | async-start | bytes 786432 | tf_op jit(solution)/shard_map/all_to_all | solution.py:32
  236.4 12.3 %all-to-all-start.5 = ((bf16[32,8,672]{2,0,1:T(8,128)(2,1)}), bf16[32,8,672]{2,0,1:T(8,128)(2,1)S(1)}, u32[]{:S(2)}, u32[]{:S(2)}) async-start(bf16[32,8,672]{2,0,1:T(8,128)(2,1)} %copy.151), calls=%async_computation.5 | async-start | bytes 786432 | tf_op jit(solution)/shard_map/all_to_all | solution.py:208
where the time goes:
time: 249 us
  blocking collectives  141 us (57%)
  waiting for transfers between devices  31.1 us (12%)
  starting transfers between devices  28.6 us (11%)
  local copies, waits for them, and re-layouts  24.4 us (10%)
  matrix products  9.2 us (4%)
  other arithmetic  9.15 us (4%)
  loops' own time  4.14 us (2%)
    all_gather x1, blocking collectives, turned_gather(): filled = lax.all_gather(both, axis, axis=0, tiled=True)  48.3 us
    all_to_all x3, blocking collectives, sent_and_summed(): lax.all_to_all(parts, axis, split_axis=0, concat_axis=0, tiled=True)  41.8 us
    all_to_all x3, blocking collectives, sent_to_all(): return lax.all_to_all(copies, axis, split_axis=0, concat_axis=0, tiled=True)  39.6 us
    all_to_all x1, starting transfers between devices, sent_to_all(): return lax.all_to_all(copies, axis, split_axis=0, concat_axis=0, tiled=True)  19.4 us
    all_to_all x1, waiting for transfers between devices, sent_and_summed(): lax.all_to_all(parts, axis, split_axis=0, concat_axis=0, tiled=True)  13 us
    all_to_all x1, blocking collectives, shards(): lax.all_to_all(normed_wide, 'head', split_axis=1, concat_axis=0, tiled=True)  11.3 us
    unnamed x16, local copies, waits for them, and re-layouts  11.3 us
    all_to_all x1, waiting for transfers between devices, sent_to_all(): return lax.all_to_all(copies, axis, split_axis=0, concat_axis=0, tiled=True)  9.3 us
  transfers between devices with their start and end apart: 3, of which 3 were waited for; matrix products, arithmetic and copies ran while one was open for 0% of the time, Pallas kernels for 0%

commit v1 on v0

v1 whole, which is shorter than its diff:
```python
import functools
import math

import jax
import jax.numpy as jnp
from jax import lax
from jax.experimental import pallas as pl
from jax.experimental.pallas import tpu as pltpu
from jax.sharding import Mesh
from jax.sharding import PartitionSpec as P

D = 5376
HEAD = 128
LAST_PAGE = 63
BF = jnp.bfloat16
F32 = jnp.float32
NEG = -1e30
EXP2_SCALE = 168.0 ** (-0.5) * math.log2(math.e)
EPSILON = 1e-06
CTX = ("z", "x")
HEADS = ("y", "core")
ALL = ("z", "x", "y", "core")
NZ, NX, NY, NC = 8, 4, 4, 2
GU_HALF = 768

VMEM = pl.BlockSpec(memory_space=pltpu.VMEM)
SMEM = pl.BlockSpec(memory_space=pltpu.SMEM)
HBM = pl.BlockSpec(memory_space=pl.ANY)


def pieces(value):
    high = value.astype(BF).astype(F32)
    rest = value - high
    middle = rest.astype(BF).astype(F32)
    return high, middle, rest - middle


def attend_kernel(
    pm, sel, me, q_ref, k_hbm, v_hbm, o_ref, kbuf, vbuf, ksem, vsem, s_ref, m_ref, l_ref, acc_ref
):
    chosen = [[jnp.int32(0), jnp.int32(0)], [jnp.int32(0), jnp.int32(0)]]
    causal = [jnp.int32(0), jnp.int32(0)]
    for t in range(2):
        for j in range(8):
            logical = sel[t, j]
            slot = pm[logical]
            for p in range(2):
                hit = (slot == me[0] * 2 + p).astype(jnp.int32)
                chosen[p][t] = chosen[p][t] | hit
                causal[p] = causal[p] | (hit * (logical == LAST_PAGE).astype(jnp.int32))
    used = [chosen[p][0] | chosen[p][1] for p in range(2)]

    def copies(p):
        return (
            pltpu.make_async_copy(k_hbm.at[p], kbuf.at[p], ksem.at[p]),
            pltpu.make_async_copy(v_hbm.at[p], vbuf.at[p], vsem.at[p]),
        )

    for p in range(2):

        @pl.when(used[p] != 0)
        def _(p=p):
            for c in copies(p):
                c.start()

    m_ref[...] = jnp.full_like(m_ref, NEG)
    l_ref[...] = jnp.zeros_like(l_ref)
    acc_ref[...] = jnp.zeros_like(acc_ref)

    def combo(p, t, is_causal):
        row = lax.broadcasted_iota(jnp.int32, (256, 512), 0)
        col = lax.broadcasted_iota(jnp.int32, (256, 512), 1)
        limit = jnp.where(is_causal != 0, 1792 - 1536 + t * 128, 1 << 20)
        visible = col <= (row & 127) + limit
        rows = pl.ds(pl.multiple_of(t * 128, 128), 128)
        for kv in range(2):
            lanes = slice(kv * 128, (kv + 1) * 128)
            q2 = jnp.concatenate(
                [q_ref[rows, (2 * kv + g) * 128 : (2 * kv + g + 1) * 128] for g in range(2)], axis=0
            )
            top = jnp.full((256, 128), NEG, F32)
            for j in range(4):
                s = lax.dot_general(
                    q2,
                    kbuf[p, j * 512 : (j + 1) * 512, lanes],
                    (((1,), (1,)), ((), ())),
                    preferred_element_type=F32,
                )
                if j == 3:
                    s = jnp.where(visible, s, NEG)
                s_ref[:, j * 512 : (j + 1) * 512] = s
                for a in range(4):
                    top = jnp.maximum(top, s[:, a * 128 : (a + 1) * 128])
            i = t * 2 + kv
            m_old = m_ref[i]
            m_new = jnp.maximum(m_old, jnp.max(top, axis=1, keepdims=True))
            alpha = jnp.exp2((m_old - m_new) * EXP2_SCALE)
            m_wide = jnp.concatenate([m_new] * 4, axis=1)
            total = jnp.zeros((256, 128), F32)
            mixture = acc_ref[i] * alpha
            for j in range(4):
                w = jnp.exp2((s_ref[:, j * 512 : (j + 1) * 512] - m_wide) * EXP2_SCALE)
                for a in range(4):
                    total = total + w[:, a * 128 : (a + 1) * 128]
                mixture = mixture + jnp.dot(
                    w.astype(BF),
                    vbuf[p, j * 512 : (j + 1) * 512, lanes],
                    preferred_element_type=F32,
                )
            m_ref[i] = m_new
            l_ref[i] = l_ref[i] * alpha + jnp.sum(total, axis=1, keepdims=True)
            acc_ref[i] = mixture

    for p in range(2):

        @pl.when(used[p] != 0)
        def _(p=p):
            for c in copies(p):
                c.wait()

            def tile(t, carry):
                picked = jnp.where(t == 0, chosen[p][0], chosen[p][1])

                @pl.when(picked != 0)
                def _():
                    combo(p, t, causal[p])

                return carry

            lax.fori_loop(0, 2, tile, 0)

    lane = lax.broadcasted_iota(jnp.int32, (128, 128), 1)
    for t in range(2):
        block = jnp.zeros((128, 128), F32)
        for h in range(4):
            i, rows = t * 2 + h // 2, slice((h % 2) * 128, (h % 2 + 1) * 128)
            total = l_ref[i, rows, :]
            some = total > 0.0
            safe = jnp.where(some, total, 1.0)
            level = jnp.where(some, m_ref[i, rows, :] * EXP2_SCALE + jnp.log2(safe), NEG)
            o_ref[t * 128 : (t + 1) * 128, h * 128 : (h + 1) * 128] = (
                acc_ref[i, rows, :] / safe
            ).astype(BF)
            for n, piece in enumerate(pieces(level)):
                block = jnp.where(lane == h + 4 * n, piece, block)
        o_ref[t * 128 : (t + 1) * 128, 512:640] = block.astype(BF)


def attend(page_map, selected, me, queries, keys, values):
    return pl.pallas_call(
        attend_kernel,
        out_shape=jax.ShapeDtypeStruct((256, 640), BF),
        in_specs=[SMEM, SMEM, SMEM, VMEM, HBM, HBM],
        out_specs=VMEM,
        scratch_shapes=[
            pltpu.VMEM((2, 2048, 256), BF),
            pltpu.VMEM((2, 2048, 256), BF),
            pltpu.SemaphoreType.DMA((2,)),
            pltpu.SemaphoreType.DMA((2,)),
            pltpu.VMEM((256, 2048), F32),
            pltpu.VMEM((4, 256, 128), F32),
            pltpu.VMEM((4, 256, 128), F32),
            pltpu.VMEM((4, 256, 128), F32),
        ],
        compiler_params=pltpu.CompilerParams(vmem_limit_bytes=32 << 20),
        cost_estimate=pl.CostEstimate(
            flops=4 * 10**9, transcendentals=4 * 10**6, bytes_accessed=10 * 2**20
        ),
        name="attend",
    )(page_map, selected, me, queries, keys, values)


def merge_kernel(x_ref, o_ref):
    x = x_ref[...].astype(F32)
    marks = x[:, :, 512:640].reshape(256, 128).astype(BF)
    source = lax.broadcasted_iota(jnp.int32, (128, 512), 0)
    target = lax.broadcasted_iota(jnp.int32, (128, 512), 1)
    spread = jnp.where((source < 12) & ((source & 3) == target // 128), 1.0, 0.0).astype(BF)
    level = jnp.dot(marks, spread, preferred_element_type=F32).reshape(32, 8, 512)
    top = jnp.max(level, axis=0, keepdims=True)
    weight = jnp.exp2(level - top)
    total = jnp.sum(weight, axis=0)
    mixed = jnp.sum(weight * x[:, :, :512], axis=0)
    o_ref[...] = (mixed / total).astype(BF)


def project_kernel(a_ref, w_ref, o_ref):
    a = a_ref[...]
    for z in range(NZ):
        o_ref[z] = jnp.dot(
            a, w_ref[z * 512 : (z + 1) * 512, :], preferred_element_type=F32
        ).astype(BF)


def gate_up_kernel(ids, x_ref, g_ref, u_ref, mine_ref, other_ref, own_ref, stream, normed):
    for x in range(NX):
        lanes = slice(x * 168, (x + 1) * 168)
        block = x_ref[:, x, :, :].astype(F32)
        part = block[:, :32, :].reshape(256, 168)
        tail = block[0, 32:40, :]
        gain = tail[0:1] + tail[1:2] + tail[2:3]
        stream[:, lanes] = part
        normed[:, lanes] = (part * gain).astype(BF)
    own_ref[...] = stream[pl.ds(pl.multiple_of(ids[0] * 8, 8), 8), :].astype(BF)
    core = ids[1]
    lane = lax.broadcasted_iota(jnp.int32, (128, GU_HALF - 672), 1)
    for ref, start in ((other_ref, (1 - core) * 128), (mine_ref, core * 128)):
        rows = pl.ds(pl.multiple_of(start, 128), 128)
        a = normed[rows, :]
        s = stream[rows, :]
        squares = jnp.sum(s * s, axis=1, keepdims=True)
        marks = jnp.zeros((128, GU_HALF - 672), F32)
        for n, piece in enumerate(pieces(squares)):
            marks = jnp.where(lane == n, piece, marks)
        ref[:, 0:672] = jnp.dot(a, g_ref[...], preferred_element_type=F32).astype(BF)
        ref[:, 672:GU_HALF] = marks.astype(BF)
        ref[:, GU_HALF : GU_HALF + 672] = jnp.dot(
            a, u_ref[...], preferred_element_type=F32
        ).astype(BF)
        ref[:, GU_HALF + 672 :] = jnp.zeros((128, GU_HALF - 672), BF)


def pair_kernel(a_ref, b_ref, o_ref):
    both = a_ref[...].astype(F32) + b_ref[...].astype(F32)
    o_ref[...] = both.astype(BF)
    squares = both[:, 672:673] + both[:, 673:674] + both[:, 674:675]
    lane = lax.broadcasted_iota(jnp.int32, (128, GU_HALF - 672), 1)
    marks = jnp.zeros((128, GU_HALF - 672), F32)
    for n, piece in enumerate(pieces(squares)):
        marks = jnp.where(lane == n, piece, marks)
    o_ref[:, 672:GU_HALF] = marks.astype(BF)


def hidden_kernel(x_ref, o_ref):
    both = jnp.sum(x_ref[...].astype(F32), axis=0)
    squares = both[:, 672:673] + both[:, 673:674] + both[:, 674:675]
    factor = lax.rsqrt(squares / D + EPSILON)
    gate = both[:, 0:672] * factor
    up = both[:, GU_HALF : GU_HALF + 672] * factor
    o_ref[...] = (jax.nn.gelu(gate, approximate=True) * up).astype(BF)


def down_kernel(ids, a_ref, b_ref, w_ref, o_ref):
    core = ids[1]
    for ref, start in ((a_ref, core * 128), (b_ref, (1 - core) * 128)):
        rows = pl.ds(pl.multiple_of(start, 128), 128)
        o_ref[rows, :] = jnp.dot(ref[...], w_ref[...], preferred_element_type=F32).astype(BF)


def final_kernel(x_ref, s_ref, o_ref):
    o_ref[...] = (jnp.sum(x_ref[...].astype(F32), axis=0) + s_ref[...].astype(F32)).astype(BF)


def call(kernel, shapes, specs, *args, scratch=()):
    many = isinstance(shapes, list)
    outs = [jax.ShapeDtypeStruct(s, BF) for s in (shapes if many else [shapes])]
    return pl.pallas_call(
        kernel,
        out_shape=outs if many else outs[0],
        in_specs=specs,
        out_specs=[VMEM] * len(outs) if many else VMEM,
        scratch_shapes=scratch,
        compiler_params=pltpu.CompilerParams(vmem_limit_bytes=32 << 20),
        name=kernel.__name__,
    )(*args)


def exchange(parts, axis):
    return lax.all_to_all(parts, axis, split_axis=0, concat_axis=0, tiled=True)


def to_all(part, axis):
    return exchange(jnp.broadcast_to(part, (lax.axis_size(axis), *part.shape)), axis)


def place(z, x, h):
    return (z * NX + x) * NY * NC + h


def shards(
    queries, keys, values, page_map, selected, residual_in, out_weight, norm_gain, gate_weight, up_weight, down_weight
):
    ctx = (lax.axis_index("z") * NX + lax.axis_index("x")).astype(jnp.int32)
    core = lax.axis_index("core").astype(jnp.int32)
    ids = jnp.stack([ctx, core])
    wide_weight = lax.all_gather(out_weight, "z", axis=0, tiled=True)
    gain_high = lax.reduce_precision(norm_gain, 8, 7)
    gain_rest = norm_gain - gain_high
    gain_middle = lax.reduce_precision(gain_rest, 8, 7)
    gain_rows = jnp.stack([gain_high, gain_middle, gain_rest - gain_middle]).astype(BF)
    carried = jnp.concatenate([residual_in, gain_rows, jnp.zeros((5, 168), BF)], axis=0)
    turned = lax.ppermute(
        carried,
        ALL,
        [(place(z, x, h), place(h, x, z)) for z in range(NZ) for x in range(NX) for h in range(NZ)],
    )

    sent = attend(page_map, selected, ids, queries, keys, values)
    arrived = exchange(sent.reshape(32, 8, 640), CTX)
    share = call(merge_kernel, (8, 512), [VMEM], arrived)
    attention = to_all(share, "x").reshape(32, 512)
    partial = call(project_kernel, (NZ, 32, 168), [VMEM, VMEM], attention, wide_weight)
    projected = exchange(partial, HEADS).astype(F32).sum(axis=0)
    stream = (turned[:32].astype(F32) + projected).astype(BF)
    rows = to_all(jnp.concatenate([stream, turned[32:]], axis=0), CTX)
    mine, other, own_stream = call(
        gate_up_kernel,
        [(128, 2 * GU_HALF), (128, 2 * GU_HALF), (8, 672)],
        [SMEM, VMEM, VMEM, VMEM],
        ids,
        rows.reshape(NZ, NX, 40, 168),
        gate_weight,
        up_weight,
        scratch=[pltpu.VMEM((256, 672), F32), pltpu.VMEM((256, 672), BF)],
    )
    swap = [(0, 1), (1, 0)]
    pair = call(pair_kernel, (128, 2 * GU_HALF), [VMEM, VMEM], mine, lax.ppermute(other, "core", swap))
    quarters = exchange(pair.reshape(NY, 32, 2 * GU_HALF), "y")
    hidden = call(hidden_kernel, (32, 672), [VMEM], quarters)
    hidden_half = to_all(hidden, "y").reshape(128, 672)
    hidden_other = lax.ppermute(hidden_half, "core", swap)
    down = call(
        down_kernel, (256, 672), [SMEM, VMEM, VMEM, VMEM], ids, hidden_half, hidden_other, down_weight
    )
    out_parts = exchange(down.reshape(32, 8, 672), CTX)
    return call(final_kernel, (8, 672), [VMEM, VMEM], out_parts, own_stream)


def solution(mesh):
    fine = Mesh(mesh.devices.reshape(NZ, NX, NY, NC), ALL)
    in_specs = (
        P(None, HEADS),
        P(CTX, None, HEADS),
        P(CTX, None, HEADS),
        P(),
        P(),
        P(HEADS, CTX),
        P(HEADS, CTX),
        P(CTX),
        P(HEADS, CTX),
        P(HEADS, CTX),
        P(CTX, HEADS),
    )
    return jax.shard_map(shards, mesh=fine, in_specs=in_specs, out_specs=P(CTX, HEADS), check_vma=False)
```

time: 249 us -> 159 us (0.64)
  blocking collectives: 141 us -> 113 us
  waiting for transfers between devices: 31.1 us -> 8.94 us
  starting transfers between devices: 28.6 us -> 8.28 us
  local copies, waits for them, and re-layouts: 24.4 us -> 8.96 us
  between operations: 1.59 us -> 13.6 us
  matrix products: 9.2 us -> 0 us
  other arithmetic: 9.15 us -> 0.13 us
  Pallas kernels: 0 us -> 6.35 us
  loops' own time: 4.14 us -> 0 us
    all_gather x1 -> x0, blocking collectives: 48.3 us -> none  [turned_gather(): filled = lax.all_gather(both, axis, axis=0, tiled=True)]
    all_to_all x3 -> x1, waiting for transfers between devices: 31.1 us -> 0.85 us  [exchange(): return lax.all_to_all(parts, axis, split_axis=0, concat_axis=0, tiled=True)]
    all_to_all x3 -> x1, starting transfers between devices: 28.6 us -> 4.47 us  [exchange(): return lax.all_to_all(parts, axis, split_axis=0, concat_axis=0, tiled=True)]
    all_to_all x7 -> x6, blocking collectives: 92.7 us -> 113 us  [exchange(): return lax.all_to_all(parts, axis, split_axis=0, concat_axis=0, tiled=True)]
    dot_general x8 -> x0, matrix products: 9.2 us -> none  [the longest x2 4.13 us: block_scores(): jnp.einsum('rkgd,jkd->kgrj', grouped_queries, block_keys, preferred_eleme...]
    pallas_call x0 -> x8, Pallas kernels: none -> 6.35 us  [the longest x7 5.25 us: call(): pl.pallas_call(kernel, out_shape=outs if many else outs[0], in_specs=spec...]
    ppermute x0 -> x3, waiting for transfers between devices: none -> 4.61 us  [the longest x1 1.71 us: shards(): lax.ppermute(other, 'core', swap)]
    another operation x5 -> x0, loops' own time: 4.14 us -> none  [the longest x1 3.98 us: owner_pass(): lax.map(one_tile, (grouped_tiles, jnp.arange(tile_count, dtype=jnp.int32)...]
  transfers between devices with their start and end apart: 3 -> 5, of which waited for: 3 -> 5; matrix products, arithmetic and copies ran while one was open for 0% -> 0% of each run, Pallas kernels for 0% -> 1%
where the time goes in v1:
time: 159 us
  blocking collectives  113 us (71%)
  between operations  13.6 us (9%)
  local copies, waits for them, and re-layouts  8.96 us (6%)
  waiting for transfers between devices  8.94 us (6%)
  starting transfers between devices  8.28 us (5%)
  Pallas kernels  6.35 us (4%)
    all_to_all x6, blocking collectives, exchange(): return lax.all_to_all(parts, axis, split_axis=0, concat_axis=0, tiled=True)  113 us
    unnamed x23, local copies, waits for them, and re-layouts  8.85 us
    pallas_call x7, Pallas kernels, call(): pl.pallas_call(kernel, out_shape=outs if many else outs[0], in_specs=spec...  5.25 us
    all_to_all x1, starting transfers between devices, exchange(): return lax.all_to_all(parts, axis, split_axis=0, concat_axis=0, tiled=True)  4.47 us
    ppermute x1, starting transfers between devices, shards(): lax.ppermute(carried, ALL, [(place(z, x, h), place(h, x, z)) for z in ran...  3.72 us
    all_gather x1, waiting for transfers between devices, shards(): wide_weight = lax.all_gather(out_weight, 'z', axis=0, tiled=True)  3.47 us
  transfers between devices with their start and end apart: 5, of which 5 were waited for; matrix products, arithmetic and copies ran while one was open for 0% of the time, Pallas kernels for 1%

profile of v1, /device:TPU:32, one launch (start us, length us, event | category | flops | bytes accessed | tf_op | source)
XLA Modules:
  0.0 158.7 jit_solution(11571264370420582595)
XLA Ops:
  6.5 0.0 all-gather.2.cloned.1.call-start
  6.5 1.8 %copy.12 = bf16[512,168]{1,0:T(8,128)(2,1)} copy(bf16[512,168]{0,1:T(8,128)(2,1)} %param.17) | data formatting | bytes 344064 | tf_op args[6]
  8.3 0.0 all-gather.2.cloned.1.call-update
  8.3 0.1 pad_add_fusion.me.ids
  8.4 0.0 copy-start.4
  8.4 1.6 %copy-done.4 = bf16[2,2048,256]{2,1,0:T(8,128)(2,1)S(1)} copy-done((bf16[2,2048,256]{2,1,0:T(8,128)(2,1)S(1)}, bf16[2,2048,256]{2,1,0:T(8,128)(2,1)}, u32[]{:S(2)}) %copy-start.4) | copy-done | bytes 2097176
  10.0 0.0 copy-start.5
  10.0 1.6 %copy-done.5 = bf16[2,2048,256]{2,1,0:T(8,128)(2,1)S(1)} copy-done((bf16[2,2048,256]{2,1,0:T(8,128)(2,1)S(1)}, bf16[2,2048,256]{2,1,0:T(8,128)(2,1)}, u32[]{:S(2)}) %copy-start.5) | copy-done | bytes 2097176
  11.6 0.0 copy-start.6
  11.6 0.9 copy-done.6
  12.5 0.0 copy-start.7
  12.5 0.7 copy-done.7
  13.2 0.0 copy-start.8
  13.2 0.7 copy-done.8
  13.9 1.1 attend.1
  15.0 0.0 copy-start.10
  15.0 0.0 copy-start.9
  15.0 30.4 %all_to_all.35.x_ref = bf16[32,8,640]{2,1,0:T(8,128)(2,1)S(1)} all-to-all(bf16[32,8,640]{2,1,0:T(8,128)(2,1)S(1)} %bitcast.13), channel_id=1, replica_groups=mesh['z'=8,'x'=4,'y'=4,'core'=2] {'z','x'}, dimensions={0} | all-to-all | bytes 655360 | tf_op jit(solution)/shard_map/all_to_all | solution.py:269
  45.4 0.3 merge_kernel.1
  45.8 8.6 %all_to_all.36 = bf16[4,8,512]{2,1,0:T(8,128)(2,1)S(1)} all-to-all(bf16[4,8,512]{2,1,0:T(8,128)(2,1)S(1)} %broadcast_in_dim.13), channel_id=1, replica_groups=mesh['z'=8,'x'=4,'y'=4,'core'=2] {'x'}, dimensions={0} | all-to-all | bytes 65536 | tf_op jit(solution)/shard_map/all_to_all | solution.py:269
  54.3 3.5 %all-gather.2.cloned.1.call-done.w_ref = bf16[4096,168]{1,0:T(8,128)(2,1)} async-done(((bf16[512,168]{1,0:T(8,128)(2,1)}), bf16[4096,168]{1,0:T(8,128)(2,1)}) %all-gather.2.cloned.1.call-update) | async-done | bytes 1376272 | tf_op jit(solution)/shard_map/all_gather | solution.py:286
  57.8 0.0 copy-start
  57.8 1.6 %copy-done = bf16[4096,168]{1,0:T(8,128)(2,1)S(1)} copy-done((bf16[4096,168]{1,0:T(8,128)(2,1)S(1)}, bf16[4096,168]{1,0:T(8,128)(2,1)}, u32[]{:S(2)}) %copy-start) | copy-done | bytes 1376280
  59.4 0.0 copy-start.1
  59.4 1.1 project_kernel.1
  60.5 4.5 %all-to-all-start.2 = ((bf16[8,32,168]{2,1,0:T(8,128)(2,1)}), bf16[8,32,168]{2,1,0:T(8,128)(2,1)S(1)}, u32[]{:S(2)}, u32[]{:S(2)}) async-start(bf16[8,32,168]{2,1,0:T(8,128)(2,1)} %project_kernel.1), calls=%async_computation.2 | async-start | bytes 262144 | tf_op jit(solution)/shard_map/all_to_all | solution.py:269
  65.0 0.0 copy-done.10
  65.1 0.0 copy-done.9
  65.1 3.7 %collective-permute-start = (bf16[40,168]{1,0:T(8,128)(2,1)S(1)}, bf16[40,168]{1,0:T(8,128)(2,1)S(1)}, u32[]{:S(2)}, u32[]{:S(2)}) collective-permute-start(bf16[40,168]{1,0:T(8,128)(2,1)S(1)} %concatenate.7), channel_id=1, source_target_pairs={{0,0},{1,32},{2,64},{3,96},{4,128},{5,160},{6,192},{7,224},{8,8},{... | collective-permute-start | bytes 40328 | tf_op jit(solution)/shard_map/ppermute | solution.py:292
  68.8 1.5 collective-permute-done
  70.3 0.8 all-to-all-done.2
  71.2 33.2 %all_to_all.37 = bf16[32,40,168]{2,1,0:T(8,128)(2,1)S(1)} all-to-all(bf16[32,40,168]{2,1,0:T(8,128)(2,1)S(1)} %broadcast_in_dim.14), channel_id=1, replica_groups=mesh['z'=8,'x'=4,'y'=4,'core'=2] {'z','x'}, dimensions={0} | all-to-all | bytes 860160 | tf_op jit(solution)/shard_map/all_to_all | solution.py:269
  104.5 0.0 copy-done.1
  104.5 0.0 copy-done.2
  104.5 1.5 gate_up_kernel.1
  106.0 0.0 copy-start.3
  106.0 0.1 collective-permute-start.1
  106.1 1.7 %collective-permute-done.1.b_ref = bf16[128,1536]{1,0:T(8,128)(2,1)S(1)} collective-permute-done((bf16[128,1536]{1,0:T(8,128)(2,1)S(1)}, bf16[128,1536]{1,0:T(8,128)(2,1)S(1)}, u32[]{:S(2)}, u32[]{:S(2)}) %collective-permute-start.1) | collective-permute-done | bytes 393248 | tf_op jit(solution)/shard_map/ppermute | solution.py:317
  107.8 0.4 pair_kernel.1
  108.2 11.4 %all_to_all.38.x_ref = bf16[4,32,1536]{2,1,0:T(8,128)(2,1)S(1)} all-to-all(bf16[4,32,1536]{2,1,0:T(8,128)(2,1)S(1)} %bitcast.10), channel_id=1, replica_groups=mesh['z'=8,'x'=4,'y'=4,'core'=2] {'y'}, dimensions={0} | all-to-all | bytes 786432 | tf_op jit(solution)/shard_map/all_to_all | solution.py:269
  119.6 0.2 hidden_kernel.1
  119.9 8.7 %all_to_all.39 = bf16[4,32,672]{2,1,0:T(8,128)(2,1)S(1)} all-to-all(bf16[4,32,672]{2,1,0:T(8,128)(2,1)S(1)} %broadcast_in_dim.15), channel_id=1, replica_groups=mesh['z'=8,'x'=4,'y'=4,'core'=2] {'y'}, dimensions={0} | all-to-all | bytes 344064 | tf_op jit(solution)/shard_map/all_to_all | solution.py:269
  128.6 0.0 collective-permute-start.2
  128.6 1.4 collective-permute-done.2.b_ref
  130.0 0.0 copy-done.3
  130.0 1.0 down_kernel.1
  131.0 20.2 %all_to_all.40.x_ref = bf16[32,8,672]{2,1,0:T(8,128)(2,1)S(1)} all-to-all(bf16[32,8,672]{2,1,0:T(8,128)(2,1)S(1)} %bitcast.9), channel_id=1, replica_groups=mesh['z'=8,'x'=4,'y'=4,'core'=2] {'z','x'}, dimensions={0} | all-to-all | bytes 688128 | tf_op jit(solution)/shard_map/all_to_all | solution.py:269
  151.2 0.7 final_kernel.1
  (14 shorter events, 0.2 us)
Async XLA Ops:
  6.5 51.3 %all-gather.2.cloned.1.call-start = ((), (), s32[]{:S(2)}) async-start(), calls=%async_computation.7 | async-start | bytes 2359296 | tf_op jit(solution)/shard_map/all_gather | solution.py:286
  8.4 1.6 %copy-start.4 = (bf16[2,2048,256]{2,1,0:T(8,128)(2,1)S(1)}, bf16[2,2048,256]{2,1,0:T(8,128)(2,1)}, u32[]{:S(2)}) copy-start(bf16[2,2048,256]{2,1,0:T(8,128)(2,1)} %k_hbm.1) | copy-start | bytes 6291460
  10.0 1.6 %copy-start.5 = (bf16[2,2048,256]{2,1,0:T(8,128)(2,1)S(1)}, bf16[2,2048,256]{2,1,0:T(8,128)(2,1)}, u32[]{:S(2)}) copy-start(bf16[2,2048,256]{2,1,0:T(8,128)(2,1)} %v_hbm.1) | copy-start | bytes 6291460
  11.6 0.9 copy-start.6
  12.5 0.7 copy-start.7
  13.2 0.7 copy-start.8
  15.0 50.0 %copy-start.10 = (f32[168]{0:T(256)S(1)}, f32[168]{0:T(256)}, u32[]{:S(2)}) copy-start(f32[168]{0:T(256)} %param.18) | copy-start | bytes 2020
  15.0 50.1 %copy-start.9 = (bf16[32,168]{1,0:T(8,128)(2,1)S(1)}, bf16[32,168]{1,0:T(8,128)(2,1)}, u32[]{:S(2)}) copy-start(bf16[32,168]{1,0:T(8,128)(2,1)} %param.16) | copy-start | bytes 32260
  57.8 1.6 %copy-start = (bf16[4096,168]{1,0:T(8,128)(2,1)S(1)}, bf16[4096,168]{1,0:T(8,128)(2,1)}, u32[]{:S(2)}) copy-start(bf16[4096,168]{1,0:T(8,128)(2,1)} %all-gather.2.cloned.1.call-done.w_ref) | copy-start | bytes 4128772
  59.4 45.1 %copy-start.1 = (bf16[672,672]{1,0:T(8,128)(2,1)S(1)}, bf16[672,672]{1,0:T(8,128)(2,1)}, u32[]{:S(2)}) copy-start(bf16[672,672]{1,0:T(8,128)(2,1)} %g_ref.1) | copy-start | bytes 2709508
  59.4 45.1 %copy-start.2 = (bf16[672,672]{1,0:T(8,128)(2,1)S(1)}, bf16[672,672]{1,0:T(8,128)(2,1)}, u32[]{:S(2)}) copy-start(bf16[672,672]{1,0:T(8,128)(2,1)} %u_ref.1) | copy-start | bytes 2709508
  60.5 10.6 %all-to-all-start.2 = ((bf16[8,32,168]{2,1,0:T(8,128)(2,1)}), bf16[8,32,168]{2,1,0:T(8,128)(2,1)S(1)}, u32[]{:S(2)}, u32[]{:S(2)}) async-start(bf16[8,32,168]{2,1,0:T(8,128)(2,1)} %project_kernel.1), calls=%async_computation.2 | async-start | bytes 262144 | tf_op jit(solution)/shard_map/all_to_all | solution.py:269
  65.1 5.2 %collective-permute-start = (bf16[40,168]{1,0:T(8,128)(2,1)S(1)}, bf16[40,168]{1,0:T(8,128)(2,1)S(1)}, u32[]{:S(2)}, u32[]{:S(2)}) collective-permute-start(bf16[40,168]{1,0:T(8,128)(2,1)S(1)} %concatenate.7), channel_id=1, source_target_pairs={{0,0},{1,32},{2,64},{3,96},{4,128},{5,160},{6,192},{7,224},{8,8},{... | collective-permute-start | bytes 40328 | tf_op jit(solution)/shard_map/ppermute | solution.py:292
  106.0 24.0 %copy-start.3 = (bf16[672,672]{1,0:T(8,128)(2,1)S(1)}, bf16[672,672]{1,0:T(8,128)(2,1)}, u32[]{:S(2)}) copy-start(bf16[672,672]{1,0:T(8,128)(2,1)} %w_ref.1) | copy-start | bytes 2709508
  106.0 1.8 %collective-permute-start.1 = (bf16[128,1536]{1,0:T(8,128)(2,1)S(1)}, bf16[128,1536]{1,0:T(8,128)(2,1)S(1)}, u32[]{:S(2)}, u32[]{:S(2)}) collective-permute-start(bf16[128,1536]{1,0:T(8,128)(2,1)S(1)} %get-tuple-element.9), channel_id=1, source_target_pairs={{0,1},{1,0},{2,3},{3,2},{4,5},{5,4},{6,7},{7,6},{8,9},{9,8},{10,11... | collective-permute-start | bytes 1179656 | tf_op jit(solution)/shard_map/ppermute | solution.py:317
  128.6 1.4 collective-permute-start.2
Sparse Core Ops, SparseCore 0:
  9.1 48.5 all-gather.1

commit v2 on v1

--- a/solution.py
+++ b/solution.py
@@ -25,7 +25,7 @@
 
 VMEM = pl.BlockSpec(memory_space=pltpu.VMEM)
 SMEM = pl.BlockSpec(memory_space=pltpu.SMEM)
-HBM = pl.BlockSpec(memory_space=pl.ANY)
+HBM = pl.BlockSpec(memory_space=pltpu.HBM)
 
 
 def pieces(value):
@@ -36,8 +36,23 @@
 
 
 def attend_kernel(
-    pm, sel, me, q_ref, k_hbm, v_hbm, o_ref, kbuf, vbuf, ksem, vsem, s_ref, m_ref, l_ref, acc_ref
+    pm_hbm, sel_hbm, ids, gain_hbm, q_hbm, k_hbm, v_hbm, o_ref,
+    pm, sel, gain_ref, q_ref, kbuf, vbuf, sems, ksem, vsem, s_ref, m_ref, l_ref, acc_ref,
 ):
+    tables = (
+        pltpu.make_async_copy(pm_hbm, pm, sems.at[0]),
+        pltpu.make_async_copy(sel_hbm, sel, sems.at[1]),
+    )
+    late = (
+        pltpu.make_async_copy(q_hbm, q_ref, sems.at[2]),
+        pltpu.make_async_copy(gain_hbm, gain_ref, sems.at[3]),
+    )
+    for c in tables:
+        c.start()
+    for c in late:
+        c.start()
+    for c in tables:
+        c.wait()
     chosen = [[jnp.int32(0), jnp.int32(0)], [jnp.int32(0), jnp.int32(0)]]
     causal = [jnp.int32(0), jnp.int32(0)]
     for t in range(2):
@@ -45,7 +60,7 @@
             logical = sel[t, j]
             slot = pm[logical]
             for p in range(2):
-                hit = (slot == me[0] * 2 + p).astype(jnp.int32)
+                hit = (slot == ids[0] * 2 + p).astype(jnp.int32)
                 chosen[p][t] = chosen[p][t] | hit
                 causal[p] = causal[p] | (hit * (logical == LAST_PAGE).astype(jnp.int32))
     used = [chosen[p][0] | chosen[p][1] for p in range(2)]
@@ -63,6 +78,8 @@
             for c in copies(p):
                 c.start()
 
+    for c in late:
+        c.wait()
     m_ref[...] = jnp.full_like(m_ref, NEG)
     l_ref[...] = jnp.zeros_like(l_ref)
     acc_ref[...] = jnp.zeros_like(acc_ref)
@@ -88,7 +105,7 @@
                 )
                 if j == 3:
                     s = jnp.where(visible, s, NEG)
-                s_ref[:, j * 512 : (j + 1) * 512] = s
+                s_ref[kv, :, j * 512 : (j + 1) * 512] = s
                 for a in range(4):
                     top = jnp.maximum(top, s[:, a * 128 : (a + 1) * 128])
             i = t * 2 + kv
@@ -99,7 +116,7 @@
             total = jnp.zeros((256, 128), F32)
             mixture = acc_ref[i] * alpha
             for j in range(4):
-                w = jnp.exp2((s_ref[:, j * 512 : (j + 1) * 512] - m_wide) * EXP2_SCALE)
+                w = jnp.exp2((s_ref[kv, :, j * 512 : (j + 1) * 512] - m_wide) * EXP2_SCALE)
                 for a in range(4):
                     total = total + w[:, a * 128 : (a + 1) * 128]
                 mixture = mixture + jnp.dot(
@@ -130,8 +147,16 @@
             lax.fori_loop(0, 2, tile, 0)
 
     lane = lax.broadcasted_iota(jnp.int32, (128, 128), 1)
+    halves = []
+    for piece in pieces(gain_ref[...]):
+        halves += [piece[:, :84], piece[:, 84:168]]
+    halves += [jnp.zeros((1, 84), F32)] * 2
+    gains = jnp.concatenate(
+        [jnp.zeros((8, 16), F32), jnp.concatenate(halves, axis=0), jnp.zeros((8, 28), F32)], axis=1
+    )
+    gains = jnp.concatenate([gains] * 16, axis=0)
     for t in range(2):
-        block = jnp.zeros((128, 128), F32)
+        block = gains
         for h in range(4):
             i, rows = t * 2 + h // 2, slice((h % 2) * 128, (h % 2 + 1) * 128)
             total = l_ref[i, rows, :]
@@ -146,18 +171,27 @@
         o_ref[t * 128 : (t + 1) * 128, 512:640] = block.astype(BF)
 
 
-def attend(page_map, selected, me, queries, keys, values):
+def in_hbm(array):
+    return pltpu.with_memory_space_constraint(array, pltpu.HBM)
+
+
+def attend(page_map, selected, ids, gain, queries, keys, values):
     return pl.pallas_call(
         attend_kernel,
         out_shape=jax.ShapeDtypeStruct((256, 640), BF),
-        in_specs=[SMEM, SMEM, SMEM, VMEM, HBM, HBM],
+        in_specs=[HBM, HBM, SMEM, HBM, HBM, HBM, HBM],
         out_specs=VMEM,
         scratch_shapes=[
+            pltpu.SMEM((64,), jnp.int32),
+            pltpu.SMEM((2, 8), jnp.int32),
+            pltpu.VMEM((1, 168), F32),
+            pltpu.VMEM((256, 512), BF),
             pltpu.VMEM((2, 2048, 256), BF),
             pltpu.VMEM((2, 2048, 256), BF),
+            pltpu.SemaphoreType.DMA((4,)),
             pltpu.SemaphoreType.DMA((2,)),
             pltpu.SemaphoreType.DMA((2,)),
-            pltpu.VMEM((256, 2048), F32),
+            pltpu.VMEM((2, 256, 2048), F32),
             pltpu.VMEM((4, 256, 128), F32),
             pltpu.VMEM((4, 256, 128), F32),
             pltpu.VMEM((4, 256, 128), F32),
@@ -167,10 +201,10 @@
             flops=4 * 10**9, transcendentals=4 * 10**6, bytes_accessed=10 * 2**20
         ),
         name="attend",
-    )(page_map, selected, me, queries, keys, values)
-
-
-def merge_kernel(x_ref, o_ref):
+    )(in_hbm(page_map), in_hbm(selected), ids, in_hbm(gain), in_hbm(queries), in_hbm(keys), in_hbm(values))
+
+
+def merge_kernel(ids, x_ref, o_ref, gain_ref):
     x = x_ref[...].astype(F32)
     marks = x[:, :, 512:640].reshape(256, 128).astype(BF)
     source = lax.broadcasted_iota(jnp.int32, (128, 512), 0)
@@ -181,26 +215,65 @@
     weight = jnp.exp2(level - top)
     total = jnp.sum(weight, axis=0)
     mixed = jnp.sum(weight * x[:, :, :512], axis=0)
-    o_ref[...] = (mixed / total).astype(BF)
-
-
-def project_kernel(a_ref, w_ref, o_ref):
+    share = (mixed / total).astype(BF)
+    for k in range(NX):
+        o_ref[k] = share
+        gain = x_ref[ids[2] * NX + k, :, 512:640].astype(F32)
+        for half in range(2):
+            gain_ref[k : k + 1, half * 84 : half * 84 + 84] = (
+                gain[half : half + 1, 16:100]
+                + gain[half + 2 : half + 3, 16:100]
+                + gain[half + 4 : half + 5, 16:100]
+            )
+
+
+def packed(rows):
+    rest = rows[:, 128:168]
+    return jnp.concatenate(
+        [
+            rows[:, :128],
+            jnp.concatenate([rest[:16], rest[16:], jnp.zeros((16, 48), rows.dtype)], axis=1),
+        ],
+        axis=0,
+    )
+
+
+def project_kernel(a_ref, w_hbm, o_ref, wbuf, sems):
+    copies = [
+        pltpu.make_async_copy(w_hbm.at[z], wbuf.at[z], sems.at[z]) for z in range(NZ)
+    ]
+    for c in copies:
+        c.start()
     a = a_ref[...]
     for z in range(NZ):
-        o_ref[z] = jnp.dot(
-            a, w_ref[z * 512 : (z + 1) * 512, :], preferred_element_type=F32
-        ).astype(BF)
-
-
-def gate_up_kernel(ids, x_ref, g_ref, u_ref, mine_ref, other_ref, own_ref, stream, normed):
+        copies[z].wait()
+        block = lax.dot_general(
+            a,
+            wbuf[z],
+            (((1,), (1,)), ((), ())),
+            preferred_element_type=F32,
+        )
+        o_ref[z] = packed(block).astype(BF)
+
+
+def stream_kernel(x_ref, r_ref, o_ref):
+    total = jnp.sum(x_ref[...].astype(F32), axis=0) + packed(r_ref[...].astype(F32))
+    stream = total.astype(BF)
+    for k in range(NZ * NX):
+        o_ref[k] = stream
+
+
+def gate_up_kernel(ids, x_ref, gain_ref, g_ref, u_ref, mine_ref, other_ref, own_ref, stream, normed):
     for x in range(NX):
-        lanes = slice(x * 168, (x + 1) * 168)
         block = x_ref[:, x, :, :].astype(F32)
-        part = block[:, :32, :].reshape(256, 168)
-        tail = block[0, 32:40, :]
-        gain = tail[0:1] + tail[1:2] + tail[2:3]
-        stream[:, lanes] = part
-        normed[:, lanes] = (part * gain).astype(BF)
+        main = block[:, :32, :].reshape(256, 128)
+        rest = jnp.concatenate([block[:, 32:48, 0:40], block[:, 32:48, 40:80]], axis=1)
+        rest = rest.reshape(256, 40)
+        first, second = slice(x * 168, x * 168 + 128), slice(x * 168 + 128, x * 168 + 168)
+        stream[:, first] = main
+        stream[:, second] = rest
+        normed[:, first] = (main * gain_ref[x : x + 1, 0:128]).astype(BF)
+        normed[:, second] = (rest * gain_ref[x : x + 1, 128:168]).astype(BF)
     own_ref[...] = stream[pl.ds(pl.multiple_of(ids[0] * 8, 8), 8), :].astype(BF)
     core = ids[1]
     lane = lax.broadcasted_iota(jnp.int32, (128, GU_HALF - 672), 1)
@@ -237,7 +310,9 @@
     factor = lax.rsqrt(squares / D + EPSILON)
     gate = both[:, 0:672] * factor
     up = both[:, GU_HALF : GU_HALF + 672] * factor
-    o_ref[...] = (jax.nn.gelu(gate, approximate=True) * up).astype(BF)
+    hidden = (jax.nn.gelu(gate, approximate=True) * up).astype(BF)
+    for k in range(NY):
+        o_ref[k] = hidden
 
 
 def down_kernel(ids, a_ref, b_ref, w_ref, o_ref):
@@ -251,26 +326,22 @@
     o_ref[...] = (jnp.sum(x_ref[...].astype(F32), axis=0) + s_ref[...].astype(F32)).astype(BF)
 
 
-def call(kernel, shapes, specs, *args, scratch=()):
-    many = isinstance(shapes, list)
-    outs = [jax.ShapeDtypeStruct(s, BF) for s in (shapes if many else [shapes])]
-    return pl.pallas_call(
+def call(kernel, outs, specs, *args, scratch=()):
+    outs = [jax.ShapeDtypeStruct(shape, dtype) for shape, dtype in outs]
+    results = pl.pallas_call(
         kernel,
-        out_shape=outs if many else outs[0],
+        out_shape=outs,
         in_specs=specs,
-        out_specs=[VMEM] * len(outs) if many else VMEM,
+        out_specs=[VMEM] * len(outs),
         scratch_shapes=scratch,
         compiler_params=pltpu.CompilerParams(vmem_limit_bytes=32 << 20),
         name=kernel.__name__,
     )(*args)
+    return results if len(outs) > 1 else results[0]
 
 
 def exchange(parts, axis):
     return lax.all_to_all(parts, axis, split_axis=0, concat_axis=0, tiled=True)
-
-
-def to_all(part, axis):
-    return exchange(jnp.broadcast_to(part, (lax.axis_size(axis), *part.shape)), axis)
 
 
 def place(z, x, h):
@@ -282,48 +353,61 @@
 ):
     ctx = (lax.axis_index("z") * NX + lax.axis_index("x")).astype(jnp.int32)
     core = lax.axis_index("core").astype(jnp.int32)
-    ids = jnp.stack([ctx, core])
-    wide_weight = lax.all_gather(out_weight, "z", axis=0, tiled=True)
-    gain_high = lax.reduce_precision(norm_gain, 8, 7)
-    gain_rest = norm_gain - gain_high
-    gain_middle = lax.reduce_precision(gain_rest, 8, 7)
-    gain_rows = jnp.stack([gain_high, gain_middle, gain_rest - gain_middle]).astype(BF)
-    carried = jnp.concatenate([residual_in, gain_rows, jnp.zeros((5, 168), BF)], axis=0)
-    turned = lax.ppermute(
-        carried,
+    head = lax.axis_index("y").astype(jnp.int32) * NC + core
+    ids = jnp.stack([ctx, core, head])
+    wide_weight = lax.all_gather(out_weight.T[None], "z", axis=0, tiled=True)
+    residual = lax.ppermute(
+        residual_in,
         ALL,
         [(place(z, x, h), place(h, x, z)) for z in range(NZ) for x in range(NX) for h in range(NZ)],
     )
-
-    sent = attend(page_map, selected, ids, queries, keys, values)
+    sent = attend(page_map, selected, ids, norm_gain.reshape(1, 168), queries, keys, values)
+    sent, residual = lax.optimization_barrier((sent, residual))
     arrived = exchange(sent.reshape(32, 8, 640), CTX)
-    share = call(merge_kernel, (8, 512), [VMEM], arrived)
-    attention = to_all(share, "x").reshape(32, 512)
-    partial = call(project_kernel, (NZ, 32, 168), [VMEM, VMEM], attention, wide_weight)
-    projected = exchange(partial, HEADS).astype(F32).sum(axis=0)
-    stream = (turned[:32].astype(F32) + projected).astype(BF)
-    rows = to_all(jnp.concatenate([stream, turned[32:]], axis=0), CTX)
+    shares, gain = call(
+        merge_kernel, [((NX, 8, 512), BF), ((NX, 168), F32)], [SMEM, VMEM], ids, arrived
+    )
+    attention = exchange(shares, "x").reshape(32, 512)
+    partial = call(
+        project_kernel,
+        [((NZ, 48, 128), BF)],
+        [VMEM, HBM],
+        attention,
+        in_hbm(wide_weight),
+        scratch=[pltpu.VMEM((NZ, 168, 512), BF), pltpu.SemaphoreType.DMA((NZ,))],
+    )
+    projected = exchange(partial, HEADS)
+    streams = call(stream_kernel, [((NZ * NX, 48, 128), BF)], [VMEM, VMEM], projected, residual)
+    rows = exchange(streams, CTX)
+    half = ((128, 2 * GU_HALF), BF)
     mine, other, own_stream = call(
         gate_up_kernel,
-        [(128, 2 * GU_HALF), (128, 2 * GU_HALF), (8, 672)],
-        [SMEM, VMEM, VMEM, VMEM],
+        [half, half, ((8, 672), BF)],
+        [SMEM, VMEM, VMEM, VMEM, VMEM],
         ids,
-        rows.reshape(NZ, NX, 40, 168),
+        rows.reshape(NZ, NX, 48, 128),
+        gain,
         gate_weight,
         up_weight,
         scratch=[pltpu.VMEM((256, 672), F32), pltpu.VMEM((256, 672), BF)],
     )
     swap = [(0, 1), (1, 0)]
-    pair = call(pair_kernel, (128, 2 * GU_HALF), [VMEM, VMEM], mine, lax.ppermute(other, "core", swap))
+    pair = call(pair_kernel, [half], [VMEM, VMEM], mine, lax.ppermute(other, "core", swap))
     quarters = exchange(pair.reshape(NY, 32, 2 * GU_HALF), "y")
-    hidden = call(hidden_kernel, (32, 672), [VMEM], quarters)
-    hidden_half = to_all(hidden, "y").reshape(128, 672)
+    hidden = call(hidden_kernel, [((NY, 32, 672), BF)], [VMEM], quarters)
+    hidden_half = exchange(hidden, "y").reshape(128, 672)
     hidden_other = lax.ppermute(hidden_half, "core", swap)
     down = call(
-        down_kernel, (256, 672), [SMEM, VMEM, VMEM, VMEM], ids, hidden_half, hidden_other, down_weight
+        down_kernel,
+        [((256, 672), BF)],
+        [SMEM, VMEM, VMEM, VMEM],
+        ids,
+        hidden_half,
+        hidden_other,
+        down_weight,
     )
     out_parts = exchange(down.reshape(32, 8, 672), CTX)
-    return call(final_kernel, (8, 672), [VMEM, VMEM], out_parts, own_stream)
+    return call(final_kernel, [((8, 672), BF)], [VMEM, VMEM], out_parts, own_stream)
 
 
 def solution(mesh):

time: 159 us -> 145 us (0.912)
  local copies, waits for them, and re-layouts: 8.96 us -> 0.02 us
  Pallas kernels: 6.35 us -> 13.4 us
  starting transfers between devices: 8.28 us -> 2.02 us
  waiting for transfers between devices: 8.94 us -> 3.86 us
  blocking collectives: 113 us -> 111 us
    unnamed x23 -> x6, local copies, waits for them, and re-layouts: 8.85 us -> 0.02 us
    all_to_all x1 -> x0, starting transfers between devices: 4.47 us -> none  [exchange(): return lax.all_to_all(parts, axis, split_axis=0, concat_axis=0, tiled=True)]
    pallas_call x1, Pallas kernels: 1.1 us -> 5.29 us  [attend(): pl.pallas_call(attend_kernel, out_shape=jax.ShapeDtypeStruct((256, 640),...]
    all_gather x1, waiting for transfers between devices: 3.47 us -> 0.01 us  [shards(): wide_weight = lax.all_gather(out_weight.T[None], 'z', axis=0, tiled=True)]
    pallas_call x7 -> x8, Pallas kernels: 5.25 us -> 8.14 us  [call(): pl.pallas_call(kernel, out_shape=outs, in_specs=specs, out_specs=[VMEM] *...]
    ppermute x1, starting transfers between devices: 3.72 us -> 1.92 us  [shards(): lax.ppermute(residual_in, ALL, [(place(z, x, h), place(h, x, z)) for z in...]
    all_to_all x6 -> x7, blocking collectives: 113 us -> 111 us  [exchange(): return lax.all_to_all(parts, axis, split_axis=0, concat_axis=0, tiled=True)]
  transfers between devices with their start and end apart: 5 -> 4, of which waited for: 5 -> 2; matrix products, arithmetic and copies ran while one was open for 0% -> 0% of each run, Pallas kernels for 1% -> 4%
where the time goes in v2:
time: 145 us; the launch traced here: 144 us
  blocking collectives  111 us (77%)
  between operations  13.5 us (9%)
  Pallas kernels  13.4 us (9%)
  waiting for transfers between devices  3.86 us (3%)
  starting transfers between devices  2.02 us (1%)
    all_to_all x7, blocking collectives, exchange(): return lax.all_to_all(parts, axis, split_axis=0, concat_axis=0, tiled=True)  111 us
    pallas_call x8, Pallas kernels, call(): pl.pallas_call(kernel, out_shape=outs, in_specs=specs, out_specs=[VMEM] *...  8.14 us
    pallas_call x1, Pallas kernels, attend(): pl.pallas_call(attend_kernel, out_shape=jax.ShapeDtypeStruct((256, 640),...  5.29 us
  transfers between devices with their start and end apart: 4, of which 2 were waited for; matrix products, arithmetic and copies ran while one was open for 0% of the time, Pallas kernels for 4%

profile of v2, /device:TPU:32, one launch (start us, length us, event | category | flops | bytes accessed | tf_op | source)
XLA Modules:
  0.0 144.1 jit_solution(1303958910814742401)
XLA Ops:
  6.5 0.0 all-gather.3.cloned.1.call-start
  6.5 0.7 all-gather.3.cloned.1.call-update
  7.3 1.9 %collective-permute-start = (bf16[32,168]{1,0:T(8,128)(2,1)}, bf16[32,168]{1,0:T(8,128)(2,1)S(1)}, u32[]{:S(2)}, u32[]{:S(2)}) collective-permute-start(bf16[32,168]{1,0:T(8,128)(2,1)} %param.16), channel_id=1, source_target_pairs={{0,0},{1,32},{2,64},{3,96},{4,128},{5,160},{6,192},{7,224},{8,8},{... | collective-permute-start | bytes 32264 | tf_op jit(solution)/shard_map/ppermute | solution.py:359
  9.2 0.1 pad_add_fusion.ids
  9.3 5.3 %attend.1 = bf16[256,640]{1,0:T(8,128)(2,1)S(1)} custom-call(s32[64]{0:T(128)} %pm_hbm.1, s32[2,8]{1,0:T(2,128)} %sel_hbm.1, s32[3]{0:T(128)S(1)} %pad_add_fusion.ids, f32[1,168]{1,0:T(1,128)} %bitcast.21, bf16[256,512]{1,0:T(8,128)(2,1)} %q_hbm.1, bf16[2,2048,256]{2,1,0:T(8,128)(2,1)} %k_hbm.1, bf16[2,2048,256]{2,1,0:T(8,128)(2,1)} %v_hbm.1), custom_call_target="tpu_custom_call" | custom-call | flops 4000000000 | bytes 10485760 | tf_op jit(solution)/shard_map/attend/pallas_call | solution.py:179
  14.6 0.0 copy-start
  14.6 0.0 copy-start.1
  14.6 0.0 collective-permute-done.r_ref
  14.6 32.4 %all_to_all.35.x_ref = bf16[32,8,640]{2,1,0:T(8,128)(2,1)S(1)} all-to-all(bf16[32,8,640]{2,1,0:T(8,128)(2,1)S(1)} %bitcast.17), channel_id=1, replica_groups=mesh['z'=8,'x'=4,'y'=4,'core'=2] {'z','x'}, dimensions={0} | all-to-all | bytes 655360 | tf_op jit(solution)/shard_map/all_to_all | solution.py:344
  47.0 0.9 merge_kernel.1
  47.9 8.1 %all_to_all.36 = bf16[4,8,512]{2,1,0:T(8,128)(2,1)S(1)} all-to-all(bf16[4,8,512]{2,1,0:T(8,128)(2,1)S(1)} %get-tuple-element.13), channel_id=1, replica_groups=mesh['z'=8,'x'=4,'y'=4,'core'=2] {'x'}, dimensions={0} | all-to-all | bytes 65536 | tf_op jit(solution)/shard_map/all_to_all | solution.py:344
  56.0 0.0 all-gather.3.cloned.1.call-done
  56.0 3.3 %project_kernel.1 = bf16[8,48,128]{2,1,0:T(8,128)(2,1)S(1)} custom-call(bf16[32,512]{1,0:T(8,128)(2,1)S(1)} %bitcast.18, bf16[8,168,512]{2,1,0:T(8,128)(2,1)} %bitcast.19), custom_call_target="tpu_custom_call" | custom-call | tf_op jit(solution)/shard_map/project_kernel/pallas_call | solution.py:331
  59.3 9.2 %all_to_all.37.x_ref = bf16[8,48,128]{2,1,0:T(8,128)(2,1)S(1)} all-to-all(bf16[8,48,128]{2,1,0:T(8,128)(2,1)S(1)} %project_kernel.1), channel_id=1, replica_groups=mesh['z'=8,'x'=4,'y'=4,'core'=2] {'y','core'}, dimensions={0} | all-to-all | bytes 196608 | tf_op jit(solution)/shard_map/all_to_all | solution.py:344
  68.5 0.1 stream_kernel.1
  68.6 22.1 %all_to_all.38 = bf16[32,48,128]{2,1,0:T(8,128)(2,1)S(1)} all-to-all(bf16[32,48,128]{2,1,0:T(8,128)(2,1)S(1)} %stream_kernel.1), channel_id=1, replica_groups=mesh['z'=8,'x'=4,'y'=4,'core'=2] {'z','x'}, dimensions={0} | all-to-all | bytes 786432 | tf_op jit(solution)/shard_map/all_to_all | solution.py:344
  90.7 0.0 copy-done
  90.7 0.0 copy-done.1
  90.7 0.0 copy-start.2
  90.7 1.6 %gate_up_kernel.1 = (bf16[128,1536]{1,0:T(8,128)(2,1)S(1)}, bf16[128,1536]{1,0:T(8,128)(2,1)S(1)}, bf16[8,672]{1,0:T(8,128)(2,1)S(1)}) custom-call(s32[3]{0:T(128)S(1)} %pad_add_fusion.ids, bf16[8,4,48,128]{3,2,1,0:T(8,128)(2,1)S(1)} %bitcast.14, f32[4,168]{1,0:T(4,128)S(1)} %get-tuple-element.15.gain_ref, bf16[672,672]{1,0:T(8,128)(2,1)S(1)} %copy-done, ...), custom_call_target="tpu_custom_call" | custom-call | tf_op jit(solution)/shard_map/gate_up_kernel/pallas_call | solution.py:331
  92.3 0.1 collective-permute-start.1
  92.4 1.7 %collective-permute-done.1.b_ref = bf16[128,1536]{1,0:T(8,128)(2,1)S(1)} collective-permute-done((bf16[128,1536]{1,0:T(8,128)(2,1)S(1)}, bf16[128,1536]{1,0:T(8,128)(2,1)S(1)}, u32[]{:S(2)}, u32[]{:S(2)}) %collective-permute-start.1) | collective-permute-done | bytes 393248 | tf_op jit(solution)/shard_map/ppermute | solution.py:395
  94.1 0.4 pair_kernel.1
  94.5 11.0 %all_to_all.39.x_ref = bf16[4,32,1536]{2,1,0:T(8,128)(2,1)S(1)} all-to-all(bf16[4,32,1536]{2,1,0:T(8,128)(2,1)S(1)} %bitcast.13), channel_id=1, replica_groups=mesh['z'=8,'x'=4,'y'=4,'core'=2] {'y'}, dimensions={0} | all-to-all | bytes 786432 | tf_op jit(solution)/shard_map/all_to_all | solution.py:344
  105.6 0.2 hidden_kernel.1
  105.8 8.7 %all_to_all.40 = bf16[4,32,672]{2,1,0:T(8,128)(2,1)S(1)} all-to-all(bf16[4,32,672]{2,1,0:T(8,128)(2,1)S(1)} %hidden_kernel.1), channel_id=1, replica_groups=mesh['z'=8,'x'=4,'y'=4,'core'=2] {'y'}, dimensions={0} | all-to-all | bytes 344064 | tf_op jit(solution)/shard_map/all_to_all | solution.py:344
  114.5 0.0 collective-permute-start.2
  114.5 1.4 collective-permute-done.2.b_ref
  115.9 0.0 copy-done.2
  115.9 1.0 down_kernel.1
  117.0 19.7 %all_to_all.41.x_ref = bf16[32,8,672]{2,1,0:T(8,128)(2,1)S(1)} all-to-all(bf16[32,8,672]{2,1,0:T(8,128)(2,1)S(1)} %bitcast.12), channel_id=1, replica_groups=mesh['z'=8,'x'=4,'y'=4,'core'=2] {'z','x'}, dimensions={0} | all-to-all | bytes 688128 | tf_op jit(solution)/shard_map/all_to_all | solution.py:344
  136.6 0.7 final_kernel.1
Async XLA Ops:
  6.5 49.5 %all-gather.3.cloned.1.call-start = ((), (), s32[]{:S(2)}) async-start(), calls=%async_computation.7 | async-start | bytes 1548288 | tf_op jit(solution)/shard_map/all_gather | solution.py:358
  7.3 7.3 %collective-permute-start = (bf16[32,168]{1,0:T(8,128)(2,1)}, bf16[32,168]{1,0:T(8,128)(2,1)S(1)}, u32[]{:S(2)}, u32[]{:S(2)}) collective-permute-start(bf16[32,168]{1,0:T(8,128)(2,1)} %param.16), channel_id=1, source_target_pairs={{0,0},{1,32},{2,64},{3,96},{4,128},{5,160},{6,192},{7,224},{8,8},{... | collective-permute-start | bytes 32264 | tf_op jit(solution)/shard_map/ppermute | solution.py:359
  14.6 76.1 %copy-start = (bf16[672,672]{1,0:T(8,128)(2,1)S(1)}, bf16[672,672]{1,0:T(8,128)(2,1)}, u32[]{:S(2)}) copy-start(bf16[672,672]{1,0:T(8,128)(2,1)} %g_ref.1) | copy-start | bytes 2709508
  14.6 76.1 %copy-start.1 = (bf16[672,672]{1,0:T(8,128)(2,1)S(1)}, bf16[672,672]{1,0:T(8,128)(2,1)}, u32[]{:S(2)}) copy-start(bf16[672,672]{1,0:T(8,128)(2,1)} %u_ref.1) | copy-start | bytes 2709508
  90.7 25.2 %copy-start.2 = (bf16[672,672]{1,0:T(8,128)(2,1)S(1)}, bf16[672,672]{1,0:T(8,128)(2,1)}, u32[]{:S(2)}) copy-start(bf16[672,672]{1,0:T(8,128)(2,1)} %w_ref.1) | copy-start | bytes 2709508
  92.3 1.8 %collective-permute-start.1 = (bf16[128,1536]{1,0:T(8,128)(2,1)S(1)}, bf16[128,1536]{1,0:T(8,128)(2,1)S(1)}, u32[]{:S(2)}, u32[]{:S(2)}) collective-permute-start(bf16[128,1536]{1,0:T(8,128)(2,1)S(1)} %get-tuple-element.17), channel_id=1, source_target_pairs={{0,1},{1,0},{2,3},{3,2},{4,5},{5,4},{6,7},{7,6},{8,9},{9,8},{10,11... | collective-permute-start | bytes 1179656 | tf_op jit(solution)/shard_map/ppermute | solution.py:395
  114.5 1.4 %collective-permute-start.2 = (bf16[128,672]{1,0:T(8,128)(2,1)S(1)}, bf16[128,672]{1,0:T(8,128)(2,1)S(1)}, u32[]{:S(2)}, u32[]{:S(2)}) collective-permute-start(bf16[128,672]{1,0:T(8,128)(2,1)S(1)} %bitcast.15), channel_id=1, source_target_pairs={{0,1},{1,0},{2,3},{3,2},{4,5},{5,4},{6,7},{7,6},{8,9},{9,8},{10,11... | collective-permute-start | bytes 516104 | tf_op jit(solution)/shard_map/ppermute | solution.py:399
Sparse Core Ops, SparseCore 0:
  9.1 45.1 all-gather.2

commit v3 on v2

--- a/solution.py
+++ b/solution.py
@@ -216,8 +216,9 @@
     total = jnp.sum(weight, axis=0)
     mixed = jnp.sum(weight * x[:, :, :512], axis=0)
     share = (mixed / total).astype(BF)
+    for k in range(NZ * NX):
+        o_ref[k] = share
     for k in range(NX):
-        o_ref[k] = share
         gain = x_ref[ids[2] * NX + k, :, 512:640].astype(F32)
         for half in range(2):
             gain_ref[k : k + 1, half * 84 : half * 84 + 84] = (
@@ -238,29 +239,17 @@
     )
 
 
-def project_kernel(a_ref, w_hbm, o_ref, wbuf, sems):
-    copies = [
-        pltpu.make_async_copy(w_hbm.at[z], wbuf.at[z], sems.at[z]) for z in range(NZ)
-    ]
-    for c in copies:
-        c.start()
-    a = a_ref[...]
-    for z in range(NZ):
-        copies[z].wait()
-        block = lax.dot_general(
-            a,
-            wbuf[z],
-            (((1,), (1,)), ((), ())),
-            preferred_element_type=F32,
-        )
-        o_ref[z] = packed(block).astype(BF)
+def project_kernel(a_ref, w_ref, o_ref):
+    block = lax.dot_general(
+        a_ref[...], w_ref[...], (((1,), (1,)), ((), ())), preferred_element_type=F32
+    )
+    for h in range(NZ):
+        o_ref[h] = packed(block[h * 32 : (h + 1) * 32]).astype(BF)
 
 
 def stream_kernel(x_ref, r_ref, o_ref):
     total = jnp.sum(x_ref[...].astype(F32), axis=0) + packed(r_ref[...].astype(F32))
-    stream = total.astype(BF)
-    for k in range(NZ * NX):
-        o_ref[k] = stream
+    o_ref[...] = total.astype(BF)
 
 
 def gate_up_kernel(ids, x_ref, gain_ref, g_ref, u_ref, mine_ref, other_ref, own_ref, stream, normed):
@@ -355,30 +344,21 @@
     core = lax.axis_index("core").astype(jnp.int32)
     head = lax.axis_index("y").astype(jnp.int32) * NC + core
     ids = jnp.stack([ctx, core, head])
-    wide_weight = lax.all_gather(out_weight.T[None], "z", axis=0, tiled=True)
-    residual = lax.ppermute(
-        residual_in,
+    sent = attend(page_map, selected, ids, norm_gain.reshape(1, 168), queries, keys, values)
+    arrived = exchange(sent.reshape(32, 8, 640), CTX)
+    shares, gain = call(
+        merge_kernel, [((NZ * NX, 8, 512), BF), ((NX, 168), F32)], [SMEM, VMEM], ids, arrived
+    )
+    attention = exchange(shares, CTX).reshape(256, 512)
+    partial = call(project_kernel, [((NZ, 48, 128), BF)], [VMEM, VMEM], attention, out_weight.T)
+    projected = exchange(partial, HEADS)
+    stream = call(stream_kernel, [((48, 128), BF)], [VMEM, VMEM], projected, residual_in)
+    turned = lax.ppermute(
+        stream,
         ALL,
         [(place(z, x, h), place(h, x, z)) for z in range(NZ) for x in range(NX) for h in range(NZ)],
     )
-    sent = attend(page_map, selected, ids, norm_gain.reshape(1, 168), queries, keys, values)
-    sent, residual = lax.optimization_barrier((sent, residual))
-    arrived = exchange(sent.reshape(32, 8, 640), CTX)
-    shares, gain = call(
-        merge_kernel, [((NX, 8, 512), BF), ((NX, 168), F32)], [SMEM, VMEM], ids, arrived
-    )
-    attention = exchange(shares, "x").reshape(32, 512)
-    partial = call(
-        project_kernel,
-        [((NZ, 48, 128), BF)],
-        [VMEM, HBM],
-        attention,
-        in_hbm(wide_weight),
-        scratch=[pltpu.VMEM((NZ, 168, 512), BF), pltpu.SemaphoreType.DMA((NZ,))],
-    )
-    projected = exchange(partial, HEADS)
-    streams = call(stream_kernel, [((NZ * NX, 48, 128), BF)], [VMEM, VMEM], projected, residual)
-    rows = exchange(streams, CTX)
+    rows = exchange(jnp.broadcast_to(turned, (NZ * NX, 48, 128)), CTX)
     half = ((128, 2 * GU_HALF), BF)
     mine, other, own_stream = call(
         gate_up_kernel,

time: 145 us -> 133 us (0.917)
  between operations: 13.5 us -> 0.09 us
  waiting for transfers between devices: 3.86 us -> 5.81 us
    pallas_call x8, Pallas kernels: 8.14 us -> 5.24 us  [call(): pl.pallas_call(kernel, out_shape=outs, in_specs=specs, out_specs=[VMEM] *...]
    ppermute x1, waiting for transfers between devices: 0.01 us -> 2.66 us  [shards(): lax.ppermute(stream, ALL, [(place(z, x, h), place(h, x, z)) for z in rang...]
    pallas_call x1, Pallas kernels: 5.29 us -> 7.18 us  [attend(): pl.pallas_call(attend_kernel, out_shape=jax.ShapeDtypeStruct((256, 640),...]
  transfers between devices with their start and end apart: 4 -> 3, of which waited for: 2 -> 3; matrix products, arithmetic and copies ran while one was open for 0% -> 0% of each run, Pallas kernels for 4% -> 0%
where the time goes in v3:
time: 133 us; the launch traced here: 132 us
  blocking collectives  111 us (83%)
  Pallas kernels  12.4 us (9%)
  waiting for transfers between devices  5.81 us (4%)
  starting transfers between devices  2.43 us (2%)
    all_to_all x7, blocking collectives, exchange(): return lax.all_to_all(parts, axis, split_axis=0, concat_axis=0, tiled=True)  111 us
    pallas_call x1, Pallas kernels, attend(): pl.pallas_call(attend_kernel, out_shape=jax.ShapeDtypeStruct((256, 640),...  7.18 us
    pallas_call x8, Pallas kernels, call(): pl.pallas_call(kernel, out_shape=outs, in_specs=specs, out_specs=[VMEM] *...  5.24 us
  transfers between devices with their start and end apart: 3, of which 3 were waited for; matrix products, arithmetic and copies ran while one was open for 0% of the time, Pallas kernels for 0%

profile of v3, /device:TPU:32, one launch (start us, length us, event | category | flops | bytes accessed | tf_op | source)
XLA Modules:
  0.0 132.1 jit_solution(9276159087211732740)
XLA Ops:
  0.0 0.1 pad_add_fusion.ids
  0.1 0.0 copy-start.3
  0.1 7.2 %attend.1 = bf16[256,640]{1,0:T(8,128)(2,1)S(1)} custom-call(s32[64]{0:T(128)} %pm_hbm.1, s32[2,8]{1,0:T(2,128)} %sel_hbm.1, s32[3]{0:T(128)S(1)} %pad_add_fusion.ids, f32[1,168]{1,0:T(1,128)} %bitcast.19, bf16[256,512]{1,0:T(8,128)(2,1)} %q_hbm.1, bf16[2,2048,256]{2,1,0:T(8,128)(2,1)} %k_hbm.1, bf16[2,2048,256]{2,1,0:T(8,128)(2,1)} %v_hbm.1), custom_call_target="tpu_custom_call" | custom-call | flops 4000000000 | bytes 10485760 | tf_op jit(solution)/shard_map/attend/pallas_call | solution.py:179
  7.3 0.0 copy-start.4
  7.3 0.0 copy-start
  7.3 0.0 copy-start.1
  7.3 21.1 %all_to_all.35.x_ref = bf16[32,8,640]{2,1,0:T(8,128)(2,1)S(1)} all-to-all(bf16[32,8,640]{2,1,0:T(8,128)(2,1)S(1)} %bitcast.17), channel_id=1, replica_groups=mesh['z'=8,'x'=4,'y'=4,'core'=2] {'z','x'}, dimensions={0} | all-to-all | bytes 655360 | tf_op jit(solution)/shard_map/all_to_all | solution.py:333
  28.4 0.9 merge_kernel.1
  29.3 16.0 %all_to_all.36 = bf16[32,8,512]{2,1,0:T(8,128)(2,1)S(1)} all-to-all(bf16[32,8,512]{2,1,0:T(8,128)(2,1)S(1)} %get-tuple-element.10), channel_id=1, replica_groups=mesh['z'=8,'x'=4,'y'=4,'core'=2] {'z','x'}, dimensions={0} | all-to-all | bytes 524288 | tf_op jit(solution)/shard_map/all_to_all | solution.py:333
  45.3 0.0 copy-done.3
  45.3 0.3 project_kernel.1
  45.6 10.1 %all_to_all.37.x_ref = bf16[8,48,128]{2,1,0:T(8,128)(2,1)S(1)} all-to-all(bf16[8,48,128]{2,1,0:T(8,128)(2,1)S(1)} %project_kernel.1), channel_id=1, replica_groups=mesh['z'=8,'x'=4,'y'=4,'core'=2] {'y','core'}, dimensions={0} | all-to-all | bytes 196608 | tf_op jit(solution)/shard_map/all_to_all | solution.py:333
  55.7 0.0 copy-done.4
  55.7 0.1 stream_kernel.1
  55.8 2.3 %collective-permute-start = (bf16[48,128]{1,0:T(8,128)(2,1)S(1)}, bf16[48,128]{1,0:T(8,128)(2,1)S(1)}, u32[]{:S(2)}, u32[]{:S(2)}) collective-permute-start(bf16[48,128]{1,0:T(8,128)(2,1)S(1)} %stream_kernel.1), channel_id=1, source_target_pairs={{0,0},{1,32},{2,64},{3,96},{4,128},{5,160},{6,192},{7,224},{8,8},{... | collective-permute-start | bytes 36872 | tf_op jit(solution)/shard_map/ppermute | solution.py:356
  58.1 2.7 %collective-permute-done = bf16[48,128]{1,0:T(8,128)(2,1)S(1)} collective-permute-done((bf16[48,128]{1,0:T(8,128)(2,1)S(1)}, bf16[48,128]{1,0:T(8,128)(2,1)S(1)}, u32[]{:S(2)}, u32[]{:S(2)}) %collective-permute-start) | collective-permute-done | bytes 12320 | tf_op jit(solution)/shard_map/ppermute | solution.py:356
  60.8 0.1 broadcast_in_dim.3
  60.8 24.6 %all_to_all.38 = bf16[32,48,128]{2,1,0:T(8,128)(2,1)S(1)} all-to-all(bf16[32,48,128]{2,1,0:T(8,128)(2,1)S(1)} %broadcast_in_dim.3), channel_id=1, replica_groups=mesh['z'=8,'x'=4,'y'=4,'core'=2] {'z','x'}, dimensions={0} | all-to-all | bytes 786432 | tf_op jit(solution)/shard_map/all_to_all | solution.py:333
  85.4 0.0 copy-done
  85.4 0.0 copy-done.1
  85.4 0.0 copy-start.2
  85.4 1.7 %gate_up_kernel.1 = (bf16[128,1536]{1,0:T(8,128)(2,1)S(1)}, bf16[128,1536]{1,0:T(8,128)(2,1)S(1)}, bf16[8,672]{1,0:T(8,128)(2,1)S(1)}) custom-call(s32[3]{0:T(128)S(1)} %pad_add_fusion.ids, bf16[8,4,48,128]{3,2,1,0:T(8,128)(2,1)S(1)} %bitcast.13, f32[4,168]{1,0:T(4,128)S(1)} %get-tuple-element.11.gain_ref, bf16[672,672]{1,0:T(8,128)(2,1)S(1)} %copy-done, ...), custom_call_target="tpu_custom_call" | custom-call | tf_op jit(solution)/shard_map/gate_up_kernel/pallas_call | solution.py:320
  87.1 0.1 collective-permute-start.1
  87.2 1.7 %collective-permute-done.1.b_ref = bf16[128,1536]{1,0:T(8,128)(2,1)S(1)} collective-permute-done((bf16[128,1536]{1,0:T(8,128)(2,1)S(1)}, bf16[128,1536]{1,0:T(8,128)(2,1)S(1)}, u32[]{:S(2)}, u32[]{:S(2)}) %collective-permute-start.1) | collective-permute-done | bytes 393248 | tf_op jit(solution)/shard_map/ppermute | solution.py:375
  88.9 0.4 pair_kernel.1
  89.3 11.0 %all_to_all.39.x_ref = bf16[4,32,1536]{2,1,0:T(8,128)(2,1)S(1)} all-to-all(bf16[4,32,1536]{2,1,0:T(8,128)(2,1)S(1)} %bitcast.12), channel_id=1, replica_groups=mesh['z'=8,'x'=4,'y'=4,'core'=2] {'y'}, dimensions={0} | all-to-all | bytes 786432 | tf_op jit(solution)/shard_map/all_to_all | solution.py:333
  100.4 0.2 hidden_kernel.1
  100.6 8.7 %all_to_all.40 = bf16[4,32,672]{2,1,0:T(8,128)(2,1)S(1)} all-to-all(bf16[4,32,672]{2,1,0:T(8,128)(2,1)S(1)} %hidden_kernel.1), channel_id=1, replica_groups=mesh['z'=8,'x'=4,'y'=4,'core'=2] {'y'}, dimensions={0} | all-to-all | bytes 344064 | tf_op jit(solution)/shard_map/all_to_all | solution.py:333
  109.3 0.0 collective-permute-start.2
  109.3 1.4 %collective-permute-done.2.b_ref = bf16[128,672]{1,0:T(8,128)(2,1)S(1)} collective-permute-done((bf16[128,672]{1,0:T(8,128)(2,1)S(1)}, bf16[128,672]{1,0:T(8,128)(2,1)S(1)}, u32[]{:S(2)}, u32[]{:S(2)}) %collective-permute-start.2) | collective-permute-done | bytes 172064 | tf_op jit(solution)/shard_map/ppermute | solution.py:379
  110.7 0.0 copy-done.2
  110.7 1.0 down_kernel.1
  111.8 19.7 %all_to_all.41.x_ref = bf16[32,8,672]{2,1,0:T(8,128)(2,1)S(1)} all-to-all(bf16[32,8,672]{2,1,0:T(8,128)(2,1)S(1)} %bitcast.11), channel_id=1, replica_groups=mesh['z'=8,'x'=4,'y'=4,'core'=2] {'z','x'}, dimensions={0} | all-to-all | bytes 688128 | tf_op jit(solution)/shard_map/all_to_all | solution.py:333
  131.4 0.7 final_kernel.1
Async XLA Ops:
  0.1 45.2 %copy-start.3 = (bf16[512,168]{0,1:T(8,128)(2,1)S(1)}, bf16[512,168]{0,1:T(8,128)(2,1)}, u32[]{:S(2)}) copy-start(bf16[512,168]{0,1:T(8,128)(2,1)} %param.17) | copy-start | bytes 516100
  7.3 48.4 %copy-start.4 = (bf16[32,168]{1,0:T(8,128)(2,1)S(1)}, bf16[32,168]{1,0:T(8,128)(2,1)}, u32[]{:S(2)}) copy-start(bf16[32,168]{1,0:T(8,128)(2,1)} %r_ref.1) | copy-start | bytes 32260
  7.3 78.2 %copy-start = (bf16[672,672]{1,0:T(8,128)(2,1)S(1)}, bf16[672,672]{1,0:T(8,128)(2,1)}, u32[]{:S(2)}) copy-start(bf16[672,672]{1,0:T(8,128)(2,1)} %g_ref.1) | copy-start | bytes 2709508
  7.3 78.1 %copy-start.1 = (bf16[672,672]{1,0:T(8,128)(2,1)S(1)}, bf16[672,672]{1,0:T(8,128)(2,1)}, u32[]{:S(2)}) copy-start(bf16[672,672]{1,0:T(8,128)(2,1)} %u_ref.1) | copy-start | bytes 2709508
  55.8 5.0 %collective-permute-start = (bf16[48,128]{1,0:T(8,128)(2,1)S(1)}, bf16[48,128]{1,0:T(8,128)(2,1)S(1)}, u32[]{:S(2)}, u32[]{:S(2)}) collective-permute-start(bf16[48,128]{1,0:T(8,128)(2,1)S(1)} %stream_kernel.1), channel_id=1, source_target_pairs={{0,0},{1,32},{2,64},{3,96},{4,128},{5,160},{6,192},{7,224},{8,8},{... | collective-permute-start | bytes 36872 | tf_op jit(solution)/shard_map/ppermute | solution.py:356
  85.4 25.3 %copy-start.2 = (bf16[672,672]{1,0:T(8,128)(2,1)S(1)}, bf16[672,672]{1,0:T(8,128)(2,1)}, u32[]{:S(2)}) copy-start(bf16[672,672]{1,0:T(8,128)(2,1)} %w_ref.1) | copy-start | bytes 2709508
  87.1 1.8 %collective-permute-start.1 = (bf16[128,1536]{1,0:T(8,128)(2,1)S(1)}, bf16[128,1536]{1,0:T(8,128)(2,1)S(1)}, u32[]{:S(2)}, u32[]{:S(2)}) collective-permute-start(bf16[128,1536]{1,0:T(8,128)(2,1)S(1)} %get-tuple-element.13), channel_id=1, source_target_pairs={{0,1},{1,0},{2,3},{3,2},{4,5},{5,4},{6,7},{7,6},{8,9},{9,8},{10,11... | collective-permute-start | bytes 1179656 | tf_op jit(solution)/shard_map/ppermute | solution.py:375
  109.3 1.4 %collective-permute-start.2 = (bf16[128,672]{1,0:T(8,128)(2,1)S(1)}, bf16[128,672]{1,0:T(8,128)(2,1)S(1)}, u32[]{:S(2)}, u32[]{:S(2)}) collective-permute-start(bf16[128,672]{1,0:T(8,128)(2,1)S(1)} %bitcast.15), channel_id=1, source_target_pairs={{0,1},{1,0},{2,3},{3,2},{4,5},{5,4},{6,7},{7,6},{8,9},{9,8},{10,11... | collective-permute-start | bytes 516104 | tf_op jit(solution)/shard_map/ppermute | solution.py:379

commit v4 on v3

--- a/solution.py
+++ b/solution.py
@@ -37,7 +37,7 @@
 
 def attend_kernel(
     pm_hbm, sel_hbm, ids, gain_hbm, q_hbm, k_hbm, v_hbm, o_ref,
-    pm, sel, gain_ref, q_ref, kbuf, vbuf, sems, ksem, vsem, s_ref, m_ref, l_ref, acc_ref,
+    pm, sel, gain_ref, q_ref, kbuf, vbuf, sems, ksem, vsem, flags, m_ref, l_ref, acc_ref,
 ):
     tables = (
         pltpu.make_async_copy(pm_hbm, pm, sems.at[0]),
@@ -47,104 +47,93 @@
         pltpu.make_async_copy(q_hbm, q_ref, sems.at[2]),
         pltpu.make_async_copy(gain_hbm, gain_ref, sems.at[3]),
     )
-    for c in tables:
-        c.start()
-    for c in late:
-        c.start()
-    for c in tables:
-        c.wait()
-    chosen = [[jnp.int32(0), jnp.int32(0)], [jnp.int32(0), jnp.int32(0)]]
-    causal = [jnp.int32(0), jnp.int32(0)]
-    for t in range(2):
-        for j in range(8):
-            logical = sel[t, j]
-            slot = pm[logical]
-            for p in range(2):
-                hit = (slot == ids[0] * 2 + p).astype(jnp.int32)
-                chosen[p][t] = chosen[p][t] | hit
-                causal[p] = causal[p] | (hit * (logical == LAST_PAGE).astype(jnp.int32))
-    used = [chosen[p][0] | chosen[p][1] for p in range(2)]
-
-    def copies(p):
+
+    def page_copies(p):
         return (
             pltpu.make_async_copy(k_hbm.at[p], kbuf.at[p], ksem.at[p]),
             pltpu.make_async_copy(v_hbm.at[p], vbuf.at[p], vsem.at[p]),
         )
 
-    for p in range(2):
-
-        @pl.when(used[p] != 0)
-        def _(p=p):
-            for c in copies(p):
-                c.start()
-
-    for c in late:
-        c.wait()
+    for c in tables + late + page_copies(0) + page_copies(1):
+        c.start()
     m_ref[...] = jnp.full_like(m_ref, NEG)
     l_ref[...] = jnp.zeros_like(l_ref)
     acc_ref[...] = jnp.zeros_like(acc_ref)
-
-    def combo(p, t, is_causal):
-        row = lax.broadcasted_iota(jnp.int32, (256, 512), 0)
-        col = lax.broadcasted_iota(jnp.int32, (256, 512), 1)
-        limit = jnp.where(is_causal != 0, 1792 - 1536 + t * 128, 1 << 20)
+    for n in range(6):
+        flags[n] = jnp.int32(0)
+    for c in tables:
+        c.wait()
+
+    def look(n, carry):
+        logical = sel[n >> 3, n & 7]
+        p = pm[logical] - ids[0] * 2
+
+        @pl.when((p == 0) | (p == 1))
+        def _():
+            flags[p * 2 + (n >> 3)] = jnp.int32(1)
+
+            @pl.when(logical == LAST_PAGE)
+            def _():
+                flags[4 + p] = jnp.int32(1)
+
+        return carry
+
+    lax.fori_loop(0, 16, look, 0)
+    for c in late:
+        c.wait()
+
+    def attend_tile(p, t):
+        span = pl.ds(pl.multiple_of(t * 256, 256), 256)
+        rows = pl.ds(pl.multiple_of(t * 128, 128), 128)
+        limit = jnp.where(flags[4 + p] != 0, t * 128, 1 << 20)
+        row = lax.broadcasted_iota(jnp.int32, (256, 256), 0)
+        col = lax.broadcasted_iota(jnp.int32, (256, 256), 1)
         visible = col <= (row & 127) + limit
-        rows = pl.ds(pl.multiple_of(t * 128, 128), 128)
-        for kv in range(2):
-            lanes = slice(kv * 128, (kv + 1) * 128)
-            q2 = jnp.concatenate(
+
+        def scores(kv):
+            q = jnp.concatenate(
                 [q_ref[rows, (2 * kv + g) * 128 : (2 * kv + g + 1) * 128] for g in range(2)], axis=0
             )
-            top = jnp.full((256, 128), NEG, F32)
-            for j in range(4):
-                s = lax.dot_general(
-                    q2,
-                    kbuf[p, j * 512 : (j + 1) * 512, lanes],
-                    (((1,), (1,)), ((), ())),
-                    preferred_element_type=F32,
-                )
-                if j == 3:
-                    s = jnp.where(visible, s, NEG)
-                s_ref[kv, :, j * 512 : (j + 1) * 512] = s
-                for a in range(4):
-                    top = jnp.maximum(top, s[:, a * 128 : (a + 1) * 128])
-            i = t * 2 + kv
-            m_old = m_ref[i]
-            m_new = jnp.maximum(m_old, jnp.max(top, axis=1, keepdims=True))
-            alpha = jnp.exp2((m_old - m_new) * EXP2_SCALE)
-            m_wide = jnp.concatenate([m_new] * 4, axis=1)
-            total = jnp.zeros((256, 128), F32)
-            mixture = acc_ref[i] * alpha
-            for j in range(4):
-                w = jnp.exp2((s_ref[kv, :, j * 512 : (j + 1) * 512] - m_wide) * EXP2_SCALE)
-                for a in range(4):
-                    total = total + w[:, a * 128 : (a + 1) * 128]
-                mixture = mixture + jnp.dot(
-                    w.astype(BF),
-                    vbuf[p, j * 512 : (j + 1) * 512, lanes],
-                    preferred_element_type=F32,
-                )
-            m_ref[i] = m_new
-            l_ref[i] = l_ref[i] * alpha + jnp.sum(total, axis=1, keepdims=True)
-            acc_ref[i] = mixture
-
-    for p in range(2):
-
-        @pl.when(used[p] != 0)
-        def _(p=p):
-            for c in copies(p):
-                c.wait()
-
-            def tile(t, carry):
-                picked = jnp.where(t == 0, chosen[p][0], chosen[p][1])
-
-                @pl.when(picked != 0)
-                def _():
-                    combo(p, t, causal[p])
-
-                return carry
-
-            lax.fori_loop(0, 2, tile, 0)
+            s = lax.dot_general(
+                q,
+                kbuf[p, :, kv * 128 : (kv + 1) * 128],
+                (((1,), (1,)), ((), ())),
+                preferred_element_type=F32,
+            )
+            return jnp.concatenate([s[:, :1792], jnp.where(visible, s[:, 1792:], NEG)], axis=1)
+
+        for kv, s in enumerate([scores(0), scores(1)]):
+            old = m_ref[kv, span, :]
+            top = s[:, :128]
+            for a in range(1, 16):
+                top = jnp.maximum(top, s[:, a * 128 : (a + 1) * 128])
+            new = jnp.maximum(old, jnp.max(top, axis=1, keepdims=True))
+            keep = jnp.exp2((old - new) * EXP2_SCALE)
+            w = jnp.exp2((s - jnp.concatenate([new] * 16, axis=1)) * EXP2_SCALE)
+            part = w[:, :128]
+            for a in range(1, 16):
+                part = part + w[:, a * 128 : (a + 1) * 128]
+            mixed = jnp.dot(
+                w.astype(BF), vbuf[p, :, kv * 128 : (kv + 1) * 128], preferred_element_type=F32
+            )
+            m_ref[kv, span, :] = new
+            l_ref[kv, span, :] = l_ref[kv, span, :] * keep + part
+            acc_ref[kv, span, :] = acc_ref[kv, span, :] * keep + mixed
+
+    def page(p, carry):
+        for c in page_copies(p):
+            c.wait()
+
+        def tile(t, carry):
+            @pl.when(flags[p * 2 + t] != 0)
+            def _():
+                attend_tile(p, t)
+
+            return carry
+
+        return lax.fori_loop(0, 2, tile, carry)
+
+    lax.fori_loop(0, 2, page, 0)
 
     lane = lax.broadcasted_iota(jnp.int32, (128, 128), 1)
     halves = []
@@ -155,20 +144,24 @@
         [jnp.zeros((8, 16), F32), jnp.concatenate(halves, axis=0), jnp.zeros((8, 28), F32)], axis=1
     )
     gains = jnp.concatenate([gains] * 16, axis=0)
-    for t in range(2):
-        block = gains
+
+    def finish(t, carry):
+        marks = gains
+        out_rows = pl.ds(pl.multiple_of(t * 128, 128), 128)
         for h in range(4):
-            i, rows = t * 2 + h // 2, slice((h % 2) * 128, (h % 2 + 1) * 128)
-            total = l_ref[i, rows, :]
+            kv = h // 2
+            rows = pl.ds(pl.multiple_of(t * 256 + (h % 2) * 128, 128), 128)
+            total = jnp.sum(l_ref[kv, rows, :], axis=1, keepdims=True)
             some = total > 0.0
             safe = jnp.where(some, total, 1.0)
-            level = jnp.where(some, m_ref[i, rows, :] * EXP2_SCALE + jnp.log2(safe), NEG)
-            o_ref[t * 128 : (t + 1) * 128, h * 128 : (h + 1) * 128] = (
-                acc_ref[i, rows, :] / safe
-            ).astype(BF)
+            level = jnp.where(some, m_ref[kv, rows, :][:, :1] * EXP2_SCALE + jnp.log2(safe), NEG)
+            o_ref[out_rows, h * 128 : (h + 1) * 128] = (acc_ref[kv, rows, :] * (1.0 / safe)).astype(BF)
             for n, piece in enumerate(pieces(level)):
-                block = jnp.where(lane == h + 4 * n, piece, block)
-        o_ref[t * 128 : (t + 1) * 128, 512:640] = block.astype(BF)
+                marks = jnp.where(lane == h + 4 * n, piece, marks)
+        o_ref[out_rows, 512:640] = marks.astype(BF)
+        return carry
+
+    lax.fori_loop(0, 2, finish, 0)
 
 
 def in_hbm(array):
@@ -191,12 +184,12 @@
             pltpu.SemaphoreType.DMA((4,)),
             pltpu.SemaphoreType.DMA((2,)),
             pltpu.SemaphoreType.DMA((2,)),
-            pltpu.VMEM((2, 256, 2048), F32),
-            pltpu.VMEM((4, 256, 128), F32),
-            pltpu.VMEM((4, 256, 128), F32),
-            pltpu.VMEM((4, 256, 128), F32),
+            pltpu.SMEM((8,), jnp.int32),
+            pltpu.VMEM((2, 512, 128), F32),
+            pltpu.VMEM((2, 512, 128), F32),
+            pltpu.VMEM((2, 512, 128), F32),
         ],
-        compiler_params=pltpu.CompilerParams(vmem_limit_bytes=32 << 20),
+        compiler_params=pltpu.CompilerParams(vmem_limit_bytes=40 << 20),
         cost_estimate=pl.CostEstimate(
             flops=4 * 10**9, transcendentals=4 * 10**6, bytes_accessed=10 * 2**20
         ),

time: 133 us -> 134 us (level)
  blocking collectives: 111 us -> 115 us
  Pallas kernels: 12.4 us -> 8.96 us
    all_to_all x7, blocking collectives: 111 us -> 115 us  [exchange(): return lax.all_to_all(parts, axis, split_axis=0, concat_axis=0, tiled=True)]
    pallas_call x1, Pallas kernels: 7.18 us -> 3.72 us  [attend(): pl.pallas_call(attend_kernel, out_shape=jax.ShapeDtypeStruct((256, 640),...]
where the time goes in v4:
time: 134 us; the launch traced here: 132 us
  blocking collectives  115 us (86%)
  Pallas kernels  8.96 us (7%)
  waiting for transfers between devices  5.81 us (4%)
  starting transfers between devices  2.43 us (2%)
    all_to_all x7, blocking collectives, exchange(): return lax.all_to_all(parts, axis, split_axis=0, concat_axis=0, tiled=True)  115 us
    pallas_call x8, Pallas kernels, call(): pl.pallas_call(kernel, out_shape=outs, in_specs=specs, out_specs=[VMEM] *...  5.24 us
    pallas_call x1, Pallas kernels, attend(): pl.pallas_call(attend_kernel, out_shape=jax.ShapeDtypeStruct((256, 640),...  3.72 us
  transfers between devices with their start and end apart: 3, of which 3 were waited for; matrix products, arithmetic and copies ran while one was open for 0% of the time, Pallas kernels for 0%

profile of v4, /device:TPU:32, one launch (start us, length us, event | category | flops | bytes accessed | tf_op | source)
XLA Modules:
  0.0 132.4 jit_solution(10887588021148705213)
XLA Ops:
  0.0 0.1 pad_add_fusion.ids
  0.1 0.0 copy-start.3
  0.1 3.7 %attend.1 = bf16[256,640]{1,0:T(8,128)(2,1)S(1)} custom-call(s32[64]{0:T(128)} %pm_hbm.1, s32[2,8]{1,0:T(2,128)} %sel_hbm.1, s32[3]{0:T(128)S(1)} %pad_add_fusion.ids, f32[1,168]{1,0:T(1,128)} %bitcast.19, bf16[256,512]{1,0:T(8,128)(2,1)} %q_hbm.1, bf16[2,2048,256]{2,1,0:T(8,128)(2,1)} %k_hbm.1, bf16[2,2048,256]{2,1,0:T(8,128)(2,1)} %v_hbm.1), custom_call_target="tpu_custom_call" | custom-call | flops 4000000000 | bytes 10485760 | tf_op jit(solution)/shard_map/attend/pallas_call | solution.py:172
  3.8 0.0 copy-start.4
  3.8 0.0 copy-start
  3.8 0.0 copy-start.1
  3.8 24.9 %all_to_all.35.x_ref = bf16[32,8,640]{2,1,0:T(8,128)(2,1)S(1)} all-to-all(bf16[32,8,640]{2,1,0:T(8,128)(2,1)S(1)} %bitcast.17), channel_id=1, replica_groups=mesh['z'=8,'x'=4,'y'=4,'core'=2] {'z','x'}, dimensions={0} | all-to-all | bytes 655360 | tf_op jit(solution)/shard_map/all_to_all | solution.py:326
  28.7 0.9 merge_kernel.1
  29.6 16.0 %all_to_all.36 = bf16[32,8,512]{2,1,0:T(8,128)(2,1)S(1)} all-to-all(bf16[32,8,512]{2,1,0:T(8,128)(2,1)S(1)} %get-tuple-element.10), channel_id=1, replica_groups=mesh['z'=8,'x'=4,'y'=4,'core'=2] {'z','x'}, dimensions={0} | all-to-all | bytes 524288 | tf_op jit(solution)/shard_map/all_to_all | solution.py:326
  45.6 0.0 copy-done.3
  45.6 0.3 project_kernel.1
  45.9 10.1 %all_to_all.37.x_ref = bf16[8,48,128]{2,1,0:T(8,128)(2,1)S(1)} all-to-all(bf16[8,48,128]{2,1,0:T(8,128)(2,1)S(1)} %project_kernel.1), channel_id=1, replica_groups=mesh['z'=8,'x'=4,'y'=4,'core'=2] {'y','core'}, dimensions={0} | all-to-all | bytes 196608 | tf_op jit(solution)/shard_map/all_to_all | solution.py:326
  56.0 0.0 copy-done.4
  56.0 0.1 stream_kernel.1
  56.1 2.3 %collective-permute-start = (bf16[48,128]{1,0:T(8,128)(2,1)S(1)}, bf16[48,128]{1,0:T(8,128)(2,1)S(1)}, u32[]{:S(2)}, u32[]{:S(2)}) collective-permute-start(bf16[48,128]{1,0:T(8,128)(2,1)S(1)} %stream_kernel.1), channel_id=1, source_target_pairs={{0,0},{1,32},{2,64},{3,96},{4,128},{5,160},{6,192},{7,224},{8,8},{... | collective-permute-start | bytes 36872 | tf_op jit(solution)/shard_map/ppermute | solution.py:349
  58.4 2.7 %collective-permute-done = bf16[48,128]{1,0:T(8,128)(2,1)S(1)} collective-permute-done((bf16[48,128]{1,0:T(8,128)(2,1)S(1)}, bf16[48,128]{1,0:T(8,128)(2,1)S(1)}, u32[]{:S(2)}, u32[]{:S(2)}) %collective-permute-start) | collective-permute-done | bytes 12320 | tf_op jit(solution)/shard_map/ppermute | solution.py:349
  61.1 0.1 broadcast_in_dim.3
  61.1 24.6 %all_to_all.38 = bf16[32,48,128]{2,1,0:T(8,128)(2,1)S(1)} all-to-all(bf16[32,48,128]{2,1,0:T(8,128)(2,1)S(1)} %broadcast_in_dim.3), channel_id=1, replica_groups=mesh['z'=8,'x'=4,'y'=4,'core'=2] {'z','x'}, dimensions={0} | all-to-all | bytes 786432 | tf_op jit(solution)/shard_map/all_to_all | solution.py:326
  85.7 0.0 copy-done
  85.7 0.0 copy-done.1
  85.7 0.0 copy-start.2
  85.7 1.7 %gate_up_kernel.1 = (bf16[128,1536]{1,0:T(8,128)(2,1)S(1)}, bf16[128,1536]{1,0:T(8,128)(2,1)S(1)}, bf16[8,672]{1,0:T(8,128)(2,1)S(1)}) custom-call(s32[3]{0:T(128)S(1)} %pad_add_fusion.ids, bf16[8,4,48,128]{3,2,1,0:T(8,128)(2,1)S(1)} %bitcast.13, f32[4,168]{1,0:T(4,128)S(1)} %get-tuple-element.11.gain_ref, bf16[672,672]{1,0:T(8,128)(2,1)S(1)} %copy-done, ...), custom_call_target="tpu_custom_call" | custom-call | tf_op jit(solution)/shard_map/gate_up_kernel/pallas_call | solution.py:313
  87.4 0.1 collective-permute-start.1
  87.5 1.7 %collective-permute-done.1.b_ref = bf16[128,1536]{1,0:T(8,128)(2,1)S(1)} collective-permute-done((bf16[128,1536]{1,0:T(8,128)(2,1)S(1)}, bf16[128,1536]{1,0:T(8,128)(2,1)S(1)}, u32[]{:S(2)}, u32[]{:S(2)}) %collective-permute-start.1) | collective-permute-done | bytes 393248 | tf_op jit(solution)/shard_map/ppermute | solution.py:368
  89.2 0.4 pair_kernel.1
  89.6 11.0 %all_to_all.39.x_ref = bf16[4,32,1536]{2,1,0:T(8,128)(2,1)S(1)} all-to-all(bf16[4,32,1536]{2,1,0:T(8,128)(2,1)S(1)} %bitcast.12), channel_id=1, replica_groups=mesh['z'=8,'x'=4,'y'=4,'core'=2] {'y'}, dimensions={0} | all-to-all | bytes 786432 | tf_op jit(solution)/shard_map/all_to_all | solution.py:326
  100.7 0.2 hidden_kernel.1
  100.9 8.7 %all_to_all.40 = bf16[4,32,672]{2,1,0:T(8,128)(2,1)S(1)} all-to-all(bf16[4,32,672]{2,1,0:T(8,128)(2,1)S(1)} %hidden_kernel.1), channel_id=1, replica_groups=mesh['z'=8,'x'=4,'y'=4,'core'=2] {'y'}, dimensions={0} | all-to-all | bytes 344064 | tf_op jit(solution)/shard_map/all_to_all | solution.py:326
  109.6 0.0 collective-permute-start.2
  109.6 1.4 %collective-permute-done.2.b_ref = bf16[128,672]{1,0:T(8,128)(2,1)S(1)} collective-permute-done((bf16[128,672]{1,0:T(8,128)(2,1)S(1)}, bf16[128,672]{1,0:T(8,128)(2,1)S(1)}, u32[]{:S(2)}, u32[]{:S(2)}) %collective-permute-start.2) | collective-permute-done | bytes 172064 | tf_op jit(solution)/shard_map/ppermute | solution.py:372
  111.0 0.0 copy-done.2
  111.0 1.0 down_kernel.1
  112.0 19.7 %all_to_all.41.x_ref = bf16[32,8,672]{2,1,0:T(8,128)(2,1)S(1)} all-to-all(bf16[32,8,672]{2,1,0:T(8,128)(2,1)S(1)} %bitcast.11), channel_id=1, replica_groups=mesh['z'=8,'x'=4,'y'=4,'core'=2] {'z','x'}, dimensions={0} | all-to-all | bytes 688128 | tf_op jit(solution)/shard_map/all_to_all | solution.py:326
  131.7 0.7 final_kernel.1
Async XLA Ops:
  0.1 45.5 %copy-start.3 = (bf16[512,168]{0,1:T(8,128)(2,1)S(1)}, bf16[512,168]{0,1:T(8,128)(2,1)}, u32[]{:S(2)}) copy-start(bf16[512,168]{0,1:T(8,128)(2,1)} %param.17) | copy-start | bytes 516100
  3.8 52.2 %copy-start.4 = (bf16[32,168]{1,0:T(8,128)(2,1)S(1)}, bf16[32,168]{1,0:T(8,128)(2,1)}, u32[]{:S(2)}) copy-start(bf16[32,168]{1,0:T(8,128)(2,1)} %r_ref.1) | copy-start | bytes 32260
  3.8 81.9 %copy-start = (bf16[672,672]{1,0:T(8,128)(2,1)S(1)}, bf16[672,672]{1,0:T(8,128)(2,1)}, u32[]{:S(2)}) copy-start(bf16[672,672]{1,0:T(8,128)(2,1)} %g_ref.1) | copy-start | bytes 2709508
  3.8 81.9 %copy-start.1 = (bf16[672,672]{1,0:T(8,128)(2,1)S(1)}, bf16[672,672]{1,0:T(8,128)(2,1)}, u32[]{:S(2)}) copy-start(bf16[672,672]{1,0:T(8,128)(2,1)} %u_ref.1) | copy-start | bytes 2709508
  56.1 5.0 %collective-permute-start = (bf16[48,128]{1,0:T(8,128)(2,1)S(1)}, bf16[48,128]{1,0:T(8,128)(2,1)S(1)}, u32[]{:S(2)}, u32[]{:S(2)}) collective-permute-start(bf16[48,128]{1,0:T(8,128)(2,1)S(1)} %stream_kernel.1), channel_id=1, source_target_pairs={{0,0},{1,32},{2,64},{3,96},{4,128},{5,160},{6,192},{7,224},{8,8},{... | collective-permute-start | bytes 36872 | tf_op jit(solution)/shard_map/ppermute | solution.py:349
  85.7 25.3 %copy-start.2 = (bf16[672,672]{1,0:T(8,128)(2,1)S(1)}, bf16[672,672]{1,0:T(8,128)(2,1)}, u32[]{:S(2)}) copy-start(bf16[672,672]{1,0:T(8,128)(2,1)} %w_ref.1) | copy-start | bytes 2709508
  87.4 1.8 %collective-permute-start.1 = (bf16[128,1536]{1,0:T(8,128)(2,1)S(1)}, bf16[128,1536]{1,0:T(8,128)(2,1)S(1)}, u32[]{:S(2)}, u32[]{:S(2)}) collective-permute-start(bf16[128,1536]{1,0:T(8,128)(2,1)S(1)} %get-tuple-element.13), channel_id=1, source_target_pairs={{0,1},{1,0},{2,3},{3,2},{4,5},{5,4},{6,7},{7,6},{8,9},{9,8},{10,11... | collective-permute-start | bytes 1179656 | tf_op jit(solution)/shard_map/ppermute | solution.py:368
  109.6 1.4 %collective-permute-start.2 = (bf16[128,672]{1,0:T(8,128)(2,1)S(1)}, bf16[128,672]{1,0:T(8,128)(2,1)S(1)}, u32[]{:S(2)}, u32[]{:S(2)}) collective-permute-start(bf16[128,672]{1,0:T(8,128)(2,1)S(1)} %bitcast.15), channel_id=1, source_target_pairs={{0,1},{1,0},{2,3},{3,2},{4,5},{5,4},{6,7},{7,6},{8,9},{9,8},{10,11... | collective-permute-start | bytes 516104 | tf_op jit(solution)/shard_map/ppermute | solution.py:372

commit v5 on v4

--- a/solution.py
+++ b/solution.py
@@ -21,7 +21,6 @@
 HEADS = ("y", "core")
 ALL = ("z", "x", "y", "core")
 NZ, NX, NY, NC = 8, 4, 4, 2
-GU_HALF = 768
 
 VMEM = pl.BlockSpec(memory_space=pltpu.VMEM)
 SMEM = pl.BlockSpec(memory_space=pltpu.SMEM)
@@ -212,7 +211,7 @@
     for k in range(NZ * NX):
         o_ref[k] = share
     for k in range(NX):
-        gain = x_ref[ids[2] * NX + k, :, 512:640].astype(F32)
+        gain = x_ref[ids[1] * NX + k, :, 512:640].astype(F32)
         for half in range(2):
             gain_ref[k : k + 1, half * 84 : half * 84 + 84] = (
                 gain[half : half + 1, 16:100]
@@ -245,7 +244,7 @@
     o_ref[...] = total.astype(BF)
 
 
-def gate_up_kernel(ids, x_ref, gain_ref, g_ref, u_ref, mine_ref, other_ref, own_ref, stream, normed):
+def gate_up_kernel(ids, x_ref, gain_ref, g_ref, u_ref, o_ref, own_ref, stream, normed):
     for x in range(NX):
         block = x_ref[:, x, :, :].astype(F32)
         main = block[:, :32, :].reshape(256, 128)
@@ -257,51 +256,33 @@
         normed[:, first] = (main * gain_ref[x : x + 1, 0:128]).astype(BF)
         normed[:, second] = (rest * gain_ref[x : x + 1, 128:168]).astype(BF)
     own_ref[...] = stream[pl.ds(pl.multiple_of(ids[0] * 8, 8), 8), :].astype(BF)
-    core = ids[1]
-    lane = lax.broadcasted_iota(jnp.int32, (128, GU_HALF - 672), 1)
-    for ref, start in ((other_ref, (1 - core) * 128), (mine_ref, core * 128)):
-        rows = pl.ds(pl.multiple_of(start, 128), 128)
-        a = normed[rows, :]
-        s = stream[rows, :]
-        squares = jnp.sum(s * s, axis=1, keepdims=True)
-        marks = jnp.zeros((128, GU_HALF - 672), F32)
-        for n, piece in enumerate(pieces(squares)):
-            marks = jnp.where(lane == n, piece, marks)
-        ref[:, 0:672] = jnp.dot(a, g_ref[...], preferred_element_type=F32).astype(BF)
-        ref[:, 672:GU_HALF] = marks.astype(BF)
-        ref[:, GU_HALF : GU_HALF + 672] = jnp.dot(
-            a, u_ref[...], preferred_element_type=F32
-        ).astype(BF)
-        ref[:, GU_HALF + 672 :] = jnp.zeros((128, GU_HALF - 672), BF)
-
-
-def pair_kernel(a_ref, b_ref, o_ref):
-    both = a_ref[...].astype(F32) + b_ref[...].astype(F32)
-    o_ref[...] = both.astype(BF)
-    squares = both[:, 672:673] + both[:, 673:674] + both[:, 674:675]
-    lane = lax.broadcasted_iota(jnp.int32, (128, GU_HALF - 672), 1)
-    marks = jnp.zeros((128, GU_HALF - 672), F32)
+    a = normed[...]
+    s = stream[...]
+    squares = jnp.sum(s * s, axis=1, keepdims=True)
+    lane = lax.broadcasted_iota(jnp.int32, (256, 64), 1)
+    marks = jnp.zeros((256, 64), F32)
     for n, piece in enumerate(pieces(squares)):
         marks = jnp.where(lane == n, piece, marks)
-    o_ref[:, 672:GU_HALF] = marks.astype(BF)
+    gate = jnp.dot(a, g_ref[...], preferred_element_type=F32)
+    o_ref[:, 0:640] = gate[:, :640].astype(BF)
+    up = jnp.dot(a, u_ref[...], preferred_element_type=F32)
+    o_ref[:, 640:1280] = up[:, :640].astype(BF)
+    o_ref[:, 1280:] = jnp.concatenate([gate[:, 640:], up[:, 640:], marks], axis=1).astype(BF)
 
 
 def hidden_kernel(x_ref, o_ref):
     both = jnp.sum(x_ref[...].astype(F32), axis=0)
-    squares = both[:, 672:673] + both[:, 673:674] + both[:, 674:675]
+    squares = both[:, 1344:1345] + both[:, 1345:1346] + both[:, 1346:1347]
     factor = lax.rsqrt(squares / D + EPSILON)
-    gate = both[:, 0:672] * factor
-    up = both[:, GU_HALF : GU_HALF + 672] * factor
+    gate = jnp.concatenate([both[:, :640], both[:, 1280:1312]], axis=1) * factor
+    up = jnp.concatenate([both[:, 640:1280], both[:, 1312:1344]], axis=1) * factor
     hidden = (jax.nn.gelu(gate, approximate=True) * up).astype(BF)
-    for k in range(NY):
+    for k in range(NY * NC):
         o_ref[k] = hidden
 
 
-def down_kernel(ids, a_ref, b_ref, w_ref, o_ref):
-    core = ids[1]
-    for ref, start in ((a_ref, core * 128), (b_ref, (1 - core) * 128)):
-        rows = pl.ds(pl.multiple_of(start, 128), 128)
-        o_ref[rows, :] = jnp.dot(ref[...], w_ref[...], preferred_element_type=F32).astype(BF)
+def down_kernel(a_ref, w_ref, o_ref):
+    o_ref[...] = jnp.dot(a_ref[...], w_ref[...], preferred_element_type=F32).astype(BF)
 
 
 def final_kernel(x_ref, s_ref, o_ref):
@@ -334,9 +315,8 @@
     queries, keys, values, page_map, selected, residual_in, out_weight, norm_gain, gate_weight, up_weight, down_weight
 ):
     ctx = (lax.axis_index("z") * NX + lax.axis_index("x")).astype(jnp.int32)
-    core = lax.axis_index("core").astype(jnp.int32)
-    head = lax.axis_index("y").astype(jnp.int32) * NC + core
-    ids = jnp.stack([ctx, core, head])
+    head = (lax.axis_index("y") * NC + lax.axis_index("core")).astype(jnp.int32)
+    ids = jnp.stack([ctx, head])
     sent = attend(page_map, selected, ids, norm_gain.reshape(1, 168), queries, keys, values)
     arrived = exchange(sent.reshape(32, 8, 640), CTX)
     shares, gain = call(
@@ -352,10 +332,9 @@
         [(place(z, x, h), place(h, x, z)) for z in range(NZ) for x in range(NX) for h in range(NZ)],
     )
     rows = exchange(jnp.broadcast_to(turned, (NZ * NX, 48, 128)), CTX)
-    half = ((128, 2 * GU_HALF), BF)
-    mine, other, own_stream = call(
+    parts, own_stream = call(
         gate_up_kernel,
-        [half, half, ((8, 672), BF)],
+        [((256, 1408), BF), ((8, 672), BF)],
         [SMEM, VMEM, VMEM, VMEM, VMEM],
         ids,
         rows.reshape(NZ, NX, 48, 128),
@@ -364,20 +343,10 @@
         up_weight,
         scratch=[pltpu.VMEM((256, 672), F32), pltpu.VMEM((256, 672), BF)],
     )
-    swap = [(0, 1), (1, 0)]
-    pair = call(pair_kernel, [half], [VMEM, VMEM], mine, lax.ppermute(other, "core", swap))
-    quarters = exchange(pair.reshape(NY, 32, 2 * GU_HALF), "y")
-    hidden = call(hidden_kernel, [((NY, 32, 672), BF)], [VMEM], quarters)
-    hidden_half = exchange(hidden, "y").reshape(128, 672)
-    hidden_other = lax.ppermute(hidden_half, "core", swap)
+    shared = exchange(parts.reshape(NY * NC, 32, 1408), HEADS)
+    hidden = exchange(call(hidden_kernel, [((NY * NC, 32, 672), BF)], [VMEM], shared), HEADS)
     down = call(
-        down_kernel,
-        [((256, 672), BF)],
-        [SMEM, VMEM, VMEM, VMEM],
-        ids,
-        hidden_half,
-        hidden_other,
-        down_weight,
+        down_kernel, [((256, 672), BF)], [VMEM, VMEM], hidden.reshape(256, 672), down_weight
     )
     out_parts = exchange(down.reshape(32, 8, 672), CTX)
     return call(final_kernel, [((8, 672), BF)], [VMEM, VMEM], out_parts, own_stream)

time: 134 us -> 137 us (1.022); the launches traced: 132 us -> 137 us
  blocking collectives: 115 us -> 124 us
  waiting for transfers between devices: 5.81 us -> 2.67 us
    all_to_all x7, blocking collectives: 115 us -> 124 us  [exchange(): return lax.all_to_all(parts, axis, split_axis=0, concat_axis=0, tiled=True)]
    ppermute x2 -> x0, waiting for transfers between devices: 3.15 us -> none  [the longest x1 1.71 us: shards(): lax.ppermute(other, 'core', swap)]
    pallas_call x8 -> x7, Pallas kernels: 5.24 us -> 4.34 us  [call(): pl.pallas_call(kernel, out_shape=outs, in_specs=specs, out_specs=[VMEM] *...]
  transfers between devices with their start and end apart: 3 -> 1, of which waited for: 3 -> 1; matrix products, arithmetic and copies ran while one was open for 0% -> 0% of each run, Pallas kernels for 0% -> 0%
where the time goes in v5:
time: 137 us
  blocking collectives  124 us (91%)
  Pallas kernels  8.05 us (6%)
  waiting for transfers between devices  2.67 us (2%)
  starting transfers between devices  2.33 us (2%)
    all_to_all x7, blocking collectives, exchange(): return lax.all_to_all(parts, axis, split_axis=0, concat_axis=0, tiled=True)  124 us
    pallas_call x7, Pallas kernels, call(): pl.pallas_call(kernel, out_shape=outs, in_specs=specs, out_specs=[VMEM] *...  4.34 us
    pallas_call x1, Pallas kernels, attend(): pl.pallas_call(attend_kernel, out_shape=jax.ShapeDtypeStruct((256, 640),...  3.72 us
  transfers between devices with their start and end apart: 1, of which 1 were waited for; matrix products, arithmetic and copies ran while one was open for 0% of the time, Pallas kernels for 0%

profile of v5, /device:TPU:32, one launch (start us, length us, event | category | flops | bytes accessed | tf_op | source)
XLA Modules:
  0.0 137.1 jit_solution(3445428260053326310)
XLA Ops:
  0.0 0.1 pad_add_fusion.ids
  0.1 0.0 copy-start.3
  0.1 3.7 %attend.1 = bf16[256,640]{1,0:T(8,128)(2,1)S(1)} custom-call(s32[64]{0:T(128)} %pm_hbm.1, s32[2,8]{1,0:T(2,128)} %sel_hbm.1, s32[2]{0:T(128)S(1)} %pad_add_fusion.ids, f32[1,168]{1,0:T(1,128)} %bitcast.17, bf16[256,512]{1,0:T(8,128)(2,1)} %q_hbm.1, bf16[2,2048,256]{2,1,0:T(8,128)(2,1)} %k_hbm.1, bf16[2,2048,256]{2,1,0:T(8,128)(2,1)} %v_hbm.1), custom_call_target="tpu_custom_call" | custom-call | flops 4000000000 | bytes 10485760 | tf_op jit(solution)/shard_map/attend/pallas_call | solution.py:171
  3.8 0.0 copy-start.4
  3.8 0.0 copy-start.1
  3.8 0.0 copy-start.2
  3.8 27.5 %all_to_all.35.x_ref = bf16[32,8,640]{2,1,0:T(8,128)(2,1)S(1)} all-to-all(bf16[32,8,640]{2,1,0:T(8,128)(2,1)S(1)} %bitcast.15), channel_id=1, replica_groups=mesh['z'=8,'x'=4,'y'=4,'core'=2] {'z','x'}, dimensions={0} | all-to-all | bytes 655360 | tf_op jit(solution)/shard_map/all_to_all | solution.py:307
  31.4 0.9 merge_kernel.1
  32.3 16.0 %all_to_all.36 = bf16[32,8,512]{2,1,0:T(8,128)(2,1)S(1)} all-to-all(bf16[32,8,512]{2,1,0:T(8,128)(2,1)S(1)} %get-tuple-element.9), channel_id=1, replica_groups=mesh['z'=8,'x'=4,'y'=4,'core'=2] {'z','x'}, dimensions={0} | all-to-all | bytes 524288 | tf_op jit(solution)/shard_map/all_to_all | solution.py:307
  48.3 0.0 copy-done.3
  48.3 0.3 project_kernel.1
  48.6 10.1 %all_to_all.37.x_ref = bf16[8,48,128]{2,1,0:T(8,128)(2,1)S(1)} all-to-all(bf16[8,48,128]{2,1,0:T(8,128)(2,1)S(1)} %project_kernel.1), channel_id=1, replica_groups=mesh['z'=8,'x'=4,'y'=4,'core'=2] {'y','core'}, dimensions={0} | all-to-all | bytes 196608 | tf_op jit(solution)/shard_map/all_to_all | solution.py:307
  58.6 0.0 copy-done.4
  58.7 0.1 stream_kernel.1
  58.7 2.3 %collective-permute-start = (bf16[48,128]{1,0:T(8,128)(2,1)S(1)}, bf16[48,128]{1,0:T(8,128)(2,1)S(1)}, u32[]{:S(2)}, u32[]{:S(2)}) collective-permute-start(bf16[48,128]{1,0:T(8,128)(2,1)S(1)} %stream_kernel.1), channel_id=1, source_target_pairs={{0,0},{1,32},{2,64},{3,96},{4,128},{5,160},{6,192},{7,224},{8,8},{... | collective-permute-start | bytes 36872 | tf_op jit(solution)/shard_map/ppermute | solution.py:329
  61.1 2.7 %collective-permute-done = bf16[48,128]{1,0:T(8,128)(2,1)S(1)} collective-permute-done((bf16[48,128]{1,0:T(8,128)(2,1)S(1)}, bf16[48,128]{1,0:T(8,128)(2,1)S(1)}, u32[]{:S(2)}, u32[]{:S(2)}) %collective-permute-start) | collective-permute-done | bytes 12320 | tf_op jit(solution)/shard_map/ppermute | solution.py:329
  63.7 0.1 broadcast_in_dim.3
  63.8 24.6 %all_to_all.38 = bf16[32,48,128]{2,1,0:T(8,128)(2,1)S(1)} all-to-all(bf16[32,48,128]{2,1,0:T(8,128)(2,1)S(1)} %broadcast_in_dim.3), channel_id=1, replica_groups=mesh['z'=8,'x'=4,'y'=4,'core'=2] {'z','x'}, dimensions={0} | all-to-all | bytes 786432 | tf_op jit(solution)/shard_map/all_to_all | solution.py:307
  88.4 0.0 copy-done.1
  88.4 0.0 copy-done.2
  88.4 1.7 %gate_up_kernel.1 = (bf16[256,1408]{1,0:T(8,128)(2,1)S(1)}, bf16[8,672]{1,0:T(8,128)(2,1)S(1)}) custom-call(s32[2]{0:T(128)S(1)} %pad_add_fusion.ids, bf16[8,4,48,128]{3,2,1,0:T(8,128)(2,1)S(1)} %bitcast.12, f32[4,168]{1,0:T(4,128)S(1)} %get-tuple-element.10.gain_ref, bf16[672,672]{1,0:T(8,128)(2,1)S(1)} %copy-done.1, bf16[672,672]{1,0:T(8,128)(2,1)S(1)} %copy-done.2), custom_call_target="tpu_custom_call" | custom-call | tf_op jit(solution)/shard_map/gate_up_kernel/pallas_call | solution.py:294
  90.1 0.0 copy-start
  90.1 15.1 %all_to_all.39.x_ref = bf16[8,32,1408]{2,1,0:T(8,128)(2,1)S(1)} all-to-all(bf16[8,32,1408]{2,1,0:T(8,128)(2,1)S(1)} %bitcast.14), channel_id=1, replica_groups=mesh['z'=8,'x'=4,'y'=4,'core'=2] {'y','core'}, dimensions={0} | all-to-all | bytes 1441792 | tf_op jit(solution)/shard_map/all_to_all | solution.py:307
  105.2 0.2 hidden_kernel.1
  105.4 11.3 %all_to_all.40 = bf16[8,32,672]{2,1,0:T(8,128)(2,1)S(1)} all-to-all(bf16[8,32,672]{2,1,0:T(8,128)(2,1)S(1)} %hidden_kernel.1), channel_id=1, replica_groups=mesh['z'=8,'x'=4,'y'=4,'core'=2] {'y','core'}, dimensions={0} | all-to-all | bytes 688128 | tf_op jit(solution)/shard_map/all_to_all | solution.py:307
  116.7 0.0 copy-done
  116.7 0.5 down_kernel.1
  117.2 19.2 %all_to_all.41.x_ref = bf16[32,8,672]{2,1,0:T(8,128)(2,1)S(1)} all-to-all(bf16[32,8,672]{2,1,0:T(8,128)(2,1)S(1)} %bitcast.11), channel_id=1, replica_groups=mesh['z'=8,'x'=4,'y'=4,'core'=2] {'z','x'}, dimensions={0} | all-to-all | bytes 688128 | tf_op jit(solution)/shard_map/all_to_all | solution.py:307
  136.4 0.7 final_kernel.1
Async XLA Ops:
  0.1 48.2 %copy-start.3 = (bf16[512,168]{0,1:T(8,128)(2,1)S(1)}, bf16[512,168]{0,1:T(8,128)(2,1)}, u32[]{:S(2)}) copy-start(bf16[512,168]{0,1:T(8,128)(2,1)} %param.17) | copy-start | bytes 516100
  3.8 54.8 %copy-start.4 = (bf16[32,168]{1,0:T(8,128)(2,1)S(1)}, bf16[32,168]{1,0:T(8,128)(2,1)}, u32[]{:S(2)}) copy-start(bf16[32,168]{1,0:T(8,128)(2,1)} %r_ref.1) | copy-start | bytes 32260
  3.8 84.6 %copy-start.1 = (bf16[672,672]{1,0:T(8,128)(2,1)S(1)}, bf16[672,672]{1,0:T(8,128)(2,1)}, u32[]{:S(2)}) copy-start(bf16[672,672]{1,0:T(8,128)(2,1)} %g_ref.1) | copy-start | bytes 2709508
  3.8 84.6 %copy-start.2 = (bf16[672,672]{1,0:T(8,128)(2,1)S(1)}, bf16[672,672]{1,0:T(8,128)(2,1)}, u32[]{:S(2)}) copy-start(bf16[672,672]{1,0:T(8,128)(2,1)} %u_ref.1) | copy-start | bytes 2709508
  58.7 5.0 %collective-permute-start = (bf16[48,128]{1,0:T(8,128)(2,1)S(1)}, bf16[48,128]{1,0:T(8,128)(2,1)S(1)}, u32[]{:S(2)}, u32[]{:S(2)}) collective-permute-start(bf16[48,128]{1,0:T(8,128)(2,1)S(1)} %stream_kernel.1), channel_id=1, source_target_pairs={{0,0},{1,32},{2,64},{3,96},{4,128},{5,160},{6,192},{7,224},{8,8},{... | collective-permute-start | bytes 36872 | tf_op jit(solution)/shard_map/ppermute | solution.py:329
  90.1 26.6 %copy-start = (bf16[672,672]{1,0:T(8,128)(2,1)S(1)}, bf16[672,672]{1,0:T(8,128)(2,1)}, u32[]{:S(2)}) copy-start(bf16[672,672]{1,0:T(8,128)(2,1)} %w_ref.1) | copy-start | bytes 2709508

commit v6 on v5

--- a/solution.py
+++ b/solution.py
@@ -244,7 +244,20 @@
     o_ref[...] = total.astype(BF)
 
 
-def gate_up_kernel(ids, x_ref, gain_ref, g_ref, u_ref, o_ref, own_ref, stream, normed):
+def gate_up(a, squares, g_ref, u_ref):
+    lane = lax.broadcasted_iota(jnp.int32, (128, 64), 1)
+    marks = jnp.zeros((128, 64), F32)
+    for n, piece in enumerate(pieces(squares)):
+        marks = jnp.where(lane == n, piece, marks)
+    gate = jnp.dot(a, g_ref[...], preferred_element_type=F32)
+    up = jnp.dot(a, u_ref[...], preferred_element_type=F32)
+    tail = jnp.concatenate([gate[:, 640:], up[:, 640:], marks], axis=1)
+    return gate[:, :640].astype(BF), up[:, :640].astype(BF), tail.astype(BF)
+
+
+def other_half_kernel(
+    ids, x_ref, gain_ref, g_ref, u_ref, o_ref, normed_ref, squares_ref, own_ref, stream, normed
+):
     for x in range(NX):
         block = x_ref[:, x, :, :].astype(F32)
         main = block[:, :32, :].reshape(256, 128)
@@ -255,19 +268,32 @@
         stream[:, second] = rest
         normed[:, first] = (main * gain_ref[x : x + 1, 0:128]).astype(BF)
         normed[:, second] = (rest * gain_ref[x : x + 1, 128:168]).astype(BF)
+    theirs = pl.ds(pl.multiple_of((1 - ids[2]) * 128, 128), 128)
+    mine = pl.ds(pl.multiple_of(ids[2] * 128, 128), 128)
+    s = stream[theirs, :]
+    o_ref[:, :640], o_ref[:, 640:1280], o_ref[:, 1280:] = gate_up(
+        normed[theirs, :], jnp.sum(s * s, axis=1, keepdims=True), g_ref, u_ref
+    )
+    normed_ref[...] = normed[mine, :]
+    s = stream[mine, :]
+    squares_ref[...] = jnp.broadcast_to(jnp.sum(s * s, axis=1, keepdims=True), (128, 128))
     own_ref[...] = stream[pl.ds(pl.multiple_of(ids[0] * 8, 8), 8), :].astype(BF)
-    a = normed[...]
-    s = stream[...]
-    squares = jnp.sum(s * s, axis=1, keepdims=True)
-    lane = lax.broadcasted_iota(jnp.int32, (256, 64), 1)
-    marks = jnp.zeros((256, 64), F32)
-    for n, piece in enumerate(pieces(squares)):
-        marks = jnp.where(lane == n, piece, marks)
-    gate = jnp.dot(a, g_ref[...], preferred_element_type=F32)
-    o_ref[:, 0:640] = gate[:, :640].astype(BF)
-    up = jnp.dot(a, u_ref[...], preferred_element_type=F32)
-    o_ref[:, 640:1280] = up[:, :640].astype(BF)
-    o_ref[:, 1280:] = jnp.concatenate([gate[:, 640:], up[:, 640:], marks], axis=1).astype(BF)
+
+
+def own_half_kernel(a_ref, squares_ref, g_ref, u_ref, o_ref):
+    o_ref[:, :640], o_ref[:, 640:1280], o_ref[:, 1280:] = gate_up(
+        a_ref[...], squares_ref[:, :1], g_ref, u_ref
+    )
+
+
+def pair_kernel(a_ref, b_ref, o_ref):
+    both = a_ref[...].astype(F32) + b_ref[...].astype(F32)
+    o_ref[:, :1280] = both[:, :1280].astype(BF)
+    tail = both[:, 1280:]
+    lane = lax.broadcasted_iota(jnp.int32, (128, 128), 1)
+    for n, piece in enumerate(pieces(tail[:, 64:65] + tail[:, 65:66] + tail[:, 66:67])):
+        tail = jnp.where(lane == 64 + n, piece, tail)
+    o_ref[:, 1280:] = tail.astype(BF)
 
 
 def hidden_kernel(x_ref, o_ref):
@@ -282,7 +308,8 @@
 
 
 def down_kernel(a_ref, w_ref, o_ref):
-    o_ref[...] = jnp.dot(a_ref[...], w_ref[...], preferred_element_type=F32).astype(BF)
+    a = jnp.concatenate([a_ref[y * NC + c] for c in range(NC) for y in range(NY)], axis=0)
+    o_ref[...] = jnp.dot(a, w_ref[...], preferred_element_type=F32).astype(BF)
 
 
 def final_kernel(x_ref, s_ref, o_ref):
@@ -315,8 +342,9 @@
     queries, keys, values, page_map, selected, residual_in, out_weight, norm_gain, gate_weight, up_weight, down_weight
 ):
     ctx = (lax.axis_index("z") * NX + lax.axis_index("x")).astype(jnp.int32)
-    head = (lax.axis_index("y") * NC + lax.axis_index("core")).astype(jnp.int32)
-    ids = jnp.stack([ctx, head])
+    core = lax.axis_index("core").astype(jnp.int32)
+    head = lax.axis_index("y").astype(jnp.int32) * NC + core
+    ids = jnp.stack([ctx, head, core])
     sent = attend(page_map, selected, ids, norm_gain.reshape(1, 168), queries, keys, values)
     arrived = exchange(sent.reshape(32, 8, 640), CTX)
     shares, gain = call(
@@ -332,9 +360,10 @@
         [(place(z, x, h), place(h, x, z)) for z in range(NZ) for x in range(NX) for h in range(NZ)],
     )
     rows = exchange(jnp.broadcast_to(turned, (NZ * NX, 48, 128)), CTX)
-    parts, own_stream = call(
-        gate_up_kernel,
-        [((256, 1408), BF), ((8, 672), BF)],
+    half = ((128, 1408), BF)
+    other, normed, squares, own_stream = call(
+        other_half_kernel,
+        [half, ((128, 672), BF), ((128, 128), F32), ((8, 672), BF)],
         [SMEM, VMEM, VMEM, VMEM, VMEM],
         ids,
         rows.reshape(NZ, NX, 48, 128),
@@ -343,10 +372,13 @@
         up_weight,
         scratch=[pltpu.VMEM((256, 672), F32), pltpu.VMEM((256, 672), BF)],
     )
-    shared = exchange(parts.reshape(NY * NC, 32, 1408), HEADS)
+    received = lax.ppermute(other, "core", [(0, 1), (1, 0)])
+    mine = call(own_half_kernel, [half], [VMEM] * 4, normed, squares, gate_weight, up_weight)
+    pair = call(pair_kernel, [half], [VMEM, VMEM], mine, received)
+    shared = exchange(pair.reshape(NY, 32, 1408), "y")
     hidden = exchange(call(hidden_kernel, [((NY * NC, 32, 672), BF)], [VMEM], shared), HEADS)
     down = call(
-        down_kernel, [((256, 672), BF)], [VMEM, VMEM], hidden.reshape(256, 672), down_weight
+        down_kernel, [((256, 672), BF)], [VMEM, VMEM], hidden, down_weight
     )
     out_parts = exchange(down.reshape(32, 8, 672), CTX)
     return call(final_kernel, [((8, 672), BF)], [VMEM, VMEM], out_parts, own_stream)

time: 137 us -> 134 us (0.978)
  blocking collectives: 124 us -> 118 us
    all_to_all x7, blocking collectives: 124 us -> 118 us  [exchange(): return lax.all_to_all(parts, axis, split_axis=0, concat_axis=0, tiled=True)]
    pallas_call x7 -> x9, Pallas kernels: 4.34 us -> 4.83 us  [call(): pl.pallas_call(kernel, out_shape=outs, in_specs=specs, out_specs=[VMEM] *...]
  transfers between devices with their start and end apart: 1 -> 2, of which waited for: 1 -> 2; matrix products, arithmetic and copies ran while one was open for 0% -> 0% of each run, Pallas kernels for 0% -> 0%
where the time goes in v6:
time: 134 us; the launch traced here: 133 us
  blocking collectives  118 us (88%)
  Pallas kernels  8.55 us (6%)
  waiting for transfers between devices  3.75 us (3%)
  starting transfers between devices  2.42 us (2%)
    all_to_all x7, blocking collectives, exchange(): return lax.all_to_all(parts, axis, split_axis=0, concat_axis=0, tiled=True)  118 us
    pallas_call x9, Pallas kernels, call(): pl.pallas_call(kernel, out_shape=outs, in_specs=specs, out_specs=[VMEM] *...  4.83 us
    pallas_call x1, Pallas kernels, attend(): pl.pallas_call(attend_kernel, out_shape=jax.ShapeDtypeStruct((256, 640),...  3.72 us
  transfers between devices with their start and end apart: 2, of which 2 were waited for; matrix products, arithmetic and copies ran while one was open for 0% of the time, Pallas kernels for 0%

profile of v6, /device:TPU:32, one launch (start us, length us, event | category | flops | bytes accessed | tf_op | source)
XLA Modules:
  0.0 133.3 jit_solution(16067122086515422541)
XLA Ops:
  0.0 0.1 pad_add_fusion.ids
  0.1 0.0 copy-start.3
  0.1 3.7 %attend.1 = bf16[256,640]{1,0:T(8,128)(2,1)S(1)} custom-call(s32[64]{0:T(128)} %pm_hbm.1, s32[2,8]{1,0:T(2,128)} %sel_hbm.1, s32[3]{0:T(128)S(1)} %pad_add_fusion.ids, f32[1,168]{1,0:T(1,128)} %bitcast.16, bf16[256,512]{1,0:T(8,128)(2,1)} %q_hbm.1, bf16[2,2048,256]{2,1,0:T(8,128)(2,1)} %k_hbm.1, bf16[2,2048,256]{2,1,0:T(8,128)(2,1)} %v_hbm.1), custom_call_target="tpu_custom_call" | custom-call | flops 4000000000 | bytes 10485760 | tf_op jit(solution)/shard_map/attend/pallas_call | solution.py:171
  3.8 0.0 copy-start.4
  3.8 0.0 copy-start
  3.8 0.0 copy-start.1
  3.8 26.5 %all_to_all.35.x_ref = bf16[32,8,640]{2,1,0:T(8,128)(2,1)S(1)} all-to-all(bf16[32,8,640]{2,1,0:T(8,128)(2,1)S(1)} %bitcast.14), channel_id=1, replica_groups=mesh['z'=8,'x'=4,'y'=4,'core'=2] {'z','x'}, dimensions={0} | all-to-all | bytes 655360 | tf_op jit(solution)/shard_map/all_to_all | solution.py:334
  30.3 0.9 merge_kernel.1
  31.2 16.0 %all_to_all.36 = bf16[32,8,512]{2,1,0:T(8,128)(2,1)S(1)} all-to-all(bf16[32,8,512]{2,1,0:T(8,128)(2,1)S(1)} %get-tuple-element.11), channel_id=1, replica_groups=mesh['z'=8,'x'=4,'y'=4,'core'=2] {'z','x'}, dimensions={0} | all-to-all | bytes 524288 | tf_op jit(solution)/shard_map/all_to_all | solution.py:334
  47.2 0.0 copy-done.3
  47.2 0.3 project_kernel.1
  47.5 10.1 %all_to_all.37.x_ref = bf16[8,48,128]{2,1,0:T(8,128)(2,1)S(1)} all-to-all(bf16[8,48,128]{2,1,0:T(8,128)(2,1)S(1)} %project_kernel.1), channel_id=1, replica_groups=mesh['z'=8,'x'=4,'y'=4,'core'=2] {'y','core'}, dimensions={0} | all-to-all | bytes 196608 | tf_op jit(solution)/shard_map/all_to_all | solution.py:334
  57.6 0.0 copy-done.4
  57.6 0.1 stream_kernel.1
  57.7 2.3 %collective-permute-start = (bf16[48,128]{1,0:T(8,128)(2,1)S(1)}, bf16[48,128]{1,0:T(8,128)(2,1)S(1)}, u32[]{:S(2)}, u32[]{:S(2)}) collective-permute-start(bf16[48,128]{1,0:T(8,128)(2,1)S(1)} %stream_kernel.1), channel_id=1, source_target_pairs={{0,0},{1,32},{2,64},{3,96},{4,128},{5,160},{6,192},{7,224},{8,8},{... | collective-permute-start | bytes 36872 | tf_op jit(solution)/shard_map/ppermute | solution.py:357
  60.0 2.7 %collective-permute-done = bf16[48,128]{1,0:T(8,128)(2,1)S(1)} collective-permute-done((bf16[48,128]{1,0:T(8,128)(2,1)S(1)}, bf16[48,128]{1,0:T(8,128)(2,1)S(1)}, u32[]{:S(2)}, u32[]{:S(2)}) %collective-permute-start) | collective-permute-done | bytes 12320 | tf_op jit(solution)/shard_map/ppermute | solution.py:357
  62.7 0.1 broadcast_in_dim.3
  62.7 24.6 %all_to_all.38 = bf16[32,48,128]{2,1,0:T(8,128)(2,1)S(1)} all-to-all(bf16[32,48,128]{2,1,0:T(8,128)(2,1)S(1)} %broadcast_in_dim.3), channel_id=1, replica_groups=mesh['z'=8,'x'=4,'y'=4,'core'=2] {'z','x'}, dimensions={0} | all-to-all | bytes 786432 | tf_op jit(solution)/shard_map/all_to_all | solution.py:334
  87.3 0.0 copy-done
  87.3 0.0 copy-done.1
  87.3 1.4 %other_half_kernel.1 = (bf16[128,1408]{1,0:T(8,128)(2,1)S(1)}, bf16[128,672]{1,0:T(8,128)(2,1)S(1)}, f32[128,128]{1,0:T(8,128)S(1)}, bf16[8,672]{1,0:T(8,128)(2,1)S(1)}) custom-call(s32[3]{0:T(128)S(1)} %pad_add_fusion.ids, bf16[8,4,48,128]{3,2,1,0:T(8,128)(2,1)S(1)} %bitcast.11, f32[4,168]{1,0:T(4,128)S(1)} %get-tuple-element.12.gain_ref, ...), custom_call_target="tpu_custom_call" | custom-call | tf_op jit(solution)/shard_map/other_half_kernel/pallas_call | solution.py:321
  88.7 0.1 collective-permute-start.1
  88.8 0.6 own_half_kernel.1.a_ref
  89.4 0.0 copy-start.2
  89.4 1.1 collective-permute-done.1.b_ref
  90.5 0.2 pair_kernel.1
  90.7 10.7 %all_to_all.39.x_ref = bf16[4,32,1408]{2,1,0:T(8,128)(2,1)S(1)} all-to-all(bf16[4,32,1408]{2,1,0:T(8,128)(2,1)S(1)} %bitcast.12), channel_id=1, replica_groups=mesh['z'=8,'x'=4,'y'=4,'core'=2] {'y'}, dimensions={0} | all-to-all | bytes 720896 | tf_op jit(solution)/shard_map/all_to_all | solution.py:334
  101.4 0.2 hidden_kernel.1
  101.6 11.3 %all_to_all.40.a_ref = bf16[8,32,672]{2,1,0:T(8,128)(2,1)S(1)} all-to-all(bf16[8,32,672]{2,1,0:T(8,128)(2,1)S(1)} %hidden_kernel.1), channel_id=1, replica_groups=mesh['z'=8,'x'=4,'y'=4,'core'=2] {'y','core'}, dimensions={0} | all-to-all | bytes 688128 | tf_op jit(solution)/shard_map/all_to_all | solution.py:334
  113.0 0.0 copy-done.2
  113.0 0.5 down_kernel.1
  113.5 19.2 %all_to_all.41.x_ref = bf16[32,8,672]{2,1,0:T(8,128)(2,1)S(1)} all-to-all(bf16[32,8,672]{2,1,0:T(8,128)(2,1)S(1)} %bitcast.10), channel_id=1, replica_groups=mesh['z'=8,'x'=4,'y'=4,'core'=2] {'z','x'}, dimensions={0} | all-to-all | bytes 688128 | tf_op jit(solution)/shard_map/all_to_all | solution.py:334
  132.6 0.7 final_kernel.1
Async XLA Ops:
  0.1 47.1 %copy-start.3 = (bf16[512,168]{0,1:T(8,128)(2,1)S(1)}, bf16[512,168]{0,1:T(8,128)(2,1)}, u32[]{:S(2)}) copy-start(bf16[512,168]{0,1:T(8,128)(2,1)} %param.17) | copy-start | bytes 516100
  3.8 53.8 %copy-start.4 = (bf16[32,168]{1,0:T(8,128)(2,1)S(1)}, bf16[32,168]{1,0:T(8,128)(2,1)}, u32[]{:S(2)}) copy-start(bf16[32,168]{1,0:T(8,128)(2,1)} %r_ref.1) | copy-start | bytes 32260
  3.8 83.5 %copy-start = (bf16[672,672]{1,0:T(8,128)(2,1)S(1)}, bf16[672,672]{1,0:T(8,128)(2,1)}, u32[]{:S(2)}) copy-start(bf16[672,672]{1,0:T(8,128)(2,1)} %g_ref.3) | copy-start | bytes 2709508
  3.8 83.5 %copy-start.1 = (bf16[672,672]{1,0:T(8,128)(2,1)S(1)}, bf16[672,672]{1,0:T(8,128)(2,1)}, u32[]{:S(2)}) copy-start(bf16[672,672]{1,0:T(8,128)(2,1)} %u_ref.3) | copy-start | bytes 2709508
  57.7 5.0 %collective-permute-start = (bf16[48,128]{1,0:T(8,128)(2,1)S(1)}, bf16[48,128]{1,0:T(8,128)(2,1)S(1)}, u32[]{:S(2)}, u32[]{:S(2)}) collective-permute-start(bf16[48,128]{1,0:T(8,128)(2,1)S(1)} %stream_kernel.1), channel_id=1, source_target_pairs={{0,0},{1,32},{2,64},{3,96},{4,128},{5,160},{6,192},{7,224},{8,8},{... | collective-permute-start | bytes 36872 | tf_op jit(solution)/shard_map/ppermute | solution.py:357
  88.7 1.8 %collective-permute-start.1 = (bf16[128,1408]{1,0:T(8,128)(2,1)S(1)}, bf16[128,1408]{1,0:T(8,128)(2,1)S(1)}, u32[]{:S(2)}, u32[]{:S(2)}) collective-permute-start(bf16[128,1408]{1,0:T(8,128)(2,1)S(1)} %get-tuple-element.15), channel_id=1, source_target_pairs={{0,1},{1,0},{2,3},{3,2},{4,5},{5,4},{6,7},{7,6},{8,9},{9,8},{10,11... | collective-permute-start | bytes 1081352 | tf_op jit(solution)/shard_map/ppermute | solution.py:375
  89.4 23.6 %copy-start.2 = (bf16[672,672]{1,0:T(8,128)(2,1)S(1)}, bf16[672,672]{1,0:T(8,128)(2,1)}, u32[]{:S(2)}) copy-start(bf16[672,672]{1,0:T(8,128)(2,1)} %w_ref.1) | copy-start | bytes 2709508

commit v7 on v6

--- a/solution.py
+++ b/solution.py
@@ -208,8 +208,7 @@
     total = jnp.sum(weight, axis=0)
     mixed = jnp.sum(weight * x[:, :, :512], axis=0)
     share = (mixed / total).astype(BF)
-    for k in range(NZ * NX):
-        o_ref[k] = share
+    o_ref[...] = share
     for k in range(NX):
         gain = x_ref[ids[1] * NX + k, :, 512:640].astype(F32)
         for half in range(2):
@@ -247,7 +246,7 @@
 def gate_up(a, squares, g_ref, u_ref):
     lane = lax.broadcasted_iota(jnp.int32, (128, 64), 1)
     marks = jnp.zeros((128, 64), F32)
-    for n, piece in enumerate(pieces(squares)):
+    for n, piece in enumerate(pieces(jnp.sum(squares, axis=1, keepdims=True))):
         marks = jnp.where(lane == n, piece, marks)
     gate = jnp.dot(a, g_ref[...], preferred_element_type=F32)
     up = jnp.dot(a, u_ref[...], preferred_element_type=F32)
@@ -255,34 +254,39 @@
     return gate[:, :640].astype(BF), up[:, :640].astype(BF), tail.astype(BF)
 
 
+def unpacked(block):
+    rest = jnp.concatenate([block[..., 32:48, 0:40], block[..., 32:48, 40:80]], axis=-2)
+    return block[..., :32, :], rest
+
+
 def other_half_kernel(
-    ids, x_ref, gain_ref, g_ref, u_ref, o_ref, normed_ref, squares_ref, own_ref, stream, normed
+    ids, x_ref, gain_ref, g_ref, u_ref, o_ref, normed_ref, squares_ref, own_ref, own, squares, normed
 ):
+    full = jnp.zeros((256, 128), F32)
+    part = jnp.zeros((256, 40), F32)
     for x in range(NX):
-        block = x_ref[:, x, :, :].astype(F32)
-        main = block[:, :32, :].reshape(256, 128)
-        rest = jnp.concatenate([block[:, 32:48, 0:40], block[:, 32:48, 40:80]], axis=1)
-        rest = rest.reshape(256, 40)
+        main, rest = unpacked(x_ref[:, x, :, :].astype(F32))
+        main, rest = main.reshape(256, 128), rest.reshape(256, 40)
         first, second = slice(x * 168, x * 168 + 128), slice(x * 168 + 128, x * 168 + 168)
-        stream[:, first] = main
-        stream[:, second] = rest
+        full = full + main * main
+        part = part + rest * rest
         normed[:, first] = (main * gain_ref[x : x + 1, 0:128]).astype(BF)
         normed[:, second] = (rest * gain_ref[x : x + 1, 128:168]).astype(BF)
+        own[:, first], own[:, second] = unpacked(x_ref[ids[0] >> 2, x, :, :].astype(F32))
+    squares[...] = full + jnp.concatenate([part, jnp.zeros((256, 88), F32)], axis=1)
     theirs = pl.ds(pl.multiple_of((1 - ids[2]) * 128, 128), 128)
     mine = pl.ds(pl.multiple_of(ids[2] * 128, 128), 128)
-    s = stream[theirs, :]
     o_ref[:, :640], o_ref[:, 640:1280], o_ref[:, 1280:] = gate_up(
-        normed[theirs, :], jnp.sum(s * s, axis=1, keepdims=True), g_ref, u_ref
+        normed[theirs, :], squares[theirs, :], g_ref, u_ref
     )
     normed_ref[...] = normed[mine, :]
-    s = stream[mine, :]
-    squares_ref[...] = jnp.broadcast_to(jnp.sum(s * s, axis=1, keepdims=True), (128, 128))
-    own_ref[...] = stream[pl.ds(pl.multiple_of(ids[0] * 8, 8), 8), :].astype(BF)
+    squares_ref[...] = squares[mine, :]
+    own_ref[...] = own[pl.ds(pl.multiple_of((ids[0] & 3) * 8, 8), 8), :].astype(BF)
 
 
 def own_half_kernel(a_ref, squares_ref, g_ref, u_ref, o_ref):
     o_ref[:, :640], o_ref[:, 640:1280], o_ref[:, 1280:] = gate_up(
-        a_ref[...], squares_ref[:, :1], g_ref, u_ref
+        a_ref[...], squares_ref[...], g_ref, u_ref
     )
 
 
@@ -347,10 +351,10 @@
     ids = jnp.stack([ctx, head, core])
     sent = attend(page_map, selected, ids, norm_gain.reshape(1, 168), queries, keys, values)
     arrived = exchange(sent.reshape(32, 8, 640), CTX)
-    shares, gain = call(
-        merge_kernel, [((NZ * NX, 8, 512), BF), ((NX, 168), F32)], [SMEM, VMEM], ids, arrived
-    )
-    attention = exchange(shares, CTX).reshape(256, 512)
+    share, gain = call(
+        merge_kernel, [((8, 512), BF), ((NX, 168), F32)], [SMEM, VMEM], ids, arrived
+    )
+    attention = exchange(jnp.broadcast_to(share, (NZ * NX, 8, 512)), CTX).reshape(256, 512)
     partial = call(project_kernel, [((NZ, 48, 128), BF)], [VMEM, VMEM], attention, out_weight.T)
     projected = exchange(partial, HEADS)
     stream = call(stream_kernel, [((48, 128), BF)], [VMEM, VMEM], projected, residual_in)
@@ -370,7 +374,7 @@
         gain,
         gate_weight,
         up_weight,
-        scratch=[pltpu.VMEM((256, 672), F32), pltpu.VMEM((256, 672), BF)],
+        scratch=[pltpu.VMEM((32, 672), F32), pltpu.VMEM((256, 128), F32), pltpu.VMEM((256, 672), BF)],
     )
     received = lax.ppermute(other, "core", [(0, 1), (1, 0)])
     mine = call(own_half_kernel, [half], [VMEM] * 4, normed, squares, gate_weight, up_weight)

time: 134 us -> 134 us (level)
  no operation moved by 1% of the time
where the time goes in v7:
time: 134 us
  blocking collectives  119 us (89%)
  Pallas kernels  8.55 us (6%)
  waiting for transfers between devices  3.74 us (3%)
  starting transfers between devices  2.43 us (2%)
    all_to_all x7, blocking collectives, exchange(): return lax.all_to_all(parts, axis, split_axis=0, concat_axis=0, tiled=True)  119 us
    pallas_call x9, Pallas kernels, call(): pl.pallas_call(kernel, out_shape=outs, in_specs=specs, out_specs=[VMEM] *...  4.83 us
    pallas_call x1, Pallas kernels, attend(): pl.pallas_call(attend_kernel, out_shape=jax.ShapeDtypeStruct((256, 640),...  3.72 us
  transfers between devices with their start and end apart: 2, of which 2 were waited for; matrix products, arithmetic and copies ran while one was open for 0% of the time, Pallas kernels for 0%

profile of v7, /device:TPU:32, one launch (start us, length us, event | category | flops | bytes accessed | tf_op | source)
XLA Modules:
  0.0 134.2 jit_solution(15287444665916315459)
XLA Ops:
  0.0 0.1 pad_add_fusion.ids
  0.1 0.0 copy-start.3
  0.1 3.7 %attend.1 = bf16[256,640]{1,0:T(8,128)(2,1)S(1)} custom-call(s32[64]{0:T(128)} %pm_hbm.1, s32[2,8]{1,0:T(2,128)} %sel_hbm.1, s32[3]{0:T(128)S(1)} %pad_add_fusion.ids, f32[1,168]{1,0:T(1,128)} %bitcast.16, bf16[256,512]{1,0:T(8,128)(2,1)} %q_hbm.1, bf16[2,2048,256]{2,1,0:T(8,128)(2,1)} %k_hbm.1, bf16[2,2048,256]{2,1,0:T(8,128)(2,1)} %v_hbm.1), custom_call_target="tpu_custom_call" | custom-call | flops 4000000000 | bytes 10485760 | tf_op jit(solution)/shard_map/attend/pallas_call | solution.py:171
  3.8 0.0 copy-start.4
  3.8 0.0 copy-start
  3.8 0.0 copy-start.1
  3.8 27.3 %all_to_all.35.x_ref = bf16[32,8,640]{2,1,0:T(8,128)(2,1)S(1)} all-to-all(bf16[32,8,640]{2,1,0:T(8,128)(2,1)S(1)} %bitcast.14), channel_id=1, replica_groups=mesh['z'=8,'x'=4,'y'=4,'core'=2] {'z','x'}, dimensions={0} | all-to-all | bytes 655360 | tf_op jit(solution)/shard_map/all_to_all | solution.py:338
  31.1 0.9 merge_kernel.1
  32.0 16.0 %all_to_all.36 = bf16[32,8,512]{2,1,0:T(8,128)(2,1)S(1)} all-to-all(bf16[32,8,512]{2,1,0:T(8,128)(2,1)S(1)} %broadcast_in_dim.6), channel_id=1, replica_groups=mesh['z'=8,'x'=4,'y'=4,'core'=2] {'z','x'}, dimensions={0} | all-to-all | bytes 524288 | tf_op jit(solution)/shard_map/all_to_all | solution.py:338
  48.0 0.0 copy-done.3
  48.0 0.3 project_kernel.1
  48.3 10.1 %all_to_all.37.x_ref = bf16[8,48,128]{2,1,0:T(8,128)(2,1)S(1)} all-to-all(bf16[8,48,128]{2,1,0:T(8,128)(2,1)S(1)} %project_kernel.1), channel_id=1, replica_groups=mesh['z'=8,'x'=4,'y'=4,'core'=2] {'y','core'}, dimensions={0} | all-to-all | bytes 196608 | tf_op jit(solution)/shard_map/all_to_all | solution.py:338
  58.4 0.0 copy-done.4
  58.4 0.1 stream_kernel.1
  58.5 2.3 %collective-permute-start = (bf16[48,128]{1,0:T(8,128)(2,1)S(1)}, bf16[48,128]{1,0:T(8,128)(2,1)S(1)}, u32[]{:S(2)}, u32[]{:S(2)}) collective-permute-start(bf16[48,128]{1,0:T(8,128)(2,1)S(1)} %stream_kernel.1), channel_id=1, source_target_pairs={{0,0},{1,32},{2,64},{3,96},{4,128},{5,160},{6,192},{7,224},{8,8},{... | collective-permute-start | bytes 36872 | tf_op jit(solution)/shard_map/ppermute | solution.py:361
  60.8 2.7 %collective-permute-done = bf16[48,128]{1,0:T(8,128)(2,1)S(1)} collective-permute-done((bf16[48,128]{1,0:T(8,128)(2,1)S(1)}, bf16[48,128]{1,0:T(8,128)(2,1)S(1)}, u32[]{:S(2)}, u32[]{:S(2)}) %collective-permute-start) | collective-permute-done | bytes 12320 | tf_op jit(solution)/shard_map/ppermute | solution.py:361
  63.5 0.1 broadcast_in_dim.7
  63.5 24.6 %all_to_all.38 = bf16[32,48,128]{2,1,0:T(8,128)(2,1)S(1)} all-to-all(bf16[32,48,128]{2,1,0:T(8,128)(2,1)S(1)} %broadcast_in_dim.7), channel_id=1, replica_groups=mesh['z'=8,'x'=4,'y'=4,'core'=2] {'z','x'}, dimensions={0} | all-to-all | bytes 786432 | tf_op jit(solution)/shard_map/all_to_all | solution.py:338
  88.1 0.0 copy-done
  88.1 0.0 copy-done.1
  88.1 1.4 %other_half_kernel.1 = (bf16[128,1408]{1,0:T(8,128)(2,1)S(1)}, bf16[128,672]{1,0:T(8,128)(2,1)S(1)}, f32[128,128]{1,0:T(8,128)S(1)}, bf16[8,672]{1,0:T(8,128)(2,1)S(1)}) custom-call(s32[3]{0:T(128)S(1)} %pad_add_fusion.ids, bf16[8,4,48,128]{3,2,1,0:T(8,128)(2,1)S(1)} %bitcast.11, f32[4,168]{1,0:T(4,128)S(1)} %get-tuple-element.12.gain_ref, ...), custom_call_target="tpu_custom_call" | custom-call | tf_op jit(solution)/shard_map/other_half_kernel/pallas_call | solution.py:325
  89.6 0.1 collective-permute-start.1
  89.7 0.6 own_half_kernel.1.a_ref
  90.2 0.0 copy-start.2
  90.3 1.1 collective-permute-done.1.b_ref
  91.3 0.2 pair_kernel.1
  91.6 10.7 %all_to_all.39.x_ref = bf16[4,32,1408]{2,1,0:T(8,128)(2,1)S(1)} all-to-all(bf16[4,32,1408]{2,1,0:T(8,128)(2,1)S(1)} %bitcast.12), channel_id=1, replica_groups=mesh['z'=8,'x'=4,'y'=4,'core'=2] {'y'}, dimensions={0} | all-to-all | bytes 720896 | tf_op jit(solution)/shard_map/all_to_all | solution.py:338
  102.3 0.2 hidden_kernel.1
  102.5 11.3 %all_to_all.40.a_ref = bf16[8,32,672]{2,1,0:T(8,128)(2,1)S(1)} all-to-all(bf16[8,32,672]{2,1,0:T(8,128)(2,1)S(1)} %hidden_kernel.1), channel_id=1, replica_groups=mesh['z'=8,'x'=4,'y'=4,'core'=2] {'y','core'}, dimensions={0} | all-to-all | bytes 688128 | tf_op jit(solution)/shard_map/all_to_all | solution.py:338
  113.8 0.0 copy-done.2
  113.8 0.5 down_kernel.1
  114.3 19.2 %all_to_all.41.x_ref = bf16[32,8,672]{2,1,0:T(8,128)(2,1)S(1)} all-to-all(bf16[32,8,672]{2,1,0:T(8,128)(2,1)S(1)} %bitcast.10), channel_id=1, replica_groups=mesh['z'=8,'x'=4,'y'=4,'core'=2] {'z','x'}, dimensions={0} | all-to-all | bytes 688128 | tf_op jit(solution)/shard_map/all_to_all | solution.py:338
  133.5 0.7 final_kernel.1
  (1 shorter events, 0.0 us)
Async XLA Ops:
  0.1 47.9 %copy-start.3 = (bf16[512,168]{0,1:T(8,128)(2,1)S(1)}, bf16[512,168]{0,1:T(8,128)(2,1)}, u32[]{:S(2)}) copy-start(bf16[512,168]{0,1:T(8,128)(2,1)} %param.17) | copy-start | bytes 516100
  3.8 54.6 %copy-start.4 = (bf16[32,168]{1,0:T(8,128)(2,1)S(1)}, bf16[32,168]{1,0:T(8,128)(2,1)}, u32[]{:S(2)}) copy-start(bf16[32,168]{1,0:T(8,128)(2,1)} %r_ref.1) | copy-start | bytes 32260
  3.8 84.3 %copy-start = (bf16[672,672]{1,0:T(8,128)(2,1)S(1)}, bf16[672,672]{1,0:T(8,128)(2,1)}, u32[]{:S(2)}) copy-start(bf16[672,672]{1,0:T(8,128)(2,1)} %g_ref.3) | copy-start | bytes 2709508
  3.8 84.3 %copy-start.1 = (bf16[672,672]{1,0:T(8,128)(2,1)S(1)}, bf16[672,672]{1,0:T(8,128)(2,1)}, u32[]{:S(2)}) copy-start(bf16[672,672]{1,0:T(8,128)(2,1)} %u_ref.3) | copy-start | bytes 2709508
  58.5 5.0 %collective-permute-start = (bf16[48,128]{1,0:T(8,128)(2,1)S(1)}, bf16[48,128]{1,0:T(8,128)(2,1)S(1)}, u32[]{:S(2)}, u32[]{:S(2)}) collective-permute-start(bf16[48,128]{1,0:T(8,128)(2,1)S(1)} %stream_kernel.1), channel_id=1, source_target_pairs={{0,0},{1,32},{2,64},{3,96},{4,128},{5,160},{6,192},{7,224},{8,8},{... | collective-permute-start | bytes 36872 | tf_op jit(solution)/shard_map/ppermute | solution.py:361
  89.6 1.8 %collective-permute-start.1 = (bf16[128,1408]{1,0:T(8,128)(2,1)S(1)}, bf16[128,1408]{1,0:T(8,128)(2,1)S(1)}, u32[]{:S(2)}, u32[]{:S(2)}) collective-permute-start(bf16[128,1408]{1,0:T(8,128)(2,1)S(1)} %get-tuple-element.15), channel_id=1, source_target_pairs={{0,1},{1,0},{2,3},{3,2},{4,5},{5,4},{6,7},{7,6},{8,9},{9,8},{10,11... | collective-permute-start | bytes 1081352 | tf_op jit(solution)/shard_map/ppermute | solution.py:379
  90.2 23.6 %copy-start.2 = (bf16[672,672]{1,0:T(8,128)(2,1)S(1)}, bf16[672,672]{1,0:T(8,128)(2,1)}, u32[]{:S(2)}) copy-start(bf16[672,672]{1,0:T(8,128)(2,1)} %w_ref.1) | copy-start | bytes 2709508

commit v8 on v7

--- a/solution.py
+++ b/solution.py
@@ -23,7 +23,6 @@
 NZ, NX, NY, NC = 8, 4, 4, 2
 
 VMEM = pl.BlockSpec(memory_space=pltpu.VMEM)
-SMEM = pl.BlockSpec(memory_space=pltpu.SMEM)
 HBM = pl.BlockSpec(memory_space=pltpu.HBM)
 
 
@@ -35,7 +34,7 @@
 
 
 def attend_kernel(
-    pm_hbm, sel_hbm, ids, gain_hbm, q_hbm, k_hbm, v_hbm, o_ref,
+    pm_hbm, sel_hbm, gain_hbm, q_hbm, k_hbm, v_hbm, o_ref,
     pm, sel, gain_ref, q_ref, kbuf, vbuf, sems, ksem, vsem, flags, m_ref, l_ref, acc_ref,
 ):
     tables = (
@@ -63,9 +62,11 @@
     for c in tables:
         c.wait()
 
+    first_slot = (lax.axis_index("z") * NX + lax.axis_index("x")) * 2
+
     def look(n, carry):
         logical = sel[n >> 3, n & 7]
-        p = pm[logical] - ids[0] * 2
+        p = pm[logical] - first_slot
 
         @pl.when((p == 0) | (p == 1))
         def _():
@@ -167,11 +168,11 @@
     return pltpu.with_memory_space_constraint(array, pltpu.HBM)
 
 
-def attend(page_map, selected, ids, gain, queries, keys, values):
+def attend(page_map, selected, gain, queries, keys, values):
     return pl.pallas_call(
         attend_kernel,
         out_shape=jax.ShapeDtypeStruct((256, 640), BF),
-        in_specs=[HBM, HBM, SMEM, HBM, HBM, HBM, HBM],
+        in_specs=[HBM] * 6,
         out_specs=VMEM,
         scratch_shapes=[
             pltpu.SMEM((64,), jnp.int32),
@@ -193,24 +194,21 @@
             flops=4 * 10**9, transcendentals=4 * 10**6, bytes_accessed=10 * 2**20
         ),
         name="attend",
-    )(in_hbm(page_map), in_hbm(selected), ids, in_hbm(gain), in_hbm(queries), in_hbm(keys), in_hbm(values))
-
-
-def merge_kernel(ids, x_ref, o_ref, gain_ref):
-    x = x_ref[...].astype(F32)
-    marks = x[:, :, 512:640].reshape(256, 128).astype(BF)
-    source = lax.broadcasted_iota(jnp.int32, (128, 512), 0)
-    target = lax.broadcasted_iota(jnp.int32, (128, 512), 1)
-    spread = jnp.where((source < 12) & ((source & 3) == target // 128), 1.0, 0.0).astype(BF)
-    level = jnp.dot(marks, spread, preferred_element_type=F32).reshape(32, 8, 512)
-    top = jnp.max(level, axis=0, keepdims=True)
-    weight = jnp.exp2(level - top)
-    total = jnp.sum(weight, axis=0)
-    mixed = jnp.sum(weight * x[:, :, :512], axis=0)
-    share = (mixed / total).astype(BF)
-    o_ref[...] = share
+    )(in_hbm(page_map), in_hbm(selected), in_hbm(gain), in_hbm(queries), in_hbm(keys), in_hbm(values))
+
+
+def merge_kernel(x_ref, o_ref, gain_ref):
+    marks = x_ref[:, :, 512:640].astype(F32).reshape(256, 128).astype(BF)
+    source = lax.broadcasted_iota(jnp.int32, (128, 128), 0)
+    for h in range(4):
+        spread = jnp.where((source < 12) & ((source & 3) == h), 1.0, 0.0).astype(BF)
+        level = jnp.dot(marks, spread, preferred_element_type=F32).reshape(32, 8, 128)
+        weight = jnp.exp2(level - jnp.max(level, axis=0, keepdims=True))
+        mixed = jnp.sum(weight * x_ref[:, :, h * 128 : (h + 1) * 128].astype(F32), axis=0)
+        o_ref[:, h * 128 : (h + 1) * 128] = (mixed / jnp.sum(weight, axis=0)).astype(BF)
+    head = lax.axis_index("y") * NC + lax.axis_index("core")
     for k in range(NX):
-        gain = x_ref[ids[1] * NX + k, :, 512:640].astype(F32)
+        gain = x_ref[head * NX + k, :, 512:640].astype(F32)
         for half in range(2):
             gain_ref[k : k + 1, half * 84 : half * 84 + 84] = (
                 gain[half : half + 1, 16:100]
@@ -260,8 +258,9 @@
 
 
 def other_half_kernel(
-    ids, x_ref, gain_ref, g_ref, u_ref, o_ref, normed_ref, squares_ref, own_ref, own, squares, normed
+    x_ref, gain_ref, g_ref, u_ref, o_ref, normed_ref, squares_ref, own_ref, own, squares, normed
 ):
+    core = lax.axis_index("core")
     full = jnp.zeros((256, 128), F32)
     part = jnp.zeros((256, 40), F32)
     for x in range(NX):
@@ -272,16 +271,16 @@
         part = part + rest * rest
         normed[:, first] = (main * gain_ref[x : x + 1, 0:128]).astype(BF)
         normed[:, second] = (rest * gain_ref[x : x + 1, 128:168]).astype(BF)
-        own[:, first], own[:, second] = unpacked(x_ref[ids[0] >> 2, x, :, :].astype(F32))
+        own[:, first], own[:, second] = unpacked(x_ref[lax.axis_index("z"), x, :, :].astype(F32))
     squares[...] = full + jnp.concatenate([part, jnp.zeros((256, 88), F32)], axis=1)
-    theirs = pl.ds(pl.multiple_of((1 - ids[2]) * 128, 128), 128)
-    mine = pl.ds(pl.multiple_of(ids[2] * 128, 128), 128)
+    theirs = pl.ds(pl.multiple_of((1 - core) * 128, 128), 128)
+    mine = pl.ds(pl.multiple_of(core * 128, 128), 128)
     o_ref[:, :640], o_ref[:, 640:1280], o_ref[:, 1280:] = gate_up(
         normed[theirs, :], squares[theirs, :], g_ref, u_ref
     )
     normed_ref[...] = normed[mine, :]
     squares_ref[...] = squares[mine, :]
-    own_ref[...] = own[pl.ds(pl.multiple_of((ids[0] & 3) * 8, 8), 8), :].astype(BF)
+    own_ref[...] = own[pl.ds(pl.multiple_of(lax.axis_index("x") * 8, 8), 8), :].astype(BF)
 
 
 def own_half_kernel(a_ref, squares_ref, g_ref, u_ref, o_ref):
@@ -345,14 +344,10 @@
 def shards(
     queries, keys, values, page_map, selected, residual_in, out_weight, norm_gain, gate_weight, up_weight, down_weight
 ):
-    ctx = (lax.axis_index("z") * NX + lax.axis_index("x")).astype(jnp.int32)
-    core = lax.axis_index("core").astype(jnp.int32)
-    head = lax.axis_index("y").astype(jnp.int32) * NC + core
-    ids = jnp.stack([ctx, head, core])
-    sent = attend(page_map, selected, ids, norm_gain.reshape(1, 168), queries, keys, values)
+    sent = attend(page_map, selected, norm_gain.reshape(1, 168), queries, keys, values)
     arrived = exchange(sent.reshape(32, 8, 640), CTX)
     share, gain = call(
-        merge_kernel, [((8, 512), BF), ((NX, 168), F32)], [SMEM, VMEM], ids, arrived
+        merge_kernel, [((8, 512), BF), ((NX, 168), F32)], [VMEM], arrived
     )
     attention = exchange(jnp.broadcast_to(share, (NZ * NX, 8, 512)), CTX).reshape(256, 512)
     partial = call(project_kernel, [((NZ, 48, 128), BF)], [VMEM, VMEM], attention, out_weight.T)
@@ -368,8 +363,7 @@
     other, normed, squares, own_stream = call(
         other_half_kernel,
         [half, ((128, 672), BF), ((128, 128), F32), ((8, 672), BF)],
-        [SMEM, VMEM, VMEM, VMEM, VMEM],
-        ids,
+        [VMEM, VMEM, VMEM, VMEM],
         rows.reshape(NZ, NX, 48, 128),
         gain,
         gate_weight,

time: 134 us -> 132 us (0.985)
  Pallas kernels: 8.55 us -> 6.87 us
where the time goes in v8:
time: 132 us
  blocking collectives  119 us (90%)
  Pallas kernels  6.87 us (5%)
  waiting for transfers between devices  3.75 us (3%)
  starting transfers between devices  2.43 us (2%)
    all_to_all x7, blocking collectives, exchange(): return lax.all_to_all(parts, axis, split_axis=0, concat_axis=0, tiled=True)  119 us
    pallas_call x9, Pallas kernels, call(): pl.pallas_call(kernel, out_shape=outs, in_specs=specs, out_specs=[VMEM] *...  3.66 us
    pallas_call x1, Pallas kernels, attend(): pl.pallas_call(attend_kernel, out_shape=jax.ShapeDtypeStruct((256, 640),...  3.21 us
    ppermute x1, waiting for transfers between devices, shards(): lax.ppermute(stream, ALL, [(place(z, x, h), place(h, x, z)) for z in rang...  2.66 us
  transfers between devices with their start and end apart: 2, of which 2 were waited for; matrix products, arithmetic and copies ran while one was open for 0% of the time, Pallas kernels for 0%

profile of v8, /device:TPU:32, one launch (start us, length us, event | category | flops | bytes accessed | tf_op | source)
XLA Modules:
  0.0 131.8 jit_solution(15764912181673934798)
XLA Ops:
  0.0 0.0 copy-start.3
  0.0 3.2 %attend.1 = bf16[256,640]{1,0:T(8,128)(2,1)S(1)} custom-call(s32[64]{0:T(128)} %pm_hbm.1, s32[2,8]{1,0:T(2,128)} %sel_hbm.1, f32[1,168]{1,0:T(1,128)} %bitcast.13, bf16[256,512]{1,0:T(8,128)(2,1)} %q_hbm.1, bf16[2,2048,256]{2,1,0:T(8,128)(2,1)} %k_hbm.1, bf16[2,2048,256]{2,1,0:T(8,128)(2,1)} %v_hbm.1), custom_call_target="tpu_custom_call" | custom-call | flops 4000000000 | bytes 10485760 | tf_op jit(solution)/shard_map/attend/pallas_call | solution.py:172
  3.2 0.0 copy-start.4
  3.2 0.0 copy-start
  3.2 0.0 copy-start.1
  3.3 26.7 %all_to_all.35.x_ref = bf16[32,8,640]{2,1,0:T(8,128)(2,1)S(1)} all-to-all(bf16[32,8,640]{2,1,0:T(8,128)(2,1)S(1)} %bitcast.11), channel_id=1, replica_groups=mesh['z'=8,'x'=4,'y'=4,'core'=2] {'z','x'}, dimensions={0} | all-to-all | bytes 655360 | tf_op jit(solution)/shard_map/all_to_all | solution.py:337
  29.9 0.3 merge_kernel.1
  30.2 16.0 %all_to_all.36 = bf16[32,8,512]{2,1,0:T(8,128)(2,1)S(1)} all-to-all(bf16[32,8,512]{2,1,0:T(8,128)(2,1)S(1)} %broadcast_in_dim.6), channel_id=1, replica_groups=mesh['z'=8,'x'=4,'y'=4,'core'=2] {'z','x'}, dimensions={0} | all-to-all | bytes 524288 | tf_op jit(solution)/shard_map/all_to_all | solution.py:337
  46.3 0.0 copy-done.3
  46.3 0.3 project_kernel.1
  46.6 10.1 %all_to_all.37.x_ref = bf16[8,48,128]{2,1,0:T(8,128)(2,1)S(1)} all-to-all(bf16[8,48,128]{2,1,0:T(8,128)(2,1)S(1)} %project_kernel.1), channel_id=1, replica_groups=mesh['z'=8,'x'=4,'y'=4,'core'=2] {'y','core'}, dimensions={0} | all-to-all | bytes 196608 | tf_op jit(solution)/shard_map/all_to_all | solution.py:337
  56.6 0.0 copy-done.4
  56.6 0.1 stream_kernel.1
  56.7 2.3 %collective-permute-start = (bf16[48,128]{1,0:T(8,128)(2,1)S(1)}, bf16[48,128]{1,0:T(8,128)(2,1)S(1)}, u32[]{:S(2)}, u32[]{:S(2)}) collective-permute-start(bf16[48,128]{1,0:T(8,128)(2,1)S(1)} %stream_kernel.1), channel_id=1, source_target_pairs={{0,0},{1,32},{2,64},{3,96},{4,128},{5,160},{6,192},{7,224},{8,8},{... | collective-permute-start | bytes 36872 | tf_op jit(solution)/shard_map/ppermute | solution.py:356
  59.0 2.7 %collective-permute-done = bf16[48,128]{1,0:T(8,128)(2,1)S(1)} collective-permute-done((bf16[48,128]{1,0:T(8,128)(2,1)S(1)}, bf16[48,128]{1,0:T(8,128)(2,1)S(1)}, u32[]{:S(2)}, u32[]{:S(2)}) %collective-permute-start) | collective-permute-done | bytes 12320 | tf_op jit(solution)/shard_map/ppermute | solution.py:356
  61.7 0.1 broadcast_in_dim.7
  61.8 24.6 %all_to_all.38 = bf16[32,48,128]{2,1,0:T(8,128)(2,1)S(1)} all-to-all(bf16[32,48,128]{2,1,0:T(8,128)(2,1)S(1)} %broadcast_in_dim.7), channel_id=1, replica_groups=mesh['z'=8,'x'=4,'y'=4,'core'=2] {'z','x'}, dimensions={0} | all-to-all | bytes 786432 | tf_op jit(solution)/shard_map/all_to_all | solution.py:337
  86.4 0.0 copy-done
  86.4 0.0 copy-done.1
  86.4 0.8 other_half_kernel.1
  87.2 0.1 collective-permute-start.1
  87.3 0.6 own_half_kernel.1.a_ref
  87.9 0.0 copy-start.2
  87.9 1.1 collective-permute-done.1.b_ref
  89.0 0.2 pair_kernel.1
  89.2 10.7 %all_to_all.39.x_ref = bf16[4,32,1408]{2,1,0:T(8,128)(2,1)S(1)} all-to-all(bf16[4,32,1408]{2,1,0:T(8,128)(2,1)S(1)} %bitcast.9), channel_id=1, replica_groups=mesh['z'=8,'x'=4,'y'=4,'core'=2] {'y'}, dimensions={0} | all-to-all | bytes 720896 | tf_op jit(solution)/shard_map/all_to_all | solution.py:337
  99.9 0.2 hidden_kernel.1
  100.1 11.3 %all_to_all.40.a_ref = bf16[8,32,672]{2,1,0:T(8,128)(2,1)S(1)} all-to-all(bf16[8,32,672]{2,1,0:T(8,128)(2,1)S(1)} %hidden_kernel.1), channel_id=1, replica_groups=mesh['z'=8,'x'=4,'y'=4,'core'=2] {'y','core'}, dimensions={0} | all-to-all | bytes 688128 | tf_op jit(solution)/shard_map/all_to_all | solution.py:337
  111.4 0.0 copy-done.2
  111.4 0.5 down_kernel.1
  111.9 19.2 %all_to_all.41.x_ref = bf16[32,8,672]{2,1,0:T(8,128)(2,1)S(1)} all-to-all(bf16[32,8,672]{2,1,0:T(8,128)(2,1)S(1)} %bitcast.8), channel_id=1, replica_groups=mesh['z'=8,'x'=4,'y'=4,'core'=2] {'z','x'}, dimensions={0} | all-to-all | bytes 688128 | tf_op jit(solution)/shard_map/all_to_all | solution.py:337
  131.1 0.7 final_kernel.1
  (1 shorter events, 0.0 us)
Async XLA Ops:
  0.0 46.3 %copy-start.3 = (bf16[512,168]{0,1:T(8,128)(2,1)S(1)}, bf16[512,168]{0,1:T(8,128)(2,1)}, u32[]{:S(2)}) copy-start(bf16[512,168]{0,1:T(8,128)(2,1)} %param.17) | copy-start | bytes 516100
  3.2 53.4 %copy-start.4 = (bf16[32,168]{1,0:T(8,128)(2,1)S(1)}, bf16[32,168]{1,0:T(8,128)(2,1)}, u32[]{:S(2)}) copy-start(bf16[32,168]{1,0:T(8,128)(2,1)} %r_ref.1) | copy-start | bytes 32260
  3.2 83.1 %copy-start = (bf16[672,672]{1,0:T(8,128)(2,1)S(1)}, bf16[672,672]{1,0:T(8,128)(2,1)}, u32[]{:S(2)}) copy-start(bf16[672,672]{1,0:T(8,128)(2,1)} %g_ref.3) | copy-start | bytes 2709508
  3.2 83.1 %copy-start.1 = (bf16[672,672]{1,0:T(8,128)(2,1)S(1)}, bf16[672,672]{1,0:T(8,128)(2,1)}, u32[]{:S(2)}) copy-start(bf16[672,672]{1,0:T(8,128)(2,1)} %u_ref.3) | copy-start | bytes 2709508
  56.7 5.0 %collective-permute-start = (bf16[48,128]{1,0:T(8,128)(2,1)S(1)}, bf16[48,128]{1,0:T(8,128)(2,1)S(1)}, u32[]{:S(2)}, u32[]{:S(2)}) collective-permute-start(bf16[48,128]{1,0:T(8,128)(2,1)S(1)} %stream_kernel.1), channel_id=1, source_target_pairs={{0,0},{1,32},{2,64},{3,96},{4,128},{5,160},{6,192},{7,224},{8,8},{... | collective-permute-start | bytes 36872 | tf_op jit(solution)/shard_map/ppermute | solution.py:356
  87.2 1.8 %collective-permute-start.1 = (bf16[128,1408]{1,0:T(8,128)(2,1)S(1)}, bf16[128,1408]{1,0:T(8,128)(2,1)S(1)}, u32[]{:S(2)}, u32[]{:S(2)}) collective-permute-start(bf16[128,1408]{1,0:T(8,128)(2,1)S(1)} %get-tuple-element.15), channel_id=1, source_target_pairs={{0,1},{1,0},{2,3},{3,2},{4,5},{5,4},{6,7},{7,6},{8,9},{9,8},{10,11... | collective-permute-start | bytes 1081352 | tf_op jit(solution)/shard_map/ppermute | solution.py:373
  87.9 23.6 %copy-start.2 = (bf16[672,672]{1,0:T(8,128)(2,1)S(1)}, bf16[672,672]{1,0:T(8,128)(2,1)}, u32[]{:S(2)}) copy-start(bf16[672,672]{1,0:T(8,128)(2,1)} %w_ref.1) | copy-start | bytes 2709508

commit v9 on v8

--- a/solution.py
+++ b/solution.py
@@ -35,7 +35,7 @@
 
 def attend_kernel(
     pm_hbm, sel_hbm, gain_hbm, q_hbm, k_hbm, v_hbm, o_ref,
-    pm, sel, gain_ref, q_ref, kbuf, vbuf, sems, ksem, vsem, flags, m_ref, l_ref, acc_ref,
+    pm, sel, gain_ref, q_ref, kbuf, vbuf, sems, ksem, vsem, flags, gains_ref, m_ref, l_ref, acc_ref,
 ):
     tables = (
         pltpu.make_async_copy(pm_hbm, pm, sems.at[0]),
@@ -81,6 +81,13 @@
     lax.fori_loop(0, 16, look, 0)
     for c in late:
         c.wait()
+    halves = []
+    for piece in pieces(gain_ref[...]):
+        halves += [piece[:, :84], piece[:, 84:168]]
+    halves += [jnp.zeros((1, 84), F32)] * 2
+    gains_ref[...] = jnp.concatenate(
+        [jnp.zeros((8, 16), F32), jnp.concatenate(halves, axis=0), jnp.zeros((8, 28), F32)], axis=1
+    )
 
     def attend_tile(p, t):
         span = pl.ds(pl.multiple_of(t * 256, 256), 256)
@@ -136,17 +143,9 @@
     lax.fori_loop(0, 2, page, 0)
 
     lane = lax.broadcasted_iota(jnp.int32, (128, 128), 1)
-    halves = []
-    for piece in pieces(gain_ref[...]):
-        halves += [piece[:, :84], piece[:, 84:168]]
-    halves += [jnp.zeros((1, 84), F32)] * 2
-    gains = jnp.concatenate(
-        [jnp.zeros((8, 16), F32), jnp.concatenate(halves, axis=0), jnp.zeros((8, 28), F32)], axis=1
-    )
-    gains = jnp.concatenate([gains] * 16, axis=0)
 
     def finish(t, carry):
-        marks = gains
+        marks = jnp.concatenate([gains_ref[...]] * 16, axis=0)
         out_rows = pl.ds(pl.multiple_of(t * 128, 128), 128)
         for h in range(4):
             kv = h // 2
@@ -185,6 +184,7 @@
             pltpu.SemaphoreType.DMA((2,)),
             pltpu.SemaphoreType.DMA((2,)),
             pltpu.SMEM((8,), jnp.int32),
+            pltpu.VMEM((8, 128), F32),
             pltpu.VMEM((2, 512, 128), F32),
             pltpu.VMEM((2, 512, 128), F32),
             pltpu.VMEM((2, 512, 128), F32),

time: 132 us -> 133 us (level)
  no operation moved by 1% of the time
where the time goes in v9:
time: 133 us
  blocking collectives  120 us (90%)
  Pallas kernels  6.73 us (5%)
  waiting for transfers between devices  3.75 us (3%)
  starting transfers between devices  2.42 us (2%)
    all_to_all x7, blocking collectives, exchange(): return lax.all_to_all(parts, axis, split_axis=0, concat_axis=0, tiled=True)  120 us
    pallas_call x9, Pallas kernels, call(): pl.pallas_call(kernel, out_shape=outs, in_specs=specs, out_specs=[VMEM] *...  3.67 us
    pallas_call x1, Pallas kernels, attend(): pl.pallas_call(attend_kernel, out_shape=jax.ShapeDtypeStruct((256, 640),...  3.05 us
    ppermute x1, waiting for transfers between devices, shards(): lax.ppermute(stream, ALL, [(place(z, x, h), place(h, x, z)) for z in rang...  2.67 us
  transfers between devices with their start and end apart: 2, of which 2 were waited for; matrix products, arithmetic and copies ran while one was open for 0% of the time, Pallas kernels for 0%

profile of v9, /device:TPU:32, one launch (start us, length us, event | category | flops | bytes accessed | tf_op | source)
XLA Modules:
  0.0 132.7 jit_solution(10102488647181663567)
XLA Ops:
  0.0 0.0 copy-start.3
  0.0 3.1 %attend.1 = bf16[256,640]{1,0:T(8,128)(2,1)S(1)} custom-call(s32[64]{0:T(128)} %pm_hbm.1, s32[2,8]{1,0:T(2,128)} %sel_hbm.1, f32[1,168]{1,0:T(1,128)} %bitcast.13, bf16[256,512]{1,0:T(8,128)(2,1)} %q_hbm.1, bf16[2,2048,256]{2,1,0:T(8,128)(2,1)} %k_hbm.1, bf16[2,2048,256]{2,1,0:T(8,128)(2,1)} %v_hbm.1), custom_call_target="tpu_custom_call" | custom-call | flops 4000000000 | bytes 10485760 | tf_op jit(solution)/shard_map/attend/pallas_call | solution.py:171
  3.1 0.0 copy-start.4
  3.1 0.0 copy-start
  3.1 0.0 copy-start.1
  3.1 27.7 %all_to_all.35.x_ref = bf16[32,8,640]{2,1,0:T(8,128)(2,1)S(1)} all-to-all(bf16[32,8,640]{2,1,0:T(8,128)(2,1)S(1)} %bitcast.11), channel_id=1, replica_groups=mesh['z'=8,'x'=4,'y'=4,'core'=2] {'z','x'}, dimensions={0} | all-to-all | bytes 655360 | tf_op jit(solution)/shard_map/all_to_all | solution.py:337
  30.8 0.3 merge_kernel.1
  31.1 16.0 %all_to_all.36 = bf16[32,8,512]{2,1,0:T(8,128)(2,1)S(1)} all-to-all(bf16[32,8,512]{2,1,0:T(8,128)(2,1)S(1)} %broadcast_in_dim.6), channel_id=1, replica_groups=mesh['z'=8,'x'=4,'y'=4,'core'=2] {'z','x'}, dimensions={0} | all-to-all | bytes 524288 | tf_op jit(solution)/shard_map/all_to_all | solution.py:337
  47.1 0.0 copy-done.3
  47.1 0.3 project_kernel.1
  47.4 10.0 %all_to_all.37.x_ref = bf16[8,48,128]{2,1,0:T(8,128)(2,1)S(1)} all-to-all(bf16[8,48,128]{2,1,0:T(8,128)(2,1)S(1)} %project_kernel.1), channel_id=1, replica_groups=mesh['z'=8,'x'=4,'y'=4,'core'=2] {'y','core'}, dimensions={0} | all-to-all | bytes 196608 | tf_op jit(solution)/shard_map/all_to_all | solution.py:337
  57.5 0.0 copy-done.4
  57.5 0.1 stream_kernel.1
  57.6 2.3 %collective-permute-start = (bf16[48,128]{1,0:T(8,128)(2,1)S(1)}, bf16[48,128]{1,0:T(8,128)(2,1)S(1)}, u32[]{:S(2)}, u32[]{:S(2)}) collective-permute-start(bf16[48,128]{1,0:T(8,128)(2,1)S(1)} %stream_kernel.1), channel_id=1, source_target_pairs={{0,0},{1,32},{2,64},{3,96},{4,128},{5,160},{6,192},{7,224},{8,8},{... | collective-permute-start | bytes 36872 | tf_op jit(solution)/shard_map/ppermute | solution.py:356
  59.9 2.7 %collective-permute-done = bf16[48,128]{1,0:T(8,128)(2,1)S(1)} collective-permute-done((bf16[48,128]{1,0:T(8,128)(2,1)S(1)}, bf16[48,128]{1,0:T(8,128)(2,1)S(1)}, u32[]{:S(2)}, u32[]{:S(2)}) %collective-permute-start) | collective-permute-done | bytes 12320 | tf_op jit(solution)/shard_map/ppermute | solution.py:356
  62.6 0.1 broadcast_in_dim.7
  62.6 24.6 %all_to_all.38 = bf16[32,48,128]{2,1,0:T(8,128)(2,1)S(1)} all-to-all(bf16[32,48,128]{2,1,0:T(8,128)(2,1)S(1)} %broadcast_in_dim.7), channel_id=1, replica_groups=mesh['z'=8,'x'=4,'y'=4,'core'=2] {'z','x'}, dimensions={0} | all-to-all | bytes 786432 | tf_op jit(solution)/shard_map/all_to_all | solution.py:337
  87.2 0.0 copy-done
  87.2 0.0 copy-done.1
  87.2 0.8 other_half_kernel.1
  88.1 0.1 collective-permute-start.1
  88.2 0.6 own_half_kernel.1.a_ref
  88.7 0.0 copy-start.2
  88.8 1.1 collective-permute-done.1.b_ref
  89.8 0.2 pair_kernel.1
  90.1 10.7 %all_to_all.39.x_ref = bf16[4,32,1408]{2,1,0:T(8,128)(2,1)S(1)} all-to-all(bf16[4,32,1408]{2,1,0:T(8,128)(2,1)S(1)} %bitcast.9), channel_id=1, replica_groups=mesh['z'=8,'x'=4,'y'=4,'core'=2] {'y'}, dimensions={0} | all-to-all | bytes 720896 | tf_op jit(solution)/shard_map/all_to_all | solution.py:337
  100.8 0.2 hidden_kernel.1
  101.0 11.3 %all_to_all.40.a_ref = bf16[8,32,672]{2,1,0:T(8,128)(2,1)S(1)} all-to-all(bf16[8,32,672]{2,1,0:T(8,128)(2,1)S(1)} %hidden_kernel.1), channel_id=1, replica_groups=mesh['z'=8,'x'=4,'y'=4,'core'=2] {'y','core'}, dimensions={0} | all-to-all | bytes 688128 | tf_op jit(solution)/shard_map/all_to_all | solution.py:337
  112.3 0.0 copy-done.2
  112.3 0.5 down_kernel.1
  112.8 19.2 %all_to_all.41.x_ref = bf16[32,8,672]{2,1,0:T(8,128)(2,1)S(1)} all-to-all(bf16[32,8,672]{2,1,0:T(8,128)(2,1)S(1)} %bitcast.8), channel_id=1, replica_groups=mesh['z'=8,'x'=4,'y'=4,'core'=2] {'z','x'}, dimensions={0} | all-to-all | bytes 688128 | tf_op jit(solution)/shard_map/all_to_all | solution.py:337
  132.0 0.7 final_kernel.1
  (1 shorter events, 0.0 us)
Async XLA Ops:
  0.0 47.1 %copy-start.3 = (bf16[512,168]{0,1:T(8,128)(2,1)S(1)}, bf16[512,168]{0,1:T(8,128)(2,1)}, u32[]{:S(2)}) copy-start(bf16[512,168]{0,1:T(8,128)(2,1)} %param.17) | copy-start | bytes 516100
  3.1 54.4 %copy-start.4 = (bf16[32,168]{1,0:T(8,128)(2,1)S(1)}, bf16[32,168]{1,0:T(8,128)(2,1)}, u32[]{:S(2)}) copy-start(bf16[32,168]{1,0:T(8,128)(2,1)} %r_ref.1) | copy-start | bytes 32260
  3.1 84.2 %copy-start = (bf16[672,672]{1,0:T(8,128)(2,1)S(1)}, bf16[672,672]{1,0:T(8,128)(2,1)}, u32[]{:S(2)}) copy-start(bf16[672,672]{1,0:T(8,128)(2,1)} %g_ref.3) | copy-start | bytes 2709508
  3.1 84.1 %copy-start.1 = (bf16[672,672]{1,0:T(8,128)(2,1)S(1)}, bf16[672,672]{1,0:T(8,128)(2,1)}, u32[]{:S(2)}) copy-start(bf16[672,672]{1,0:T(8,128)(2,1)} %u_ref.3) | copy-start | bytes 2709508
  57.6 5.0 %collective-permute-start = (bf16[48,128]{1,0:T(8,128)(2,1)S(1)}, bf16[48,128]{1,0:T(8,128)(2,1)S(1)}, u32[]{:S(2)}, u32[]{:S(2)}) collective-permute-start(bf16[48,128]{1,0:T(8,128)(2,1)S(1)} %stream_kernel.1), channel_id=1, source_target_pairs={{0,0},{1,32},{2,64},{3,96},{4,128},{5,160},{6,192},{7,224},{8,8},{... | collective-permute-start | bytes 36872 | tf_op jit(solution)/shard_map/ppermute | solution.py:356
  88.1 1.8 %collective-permute-start.1 = (bf16[128,1408]{1,0:T(8,128)(2,1)S(1)}, bf16[128,1408]{1,0:T(8,128)(2,1)S(1)}, u32[]{:S(2)}, u32[]{:S(2)}) collective-permute-start(bf16[128,1408]{1,0:T(8,128)(2,1)S(1)} %get-tuple-element.15), channel_id=1, source_target_pairs={{0,1},{1,0},{2,3},{3,2},{4,5},{5,4},{6,7},{7,6},{8,9},{9,8},{10,11... | collective-permute-start | bytes 1081352 | tf_op jit(solution)/shard_map/ppermute | solution.py:373
  88.7 23.6 %copy-start.2 = (bf16[672,672]{1,0:T(8,128)(2,1)S(1)}, bf16[672,672]{1,0:T(8,128)(2,1)}, u32[]{:S(2)}) copy-start(bf16[672,672]{1,0:T(8,128)(2,1)} %w_ref.1) | copy-start | bytes 2709508

commit v10 on v9

--- a/solution.py
+++ b/solution.py
@@ -305,14 +305,28 @@
     factor = lax.rsqrt(squares / D + EPSILON)
     gate = jnp.concatenate([both[:, :640], both[:, 1280:1312]], axis=1) * factor
     up = jnp.concatenate([both[:, 640:1280], both[:, 1312:1344]], axis=1) * factor
-    hidden = (jax.nn.gelu(gate, approximate=True) * up).astype(BF)
+    hidden = jax.nn.gelu(gate, approximate=True) * up
+    tail = jnp.concatenate([hidden[g * 8 : (g + 1) * 8, 640:] for g in range(4)], axis=1)
+    blocks = [hidden[:, j * 128 : (j + 1) * 128] for j in range(5)]
+    rows = jnp.concatenate(blocks + [tail], axis=0).astype(BF)
     for k in range(NY * NC):
-        o_ref[k] = hidden
+        o_ref[k] = rows
 
 
 def down_kernel(a_ref, w_ref, o_ref):
-    a = jnp.concatenate([a_ref[y * NC + c] for c in range(NC) for y in range(NY)], axis=0)
-    o_ref[...] = jnp.dot(a, w_ref[...], preferred_element_type=F32).astype(BF)
+    mains, tails = [], []
+    for c in range(NC):
+        for y in range(NY):
+            rows = a_ref[y * NC + c].astype(F32)
+            mains.append(
+                jnp.concatenate([rows[j * 32 : (j + 1) * 32] for j in range(5)], axis=1).astype(BF)
+            )
+            tails += [rows[160:, g * 32 : (g + 1) * 32] for g in range(4)]
+    main = jnp.concatenate(mains, axis=0)
+    tail = jnp.concatenate(tails, axis=0).astype(BF)
+    total = jnp.dot(main, w_ref[:640, :], preferred_element_type=F32)
+    total = total + jnp.dot(tail, w_ref[640:, :], preferred_element_type=F32)
+    o_ref[...] = total.astype(BF)
 
 
 def final_kernel(x_ref, s_ref, o_ref):
@@ -374,7 +388,7 @@
     mine = call(own_half_kernel, [half], [VMEM] * 4, normed, squares, gate_weight, up_weight)
     pair = call(pair_kernel, [half], [VMEM, VMEM], mine, received)
     shared = exchange(pair.reshape(NY, 32, 1408), "y")
-    hidden = exchange(call(hidden_kernel, [((NY * NC, 32, 672), BF)], [VMEM], shared), HEADS)
+    hidden = exchange(call(hidden_kernel, [((NY * NC, 168, 128), BF)], [VMEM], shared), HEADS)
     down = call(
         down_kernel, [((256, 672), BF)], [VMEM, VMEM], hidden, down_weight
     )

time: 133 us -> 131 us (0.985)
  blocking collectives: 120 us -> 117 us
    all_to_all x7, blocking collectives: 120 us -> 117 us  [exchange(): return lax.all_to_all(parts, axis, split_axis=0, concat_axis=0, tiled=True)]
where the time goes in v10:
time: 131 us
  blocking collectives  117 us (89%)
  Pallas kernels  7.84 us (6%)
  waiting for transfers between devices  3.75 us (3%)
  starting transfers between devices  2.43 us (2%)
    all_to_all x7, blocking collectives, exchange(): return lax.all_to_all(parts, axis, split_axis=0, concat_axis=0, tiled=True)  117 us
    pallas_call x1, Pallas kernels, attend(): pl.pallas_call(attend_kernel, out_shape=jax.ShapeDtypeStruct((256, 640),...  4.01 us
    pallas_call x9, Pallas kernels, call(): pl.pallas_call(kernel, out_shape=outs, in_specs=specs, out_specs=[VMEM] *...  3.83 us
    ppermute x1, waiting for transfers between devices, shards(): lax.ppermute(stream, ALL, [(place(z, x, h), place(h, x, z)) for z in rang...  2.66 us
  transfers between devices with their start and end apart: 2, of which 2 were waited for; matrix products, arithmetic and copies ran while one was open for 0% of the time, Pallas kernels for 0%

profile of v10, /device:TPU:32, one launch (start us, length us, event | category | flops | bytes accessed | tf_op | source)
XLA Modules:
  0.0 131.5 jit_solution(3585546514942735410)
XLA Ops:
  0.0 0.0 copy-start.3
  0.0 4.0 %attend.1 = bf16[256,640]{1,0:T(8,128)(2,1)S(1)} custom-call(s32[64]{0:T(128)} %pm_hbm.1, s32[2,8]{1,0:T(2,128)} %sel_hbm.1, f32[1,168]{1,0:T(1,128)} %bitcast.13, bf16[256,512]{1,0:T(8,128)(2,1)} %q_hbm.1, bf16[2,2048,256]{2,1,0:T(8,128)(2,1)} %k_hbm.1, bf16[2,2048,256]{2,1,0:T(8,128)(2,1)} %v_hbm.1), custom_call_target="tpu_custom_call" | custom-call | flops 4000000000 | bytes 10485760 | tf_op jit(solution)/shard_map/attend/pallas_call | solution.py:171
  4.0 0.0 copy-start.4
  4.0 0.0 copy-start
  4.0 0.0 copy-start.1
  4.1 25.8 %all_to_all.35.x_ref = bf16[32,8,640]{2,1,0:T(8,128)(2,1)S(1)} all-to-all(bf16[32,8,640]{2,1,0:T(8,128)(2,1)S(1)} %bitcast.11), channel_id=1, replica_groups=mesh['z'=8,'x'=4,'y'=4,'core'=2] {'z','x'}, dimensions={0} | all-to-all | bytes 655360 | tf_op jit(solution)/shard_map/all_to_all | solution.py:351
  29.9 0.3 merge_kernel.1
  30.2 16.0 %all_to_all.36 = bf16[32,8,512]{2,1,0:T(8,128)(2,1)S(1)} all-to-all(bf16[32,8,512]{2,1,0:T(8,128)(2,1)S(1)} %broadcast_in_dim.6), channel_id=1, replica_groups=mesh['z'=8,'x'=4,'y'=4,'core'=2] {'z','x'}, dimensions={0} | all-to-all | bytes 524288 | tf_op jit(solution)/shard_map/all_to_all | solution.py:351
  46.2 0.0 copy-done.3
  46.2 0.3 project_kernel.1
  46.5 10.1 %all_to_all.37.x_ref = bf16[8,48,128]{2,1,0:T(8,128)(2,1)S(1)} all-to-all(bf16[8,48,128]{2,1,0:T(8,128)(2,1)S(1)} %project_kernel.1), channel_id=1, replica_groups=mesh['z'=8,'x'=4,'y'=4,'core'=2] {'y','core'}, dimensions={0} | all-to-all | bytes 196608 | tf_op jit(solution)/shard_map/all_to_all | solution.py:351
  56.6 0.0 copy-done.4
  56.6 0.1 stream_kernel.1
  56.7 2.3 %collective-permute-start = (bf16[48,128]{1,0:T(8,128)(2,1)S(1)}, bf16[48,128]{1,0:T(8,128)(2,1)S(1)}, u32[]{:S(2)}, u32[]{:S(2)}) collective-permute-start(bf16[48,128]{1,0:T(8,128)(2,1)S(1)} %stream_kernel.1), channel_id=1, source_target_pairs={{0,0},{1,32},{2,64},{3,96},{4,128},{5,160},{6,192},{7,224},{8,8},{... | collective-permute-start | bytes 36872 | tf_op jit(solution)/shard_map/ppermute | solution.py:370
  59.0 2.7 %collective-permute-done = bf16[48,128]{1,0:T(8,128)(2,1)S(1)} collective-permute-done((bf16[48,128]{1,0:T(8,128)(2,1)S(1)}, bf16[48,128]{1,0:T(8,128)(2,1)S(1)}, u32[]{:S(2)}, u32[]{:S(2)}) %collective-permute-start) | collective-permute-done | bytes 12320 | tf_op jit(solution)/shard_map/ppermute | solution.py:370
  61.7 0.1 broadcast_in_dim.7
  61.7 24.6 %all_to_all.38 = bf16[32,48,128]{2,1,0:T(8,128)(2,1)S(1)} all-to-all(bf16[32,48,128]{2,1,0:T(8,128)(2,1)S(1)} %broadcast_in_dim.7), channel_id=1, replica_groups=mesh['z'=8,'x'=4,'y'=4,'core'=2] {'z','x'}, dimensions={0} | all-to-all | bytes 786432 | tf_op jit(solution)/shard_map/all_to_all | solution.py:351
  86.3 0.0 copy-done
  86.3 0.0 copy-done.1
  86.3 0.8 other_half_kernel.1
  87.2 0.1 collective-permute-start.1
  87.3 0.6 own_half_kernel.1.a_ref
  87.9 0.0 copy-start.2
  87.9 1.1 collective-permute-done.1.b_ref
  89.0 0.2 pair_kernel.1
  89.2 10.7 %all_to_all.39.x_ref = bf16[4,32,1408]{2,1,0:T(8,128)(2,1)S(1)} all-to-all(bf16[4,32,1408]{2,1,0:T(8,128)(2,1)S(1)} %bitcast.9), channel_id=1, replica_groups=mesh['z'=8,'x'=4,'y'=4,'core'=2] {'y'}, dimensions={0} | all-to-all | bytes 720896 | tf_op jit(solution)/shard_map/all_to_all | solution.py:351
  99.9 0.2 hidden_kernel.1
  100.1 10.8 %all_to_all.40.a_ref = bf16[8,168,128]{2,1,0:T(8,128)(2,1)S(1)} all-to-all(bf16[8,168,128]{2,1,0:T(8,128)(2,1)S(1)} %hidden_kernel.1), channel_id=1, replica_groups=mesh['z'=8,'x'=4,'y'=4,'core'=2] {'y','core'}, dimensions={0} | all-to-all | bytes 688128 | tf_op jit(solution)/shard_map/all_to_all | solution.py:351
  110.9 0.0 copy-done.2
  110.9 0.6 down_kernel.1
  111.5 19.3 %all_to_all.41.x_ref = bf16[32,8,672]{2,1,0:T(8,128)(2,1)S(1)} all-to-all(bf16[32,8,672]{2,1,0:T(8,128)(2,1)S(1)} %bitcast.8), channel_id=1, replica_groups=mesh['z'=8,'x'=4,'y'=4,'core'=2] {'z','x'}, dimensions={0} | all-to-all | bytes 688128 | tf_op jit(solution)/shard_map/all_to_all | solution.py:351
  130.8 0.7 final_kernel.1
  (1 shorter events, 0.0 us)
Async XLA Ops:
  0.0 46.2 %copy-start.3 = (bf16[512,168]{0,1:T(8,128)(2,1)S(1)}, bf16[512,168]{0,1:T(8,128)(2,1)}, u32[]{:S(2)}) copy-start(bf16[512,168]{0,1:T(8,128)(2,1)} %param.17) | copy-start | bytes 516100
  4.0 52.6 %copy-start.4 = (bf16[32,168]{1,0:T(8,128)(2,1)S(1)}, bf16[32,168]{1,0:T(8,128)(2,1)}, u32[]{:S(2)}) copy-start(bf16[32,168]{1,0:T(8,128)(2,1)} %r_ref.1) | copy-start | bytes 32260
  4.0 82.3 %copy-start = (bf16[672,672]{1,0:T(8,128)(2,1)S(1)}, bf16[672,672]{1,0:T(8,128)(2,1)}, u32[]{:S(2)}) copy-start(bf16[672,672]{1,0:T(8,128)(2,1)} %g_ref.3) | copy-start | bytes 2709508
  4.0 82.3 %copy-start.1 = (bf16[672,672]{1,0:T(8,128)(2,1)S(1)}, bf16[672,672]{1,0:T(8,128)(2,1)}, u32[]{:S(2)}) copy-start(bf16[672,672]{1,0:T(8,128)(2,1)} %u_ref.3) | copy-start | bytes 2709508
  56.7 5.0 %collective-permute-start = (bf16[48,128]{1,0:T(8,128)(2,1)S(1)}, bf16[48,128]{1,0:T(8,128)(2,1)S(1)}, u32[]{:S(2)}, u32[]{:S(2)}) collective-permute-start(bf16[48,128]{1,0:T(8,128)(2,1)S(1)} %stream_kernel.1), channel_id=1, source_target_pairs={{0,0},{1,32},{2,64},{3,96},{4,128},{5,160},{6,192},{7,224},{8,8},{... | collective-permute-start | bytes 36872 | tf_op jit(solution)/shard_map/ppermute | solution.py:370
  87.2 1.8 %collective-permute-start.1 = (bf16[128,1408]{1,0:T(8,128)(2,1)S(1)}, bf16[128,1408]{1,0:T(8,128)(2,1)S(1)}, u32[]{:S(2)}, u32[]{:S(2)}) collective-permute-start(bf16[128,1408]{1,0:T(8,128)(2,1)S(1)} %get-tuple-element.15), channel_id=1, source_target_pairs={{0,1},{1,0},{2,3},{3,2},{4,5},{5,4},{6,7},{7,6},{8,9},{9,8},{10,11... | collective-permute-start | bytes 1081352 | tf_op jit(solution)/shard_map/ppermute | solution.py:387
  87.9 23.1 %copy-start.2 = (bf16[672,672]{1,0:T(8,128)(2,1)S(1)}, bf16[672,672]{1,0:T(8,128)(2,1)}, u32[]{:S(2)}) copy-start(bf16[672,672]{1,0:T(8,128)(2,1)} %w_ref.1) | copy-start | bytes 2709508

commit v11 on v10

--- a/solution.py
+++ b/solution.py
@@ -317,11 +317,11 @@
     mains, tails = [], []
     for c in range(NC):
         for y in range(NY):
-            rows = a_ref[y * NC + c].astype(F32)
-            mains.append(
-                jnp.concatenate([rows[j * 32 : (j + 1) * 32] for j in range(5)], axis=1).astype(BF)
-            )
-            tails += [rows[160:, g * 32 : (g + 1) * 32] for g in range(4)]
+            k = y * NC + c
+            blocks = [a_ref[k, j * 32 : (j + 1) * 32, :] for j in range(5)]
+            mains.append(jnp.concatenate(blocks, axis=1))
+            rest = a_ref[k, 160:168, :].astype(F32)
+            tails += [rest[:, g * 32 : (g + 1) * 32] for g in range(4)]
     main = jnp.concatenate(mains, axis=0)
     tail = jnp.concatenate(tails, axis=0).astype(BF)
     total = jnp.dot(main, w_ref[:640, :], preferred_element_type=F32)

time: 131 us -> 131 us (level)
  no operation moved by 1% of the time
where the time goes in v11:
time: 131 us
  blocking collectives  117 us (89%)
  Pallas kernels  6.89 us (5%)
  waiting for transfers between devices  3.76 us (3%)
  starting transfers between devices  2.41 us (2%)
    all_to_all x7, blocking collectives, exchange(): return lax.all_to_all(parts, axis, split_axis=0, concat_axis=0, tiled=True)  117 us
    pallas_call x9, Pallas kernels, call(): pl.pallas_call(kernel, out_shape=outs, in_specs=specs, out_specs=[VMEM] *...  3.83 us
    pallas_call x1, Pallas kernels, attend(): pl.pallas_call(attend_kernel, out_shape=jax.ShapeDtypeStruct((256, 640),...  3.05 us
    ppermute x1, waiting for transfers between devices, shards(): lax.ppermute(stream, ALL, [(place(z, x, h), place(h, x, z)) for z in rang...  2.67 us
  transfers between devices with their start and end apart: 2, of which 2 were waited for; matrix products, arithmetic and copies ran while one was open for 0% of the time, Pallas kernels for 0%

profile of v11, /device:TPU:32, one launch (start us, length us, event | category | flops | bytes accessed | tf_op | source)
XLA Modules:
  0.0 130.5 jit_solution(3585546514942735410)
XLA Ops:
  0.0 0.0 copy-start.3
  0.0 3.1 %attend.1 = bf16[256,640]{1,0:T(8,128)(2,1)S(1)} custom-call(s32[64]{0:T(128)} %pm_hbm.1, s32[2,8]{1,0:T(2,128)} %sel_hbm.1, f32[1,168]{1,0:T(1,128)} %bitcast.13, bf16[256,512]{1,0:T(8,128)(2,1)} %q_hbm.1, bf16[2,2048,256]{2,1,0:T(8,128)(2,1)} %k_hbm.1, bf16[2,2048,256]{2,1,0:T(8,128)(2,1)} %v_hbm.1), custom_call_target="tpu_custom_call" | custom-call | flops 4000000000 | bytes 10485760 | tf_op jit(solution)/shard_map/attend/pallas_call | solution.py:171
  3.1 0.0 copy-start.4
  3.1 0.0 copy-start
  3.1 0.0 copy-start.1
  3.1 25.8 %all_to_all.35.x_ref = bf16[32,8,640]{2,1,0:T(8,128)(2,1)S(1)} all-to-all(bf16[32,8,640]{2,1,0:T(8,128)(2,1)S(1)} %bitcast.11), channel_id=1, replica_groups=mesh['z'=8,'x'=4,'y'=4,'core'=2] {'z','x'}, dimensions={0} | all-to-all | bytes 655360 | tf_op jit(solution)/shard_map/all_to_all | solution.py:351
  28.9 0.3 merge_kernel.1
  29.3 16.0 %all_to_all.36 = bf16[32,8,512]{2,1,0:T(8,128)(2,1)S(1)} all-to-all(bf16[32,8,512]{2,1,0:T(8,128)(2,1)S(1)} %broadcast_in_dim.6), channel_id=1, replica_groups=mesh['z'=8,'x'=4,'y'=4,'core'=2] {'z','x'}, dimensions={0} | all-to-all | bytes 524288 | tf_op jit(solution)/shard_map/all_to_all | solution.py:351
  45.3 0.0 copy-done.3
  45.3 0.3 project_kernel.1
  45.6 10.1 %all_to_all.37.x_ref = bf16[8,48,128]{2,1,0:T(8,128)(2,1)S(1)} all-to-all(bf16[8,48,128]{2,1,0:T(8,128)(2,1)S(1)} %project_kernel.1), channel_id=1, replica_groups=mesh['z'=8,'x'=4,'y'=4,'core'=2] {'y','core'}, dimensions={0} | all-to-all | bytes 196608 | tf_op jit(solution)/shard_map/all_to_all | solution.py:351
  55.7 0.0 copy-done.4
  55.7 0.1 stream_kernel.1
  55.7 2.3 %collective-permute-start = (bf16[48,128]{1,0:T(8,128)(2,1)S(1)}, bf16[48,128]{1,0:T(8,128)(2,1)S(1)}, u32[]{:S(2)}, u32[]{:S(2)}) collective-permute-start(bf16[48,128]{1,0:T(8,128)(2,1)S(1)} %stream_kernel.1), channel_id=1, source_target_pairs={{0,0},{1,32},{2,64},{3,96},{4,128},{5,160},{6,192},{7,224},{8,8},{... | collective-permute-start | bytes 36872 | tf_op jit(solution)/shard_map/ppermute | solution.py:370
  58.1 2.7 %collective-permute-done = bf16[48,128]{1,0:T(8,128)(2,1)S(1)} collective-permute-done((bf16[48,128]{1,0:T(8,128)(2,1)S(1)}, bf16[48,128]{1,0:T(8,128)(2,1)S(1)}, u32[]{:S(2)}, u32[]{:S(2)}) %collective-permute-start) | collective-permute-done | bytes 12320 | tf_op jit(solution)/shard_map/ppermute | solution.py:370
  60.7 0.1 broadcast_in_dim.7
  60.8 24.6 %all_to_all.38 = bf16[32,48,128]{2,1,0:T(8,128)(2,1)S(1)} all-to-all(bf16[32,48,128]{2,1,0:T(8,128)(2,1)S(1)} %broadcast_in_dim.7), channel_id=1, replica_groups=mesh['z'=8,'x'=4,'y'=4,'core'=2] {'z','x'}, dimensions={0} | all-to-all | bytes 786432 | tf_op jit(solution)/shard_map/all_to_all | solution.py:351
  85.4 0.0 copy-done
  85.4 0.0 copy-done.1
  85.4 0.8 other_half_kernel.1
  86.2 0.1 collective-permute-start.1
  86.3 0.6 own_half_kernel.1.a_ref
  86.9 0.0 copy-start.2
  86.9 1.1 collective-permute-done.1.b_ref
  88.0 0.2 pair_kernel.1
  88.2 10.7 %all_to_all.39.x_ref = bf16[4,32,1408]{2,1,0:T(8,128)(2,1)S(1)} all-to-all(bf16[4,32,1408]{2,1,0:T(8,128)(2,1)S(1)} %bitcast.9), channel_id=1, replica_groups=mesh['z'=8,'x'=4,'y'=4,'core'=2] {'y'}, dimensions={0} | all-to-all | bytes 720896 | tf_op jit(solution)/shard_map/all_to_all | solution.py:351
  98.9 0.2 hidden_kernel.1
  99.2 10.8 %all_to_all.40.a_ref = bf16[8,168,128]{2,1,0:T(8,128)(2,1)S(1)} all-to-all(bf16[8,168,128]{2,1,0:T(8,128)(2,1)S(1)} %hidden_kernel.1), channel_id=1, replica_groups=mesh['z'=8,'x'=4,'y'=4,'core'=2] {'y','core'}, dimensions={0} | all-to-all | bytes 688128 | tf_op jit(solution)/shard_map/all_to_all | solution.py:351
  110.0 0.0 copy-done.2
  110.0 0.6 down_kernel.1
  110.6 19.3 %all_to_all.41.x_ref = bf16[32,8,672]{2,1,0:T(8,128)(2,1)S(1)} all-to-all(bf16[32,8,672]{2,1,0:T(8,128)(2,1)S(1)} %bitcast.8), channel_id=1, replica_groups=mesh['z'=8,'x'=4,'y'=4,'core'=2] {'z','x'}, dimensions={0} | all-to-all | bytes 688128 | tf_op jit(solution)/shard_map/all_to_all | solution.py:351
  129.8 0.7 final_kernel.1
  (1 shorter events, 0.0 us)
Async XLA Ops:
  0.0 45.3 %copy-start.3 = (bf16[512,168]{0,1:T(8,128)(2,1)S(1)}, bf16[512,168]{0,1:T(8,128)(2,1)}, u32[]{:S(2)}) copy-start(bf16[512,168]{0,1:T(8,128)(2,1)} %param.17) | copy-start | bytes 516100
  3.1 52.6 %copy-start.4 = (bf16[32,168]{1,0:T(8,128)(2,1)S(1)}, bf16[32,168]{1,0:T(8,128)(2,1)}, u32[]{:S(2)}) copy-start(bf16[32,168]{1,0:T(8,128)(2,1)} %r_ref.1) | copy-start | bytes 32260
  3.1 82.3 %copy-start = (bf16[672,672]{1,0:T(8,128)(2,1)S(1)}, bf16[672,672]{1,0:T(8,128)(2,1)}, u32[]{:S(2)}) copy-start(bf16[672,672]{1,0:T(8,128)(2,1)} %g_ref.3) | copy-start | bytes 2709508
  3.1 82.3 %copy-start.1 = (bf16[672,672]{1,0:T(8,128)(2,1)S(1)}, bf16[672,672]{1,0:T(8,128)(2,1)}, u32[]{:S(2)}) copy-start(bf16[672,672]{1,0:T(8,128)(2,1)} %u_ref.3) | copy-start | bytes 2709508
  55.7 5.0 %collective-permute-start = (bf16[48,128]{1,0:T(8,128)(2,1)S(1)}, bf16[48,128]{1,0:T(8,128)(2,1)S(1)}, u32[]{:S(2)}, u32[]{:S(2)}) collective-permute-start(bf16[48,128]{1,0:T(8,128)(2,1)S(1)} %stream_kernel.1), channel_id=1, source_target_pairs={{0,0},{1,32},{2,64},{3,96},{4,128},{5,160},{6,192},{7,224},{8,8},{... | collective-permute-start | bytes 36872 | tf_op jit(solution)/shard_map/ppermute | solution.py:370
  86.2 1.8 %collective-permute-start.1 = (bf16[128,1408]{1,0:T(8,128)(2,1)S(1)}, bf16[128,1408]{1,0:T(8,128)(2,1)S(1)}, u32[]{:S(2)}, u32[]{:S(2)}) collective-permute-start(bf16[128,1408]{1,0:T(8,128)(2,1)S(1)} %get-tuple-element.15), channel_id=1, source_target_pairs={{0,1},{1,0},{2,3},{3,2},{4,5},{5,4},{6,7},{7,6},{8,9},{9,8},{10,11... | collective-permute-start | bytes 1081352 | tf_op jit(solution)/shard_map/ppermute | solution.py:387
  86.9 23.1 %copy-start.2 = (bf16[672,672]{1,0:T(8,128)(2,1)S(1)}, bf16[672,672]{1,0:T(8,128)(2,1)}, u32[]{:S(2)}) copy-start(bf16[672,672]{1,0:T(8,128)(2,1)} %w_ref.1) | copy-start | bytes 2709508
